TPU v7x, 32 devices: a whole 2x2x4 slice. The times are simulated.
32 devices in a mesh: fsdp: 8 (over y, x, core), sp: 4 (over z).
Axes of the slice: x: 2, y: 2, z: 4, core: 2. Of those that a mesh axis runs over, the one named last changes fastest.
Arguments:
- hidden_in: bfloat16 [4096, 2048], P(('fsdp', 'sp')), may hold values from -6 to 6
- grad_out: bfloat16 [4096, 2048], P(('fsdp', 'sp')), may hold values from -6 to 6
- lengths: int32 [5], replicated, may hold values from 1 to 2048, 4096 in all
- attn_gain: bfloat16 [2048], P('fsdp'), may hold values from 0.25 to 1.75
- w_qkv: bfloat16 [4096, 2048], P('fsdp'), may hold values from -0.125 to 0.125
- w_head_gate: bfloat16 [16, 2048], P('fsdp'), may hold values from -0.125 to 0.125
- q_gain: bfloat16 [128], P('fsdp'), may hold values from 0.25 to 1.75
- k_gain: bfloat16 [128], P('fsdp'), may hold values from 0.25 to 1.75
- w_out: bfloat16 [2048, 2048], P('fsdp'), may hold values from -2.5 to 2.5
- ffn_gain: bfloat16 [2048], P('fsdp'), may hold values from 0.25 to 1.75
- w_gate: bfloat16 [6144, 2048], P('fsdp'), may hold values from -0.125 to 0.125
- w_up: bfloat16 [6144, 2048], P('fsdp'), may hold values from -0.125 to 0.125
- w_down: bfloat16 [6144, 2048], P('fsdp'), may hold values from -0.078125 to 0.078125
Outputs:
- hidden_out: bfloat16 [4096, 2048], P(('fsdp', 'sp'))
- grad_in: float32 [4096, 2048], P(('fsdp', 'sp'))
- grad_attn_gain: float32 [2048], P('fsdp')
- grad_w_qkv: float32 [4096, 2048], P('fsdp')
- grad_w_head_gate: float32 [16, 2048], P('fsdp')
- grad_q_gain: float32 [128], P('fsdp')
- grad_k_gain: float32 [128], P('fsdp')
- grad_w_out: float32 [2048, 2048], P('fsdp')
- grad_ffn_gain: float32 [2048], P('fsdp')
- grad_w_gate: float32 [6144, 2048], P('fsdp')
- grad_w_up: float32 [6144, 2048], P('fsdp')
- grad_w_down: float32 [6144, 2048], P('fsdp')
Inputs may be any that keep to these rules, and one draw needn't show every extreme that they name: The 5 items are packed in token order; their lengths sum to 4096 and the longest is exactly 2048.
All inputs are finite; a program needn't handle non-finite values.
Results may differ from a plain program's by a relative error of at most 0.015.
Values may be sent and summed in bfloat16 or wider, within the bound.
A program may use at most 768 MiB of HBM per device.

v0:
```python
import math

import jax
import jax.numpy as jnp
from jax import lax
from jax.sharding import PartitionSpec as P

HEADS = 16
KV_HEADS = 8
HEAD_DIM = 128


EPS = 1e-06
ROPE_BASE = 1000000.0


def mat_nt(factor, others):
    return lax.dot_general(
        factor, others, (((1,), (1,)), ((), ())), preferred_element_type=jnp.float32
    )


def mat_tn(factor, others):
    return lax.dot_general(
        factor, others, (((0,), (0,)), ((), ())), preferred_element_type=jnp.float32
    )


def inv_rms(values):
    return lax.rsqrt(jnp.mean(values * values, axis=-1, keepdims=True) + EPS)


def norm_back(grad_norm, values, inverse, scaling):
    scaled = grad_norm * scaling
    cubed = inverse * inverse * inverse
    return inverse * scaled - values * cubed * jnp.mean(scaled * values, axis=-1, keepdims=True)


def item_starts(token_index, lengths):
    ends = jnp.cumsum(lengths)
    starts = ends - lengths
    inside = (token_index[:, None] >= starts[None, :]) & (token_index[:, None] < ends[None, :])
    return jnp.sum(jnp.where(inside, starts[None, :], 0), axis=1)


def rope_tables(position):
    half_dim = HEAD_DIM // 2
    freq_steps = jnp.arange(half_dim, dtype=jnp.float32)
    frequency = jnp.exp(-math.log(ROPE_BASE) * 2.0 * freq_steps / HEAD_DIM)
    angles = position.astype(jnp.float32)[:, None] * frequency[None, :]
    return (jnp.cos(angles)[:, None, :], jnp.sin(angles)[:, None, :])


def rotate(values, cosine, sine):
    half_dim = values.shape[-1] // 2
    lower = values[..., :half_dim]
    upper = values[..., half_dim:]
    return jnp.concatenate([lower * cosine - upper * sine, upper * cosine + lower * sine], axis=-1)


def rotate_back(grad_rot, cosine, sine):
    half_dim = grad_rot.shape[-1] // 2
    lower = grad_rot[..., :half_dim]
    upper = grad_rot[..., half_dim:]
    return jnp.concatenate([lower * cosine + upper * sine, upper * cosine - lower * sine], axis=-1)


def local(
    hidden_in,
    grad_out,
    lengths,
    attn_gain,
    w_qkv,
    w_head_gate,
    q_gain,
    k_gain,
    w_out,
    ffn_gain,
    w_gate,
    w_up,
    w_down,
):
    fsdp_count = lax.axis_size("fsdp")
    sp_count = lax.axis_size("sp")
    fsdp_rank = lax.axis_index("fsdp")
    sp_rank = lax.axis_index("sp")
    tok_rows = hidden_in.shape[0]
    model_width = hidden_in.shape[1]
    query_width = HEADS * HEAD_DIM
    kv_width = KV_HEADS * HEAD_DIM
    local_kv = KV_HEADS // sp_count
    head_group = HEADS // KV_HEADS
    score_scale = HEAD_DIM ** (-0.5)
    qkv_full, out_full, gate_full, attn_gain_full, q_gain_full, k_gain_full, ffn_gain_full = (
        lax.all_gather(w_qkv, "fsdp", axis=0, tiled=True),
        lax.all_gather(w_out, "fsdp", axis=0, tiled=True),
        lax.all_gather(w_head_gate, "fsdp", axis=0, tiled=True),
        lax.all_gather(attn_gain, "fsdp", axis=0, tiled=True),
        lax.all_gather(q_gain, "fsdp", axis=0, tiled=True),
        lax.all_gather(k_gain, "fsdp", axis=0, tiled=True),
        lax.all_gather(ffn_gain, "fsdp", axis=0, tiled=True),
    )
    attn_scale = attn_gain_full.astype(jnp.float32)
    query_scale = q_gain_full.astype(jnp.float32)
    key_scale = k_gain_full.astype(jnp.float32)
    ffn_scale = ffn_gain_full.astype(jnp.float32)
    token_first = (fsdp_rank * sp_count + sp_rank) * tok_rows
    own_tokens = token_first + jnp.arange(tok_rows, dtype=jnp.int32)
    cosine, sine = rope_tables(own_tokens - item_starts(own_tokens, lengths))
    inputs = hidden_in.astype(jnp.float32)
    inv_first = inv_rms(inputs)
    normed_a = (inputs * inv_first * attn_scale).astype(jnp.bfloat16)
    projected = mat_nt(normed_a, qkv_full)
    gate_logit = mat_nt(normed_a, gate_full)
    q_raw = projected[:, :query_width].reshape(tok_rows, HEADS, HEAD_DIM)
    k_raw = projected[:, query_width : query_width + kv_width].reshape(tok_rows, KV_HEADS, HEAD_DIM)
    q_inv = inv_rms(q_raw)
    k_inv = inv_rms(k_raw)
    query = (
        rotate(q_raw * q_inv * query_scale, cosine, sine)
        .reshape(tok_rows, query_width)
        .astype(jnp.bfloat16)
    )
    keys = (
        rotate(k_raw * k_inv * key_scale, cosine, sine)
        .reshape(tok_rows, kv_width)
        .astype(jnp.bfloat16)
    )
    values = projected[:, query_width + kv_width :].astype(jnp.bfloat16)
    query_heads, key_heads, value_heads = (
        lax.all_to_all(query, "sp", split_axis=1, concat_axis=0, tiled=True),
        lax.all_to_all(keys, "sp", split_axis=1, concat_axis=0, tiled=True),
        lax.all_to_all(values, "sp", split_axis=1, concat_axis=0, tiled=True),
    )
    key_all, value_all = (
        lax.all_gather(key_heads, "fsdp", axis=0, tiled=True),
        lax.all_gather(value_heads, "fsdp", axis=0, tiled=True),
    )
    span_rows = query_heads.shape[0]
    span_first = fsdp_rank * span_rows
    span_tokens = span_first + jnp.arange(span_rows, dtype=jnp.int32)
    span_starts = item_starts(span_tokens, lengths)
    query_four = query_heads.reshape(span_rows, local_kv, head_group, HEAD_DIM)
    key_total = key_all.shape[0]
    key_block = min(1024, key_total)
    block_count = key_total // key_block
    key_blocks = key_all.reshape(block_count, key_block, local_kv, HEAD_DIM)
    value_blocks = value_all.reshape(block_count, key_block, local_kv, HEAD_DIM)
    block_firsts = jnp.arange(block_count, dtype=jnp.int32) * key_block
    lowest_key = span_starts[0]
    highest_key = span_first + span_rows - 1

    def needed(block_first):
        return (block_first <= highest_key) & (block_first + key_block - 1 >= lowest_key)

    def block_weights(key_piece, block_first):
        scores = (
            jnp.einsum("qkgd,jkd->kgqj", query_four, key_piece, preferred_element_type=jnp.float32)
            * score_scale
        )
        columns = block_first + jnp.arange(key_block, dtype=jnp.int32)
        allowed = (columns[None, :] <= span_tokens[:, None]) & (
            columns[None, :] >= span_starts[:, None]
        )
        return jnp.where(allowed[None, None], jnp.exp(scores), 0.0)

    def forward_step(running, pieces):
        key_piece, value_piece, block_first = pieces

        def forward_compute(current):
            totals, unnormed = current
            weights = block_weights(key_piece, block_first)
            totals = totals + jnp.sum(weights, axis=3)
            unnormed = unnormed + jnp.einsum(
                "kgqj,jkd->qkgd",
                weights.astype(jnp.bfloat16),
                value_piece,
                preferred_element_type=jnp.float32,
            )
            return (totals, unnormed)

        return (
            lax.cond(needed(block_first), forward_compute, lambda current: current, running),
            None,
        )

    start_state = (
        jnp.zeros((local_kv, head_group, span_rows), jnp.float32),
        jnp.zeros((span_rows, local_kv, head_group, HEAD_DIM), jnp.float32),
    )
    scanned = lax.scan(forward_step, start_state, (key_blocks, value_blocks, block_firsts))[0]
    totals, unnormed = scanned
    totals_rows = jnp.transpose(totals, (2, 0, 1))[..., None]
    attended_heads = unnormed / totals_rows
    attended_send = attended_heads.reshape(span_rows, local_kv * head_group * HEAD_DIM).astype(
        jnp.bfloat16
    )
    returned = lax.all_to_all(attended_send, "sp", split_axis=0, concat_axis=1, tiled=True)
    gate_prob = jax.nn.sigmoid(gate_logit)
    attended_tok = returned.astype(jnp.float32).reshape(tok_rows, HEADS, HEAD_DIM)
    gated = (
        (attended_tok * gate_prob[:, :, None]).reshape(tok_rows, query_width).astype(jnp.bfloat16)
    )
    middle = inputs + jnp.dot(gated, out_full, preferred_element_type=jnp.float32)
    inv_second = inv_rms(middle)
    normed_b = (middle * inv_second * ffn_scale).astype(jnp.bfloat16)
    gate_piece = lax.all_gather(w_gate, "fsdp", axis=0, tiled=True)
    up_piece = lax.all_gather(w_up, "fsdp", axis=0, tiled=True)
    down_piece = lax.all_gather(w_down, "fsdp", axis=0, tiled=True)
    gate_pre = mat_nt(normed_b, gate_piece)
    up_pre = mat_nt(normed_b, up_piece)
    hidden = (jax.nn.silu(gate_pre) * up_pre).astype(jnp.bfloat16)
    ffn_part = jnp.dot(hidden, down_piece, preferred_element_type=jnp.float32)
    hidden_out = (middle + ffn_part).astype(jnp.bfloat16)
    gate_piece = lax.all_gather(w_gate, "fsdp", axis=0, tiled=True)
    up_piece = lax.all_gather(w_up, "fsdp", axis=0, tiled=True)
    down_piece = lax.all_gather(w_down, "fsdp", axis=0, tiled=True)
    gate_pre = mat_nt(normed_b, gate_piece)
    up_pre = mat_nt(normed_b, up_piece)
    sigma = jax.nn.sigmoid(gate_pre)
    swish = gate_pre * sigma
    hidden = (swish * up_pre).astype(jnp.bfloat16)
    grad_hidden = mat_nt(grad_out, down_piece)
    grad_gate = (grad_hidden * up_pre * sigma * (1.0 + gate_pre * (1.0 - sigma))).astype(
        jnp.bfloat16
    )
    grad_up = (grad_hidden * swish).astype(jnp.bfloat16)
    grad_acc = jnp.dot(grad_gate, gate_piece, preferred_element_type=jnp.float32) + jnp.dot(
        grad_up, up_piece, preferred_element_type=jnp.float32
    )
    grad_ffn_gain_local = jnp.sum(grad_acc * middle * inv_second, axis=0)
    grad_middle = grad_out.astype(jnp.float32) + norm_back(grad_acc, middle, inv_second, ffn_scale)
    grad_mid_b = grad_middle.astype(jnp.bfloat16)
    grad_gated = mat_nt(grad_mid_b, out_full).reshape(tok_rows, HEADS, HEAD_DIM)
    grad_attended = (
        (grad_gated * gate_prob[:, :, None]).reshape(tok_rows, query_width).astype(jnp.bfloat16)
    )
    gate_grad = (jnp.sum(grad_gated * attended_tok, axis=2) * gate_prob * (1.0 - gate_prob)).astype(
        jnp.bfloat16
    )
    grad_heads = lax.all_to_all(grad_attended, "sp", split_axis=1, concat_axis=0, tiled=True)
    grad_four = grad_heads.astype(jnp.float32).reshape(span_rows, local_kv, head_group, HEAD_DIM)
    grad_scaled = (grad_four / totals_rows).astype(jnp.bfloat16)
    delta_rows = jnp.sum(grad_four * attended_heads, axis=3) / totals_rows[..., 0]
    delta_heads = jnp.transpose(delta_rows, (1, 2, 0))

    def backward_step(grad_query, pieces):
        key_piece, value_piece, block_first = pieces

        def backward_compute(current):
            weights = block_weights(key_piece, block_first)
            grad_prob = jnp.einsum(
                "qkgd,jkd->kgqj", grad_scaled, value_piece, preferred_element_type=jnp.float32
            )
            grad_score = (weights * (grad_prob - delta_heads[..., None])).astype(jnp.bfloat16)
            current = (
                current
                + jnp.einsum(
                    "kgqj,jkd->qkgd", grad_score, key_piece, preferred_element_type=jnp.float32
                )
                * score_scale
            )
            grad_key = (
                jnp.einsum(
                    "kgqj,qkgd->jkd", grad_score, query_four, preferred_element_type=jnp.float32
                )
                * score_scale
            )
            grad_value = jnp.einsum(
                "kgqj,qkgd->jkd",
                weights.astype(jnp.bfloat16),
                grad_scaled,
                preferred_element_type=jnp.float32,
            )
            return (current, (grad_key, grad_value))

        def skip(current):
            nothing = jnp.zeros((key_block, local_kv, HEAD_DIM), jnp.float32)
            return (current, (nothing, nothing))

        return lax.cond(needed(block_first), backward_compute, skip, grad_query)

    grad_query, key_value_grads = lax.scan(
        backward_step,
        jnp.zeros((span_rows, local_kv, head_group, HEAD_DIM), jnp.float32),
        (key_blocks, value_blocks, block_firsts),
    )
    key_grads, value_grads = key_value_grads
    key_sum, value_sum = (
        lax.psum_scatter(
            key_grads.reshape(key_total, local_kv * HEAD_DIM),
            "fsdp",
            scatter_dimension=0,
            tiled=True,
        ),
        lax.psum_scatter(
            value_grads.reshape(key_total, local_kv * HEAD_DIM),
            "fsdp",
            scatter_dimension=0,
            tiled=True,
        ),
    )
    query_send = grad_query.reshape(span_rows, local_kv * head_group * HEAD_DIM).astype(
        jnp.bfloat16
    )
    back_query, back_key, back_value = (
        lax.all_to_all(query_send, "sp", split_axis=0, concat_axis=1, tiled=True),
        lax.all_to_all(key_sum.astype(jnp.bfloat16), "sp", split_axis=0, concat_axis=1, tiled=True),
        lax.all_to_all(
            value_sum.astype(jnp.bfloat16), "sp", split_axis=0, concat_axis=1, tiled=True
        ),
    )
    grad_qn = rotate_back(
        back_query.astype(jnp.float32).reshape(tok_rows, HEADS, HEAD_DIM), cosine, sine
    )
    grad_kn = rotate_back(
        back_key.astype(jnp.float32).reshape(tok_rows, KV_HEADS, HEAD_DIM), cosine, sine
    )
    grad_q_gain_local = jnp.sum(grad_qn * q_raw * q_inv, axis=(0, 1))
    grad_k_gain_local = jnp.sum(grad_kn * k_raw * k_inv, axis=(0, 1))
    grad_q_raw = norm_back(grad_qn, q_raw, q_inv, query_scale).reshape(tok_rows, query_width)
    grad_k_raw = norm_back(grad_kn, k_raw, k_inv, key_scale).reshape(tok_rows, kv_width)
    grad_proj = jnp.concatenate(
        [grad_q_raw.astype(jnp.bfloat16), grad_k_raw.astype(jnp.bfloat16), back_value], axis=1
    )
    grad_normed_a = jnp.dot(grad_proj, qkv_full, preferred_element_type=jnp.float32) + jnp.dot(
        gate_grad, gate_full, preferred_element_type=jnp.float32
    )
    grad_attn_gain_local = jnp.sum(grad_normed_a * inputs * inv_first, axis=0)
    grad_in = grad_middle + norm_back(grad_normed_a, inputs, inv_first, attn_scale)
    qkv_rows = w_qkv.shape[0]
    out_rows = w_out.shape[0]
    gate_rows = w_head_gate.shape[0]
    block_rows = qkv_rows + out_rows + gate_rows + 3
    small_rows = jnp.stack(
        [
            grad_attn_gain_local,
            grad_ffn_gain_local,
            jnp.concatenate(
                [
                    grad_q_gain_local,
                    grad_k_gain_local,
                    jnp.zeros((model_width - 2 * HEAD_DIM,), jnp.float32),
                ]
            ),
        ],
        axis=0,
    )
    ffn_partial = lax.psum_scatter(
        jnp.concatenate(
            [mat_tn(grad_gate, normed_b), mat_tn(grad_up, normed_b), mat_tn(hidden, grad_out)],
            axis=1,
        ).astype(jnp.bfloat16),
        "fsdp",
        scatter_dimension=0,
        tiled=True,
    ).astype(jnp.float32)
    proj_split = grad_proj.reshape(tok_rows, fsdp_count, qkv_rows)
    gated_split = gated.reshape(tok_rows, fsdp_count, out_rows)
    gate_split = gate_grad.reshape(tok_rows, fsdp_count, gate_rows)
    owners = block_rows * lax.axis_size("fsdp") // block_rows
    qkv_term = jnp.einsum("tor,td->ord", proj_split, normed_a, preferred_element_type=jnp.float32)
    out_term = jnp.einsum(
        "tor,td->ord", gated_split, grad_mid_b, preferred_element_type=jnp.float32
    )
    gate_term = jnp.einsum("tor,td->ord", gate_split, normed_a, preferred_element_type=jnp.float32)
    small_term = jnp.broadcast_to(small_rows[None], (owners, 3, model_width))
    joined = jnp.concatenate([qkv_term, out_term, gate_term, small_term], axis=1)
    attn_partial = lax.psum_scatter(
        joined.reshape(owners * block_rows, model_width), "fsdp", scatter_dimension=0, tiled=True
    )
    ffn_total, attn_total = lax.psum((ffn_partial, attn_partial), "sp")
    grad_w_gate = ffn_total[:, :model_width]
    grad_w_up = ffn_total[:, model_width : 2 * model_width]
    grad_w_down = ffn_total[:, 2 * model_width :]
    grad_w_qkv = attn_total[:qkv_rows]
    grad_w_out = attn_total[qkv_rows : qkv_rows + out_rows]
    grad_w_head_gate = attn_total[qkv_rows + out_rows : qkv_rows + out_rows + gate_rows]
    gain_sums = attn_total[qkv_rows + out_rows + gate_rows :]
    gain_part = model_width // fsdp_count
    head_part = HEAD_DIM // fsdp_count
    grad_attn_gain = lax.dynamic_slice_in_dim(gain_sums[0], fsdp_rank * gain_part, gain_part)
    grad_ffn_gain = lax.dynamic_slice_in_dim(gain_sums[1], fsdp_rank * gain_part, gain_part)
    grad_q_gain = lax.dynamic_slice_in_dim(gain_sums[2], fsdp_rank * head_part, head_part)
    grad_k_gain = lax.dynamic_slice_in_dim(
        gain_sums[2], HEAD_DIM + fsdp_rank * head_part, head_part
    )
    return (
        hidden_out,
        grad_in,
        grad_attn_gain,
        grad_w_qkv,
        grad_w_head_gate,
        grad_q_gain,
        grad_k_gain,
        grad_w_out,
        grad_ffn_gain,
        grad_w_gate,
        grad_w_up,
        grad_w_down,
    )


def solution(mesh):
    return jax.shard_map(
        local,
        mesh=mesh,
        in_specs=(
            P(("fsdp", "sp"), None),
            P(("fsdp", "sp"), None),
            P(),
            P("fsdp"),
            P("fsdp", None),
            P("fsdp", None),
            P("fsdp"),
            P("fsdp"),
            P("fsdp", None),
            P("fsdp"),
            P("fsdp", None),
            P("fsdp", None),
            P("fsdp", None),
        ),
        out_specs=(
            P(("fsdp", "sp"), None),
            P(("fsdp", "sp"), None),
            P("fsdp"),
            P("fsdp", None),
            P("fsdp", None),
            P("fsdp"),
            P("fsdp"),
            P("fsdp", None),
            P("fsdp"),
            P("fsdp", None),
            P("fsdp", None),
            P("fsdp", None),
        ),
        check_vma=False,
    )
```

profile of v0, /device:TPU:1, one launch (start us, length us, event | category | flops | bytes accessed | tf_op | source)
XLA Modules:
  0.0 2853.1 jit_solution(13129218577774362957)
XLA Ops:
  37.9 64.5 %all-gather.11.cloned.1.call-done = bf16[4096,2048]{1,0:T(8,128)(2,1)} async-done(((bf16[512,2048]{1,0:T(8,128)(2,1)}), bf16[4096,2048]{1,0:T(8,128)(2,1)}) %all-gather.11.cloned.1.call-update) | async-done | bytes 16777232 | tf_op jit(solution)/shard_map/all_gather | solution.py:95
  168.8 17.5 all-gather.15.cloned.1.call-done
  194.5 18.4 while.39
  225.6 24.1 all-gather.1
  269.2 100.4 %all-gather.19.cloned.1.call-done = bf16[6144,2048]{1,0:T(8,128)(2,1)} async-done(((bf16[768,2048]{1,0:T(8,128)(2,1)}), bf16[6144,2048]{1,0:T(8,128)(2,1)}) %all-gather.19.cloned.1.call-update) | async-done | bytes 25165840 | tf_op jit(solution)/shard_map/all_gather | solution.py:207
  369.6 15.3 fusion.98
  384.9 111.8 %all-gather.21.cloned.1.call-done = bf16[6144,2048]{1,0:T(8,128)(2,1)} async-done(((bf16[768,2048]{1,0:T(8,128)(2,1)}), bf16[6144,2048]{1,0:T(8,128)(2,1)}) %all-gather.21.cloned.1.call-update) | async-done | bytes 25165840 | tf_op jit(solution)/shard_map/all_gather | solution.py:208
  496.7 14.8 fusion.99
  511.5 112.5 %all-gather.23.cloned.1.call-done = bf16[6144,2048]{1,0:T(8,128)(2,1)} async-done(((bf16[768,2048]{1,0:T(8,128)(2,1)}), bf16[6144,2048]{1,0:T(8,128)(2,1)}) %all-gather.23.cloned.1.call-update) | async-done | bytes 25165840 | tf_op jit(solution)/shard_map/all_gather | solution.py:209
  623.9 15.2 multiply_convert_fusion
  696.8 35.9 %while.40 = (s32[]{:T(128)}, f32[512,2,2,128]{3,0,2,1:T(8,128)}, f32[4,1024,2,128]{3,2,1,0:T(2,128)}, f32[4,1024,2,128]{3,2,1,0:T(2,128)}, s32[4]{0:T(128)S(1)},...) while((s32[]{:T(128)}, f32[512,2,2,128]{3,0,2,1:T(8,128)}, ...), condition=%wide.region_17.18_spmd.clone, body=%wide.region_14.17_spmd.clone.sunk | while | flops 2703492608 | bytes 61895064 | solution.py:283
  699.4 13.5 conditional.7
  752.2 13.3 convolution_convert_fusion.1
  790.3 23.9 reduce-scatter.8.cloned.1.call-done
  824.4 45.4 %reduce-scatter.6.cloned.1.call-done = f32[512,256]{1,0:T(8,128)} async-done(((f32[4096,256]{1,0:T(8,128)}), f32[512,256]{1,0:T(8,128)}) %reduce-scatter.6.cloned.1.call-update) | async-done | bytes 524304 | tf_op jit(solution)/shard_map/reduce_scatter | solution.py:290
  912.4 33.8 %pad_maximum_fusion.1 = f32[8,773,2048]{2,1,0:T(8,128)} fusion(f32[8,3,2048]{2,1,0:T(4,128)S(1)} %broadcast_in_dim.129, f32[8,2,2048]{2,1,0:T(2,128)S(1)} %copy-done.37, f32[8,256,2048]{2,1,0:T(8,128)} %fusion.76, f32[8,512,2048]{2,1,0:T(8,128)} %fusion.80), kind=kLoop, calls=%fused_computation.57 | loop fusion | flops 37994496 | bytes 101318656 | tf_op jit(solution)/shard_map/concatenate | solution.py:368
  946.2 39.4 %reshape.442 = f32[6184,2048]{1,0:T(8,128)} reshape(f32[8,773,2048]{2,1,0:T(8,128)} %pad_maximum_fusion.1) | data formatting | bytes 101318656 | tf_op jit(solution)/shard_map/reshape | solution.py:370
  985.6 499.7 %fusion.4 = f32[784,2048]{1,0:T(8,128)} fusion(f32[6184,2048]{1,0:T(8,128)} %reshape.442), kind=kCustom, calls=%all-reduce-scatter | all-reduce-scatter fusion | flops 12845057 | bytes 57082368
  1503.7 18.8 concatenate.41
  1542.8 50.9 %pad_maximum_fusion = bf16[6144,6144]{0,1:T(8,128)(2,1)} fusion(bf16[6144,2048]{0,1:T(8,128)(2,1)} %convolution_convert_fusion, bf16[6144,2048]{0,1:T(8,128)(2,1)} %convolution_convert_fusion.1, bf16[6144,2048]{0,1:T(8,128)(2,1)} %convolution_convert_fusion.2), kind=kLoop, calls=%fused_computation.56 | loop fusion | flops 226492416 | bytes 150994944 | tf_op jit(solution)/shard_map/concatenate | solution.py:350
  1607.6 145.8 %all-reduce.8.cloned.1.call-done = f32[773,2048]{1,0:T(8,128)} async-done(((f32[773,2048]{1,0:T(8,128)}), f32[773,2048]{1,0:T(8,128)}) %all-reduce.8.cloned.1.call-update) | async-done | bytes 6332432 | tf_op jit(solution)/shard_map/psum | solution.py:372
  1764.9 415.3 %reduce-scatter.10.cloned.1.call-done = bf16[768,6144]{0,1:T(8,128)(2,1)} async-done(((bf16[6144,6144]{0,1:T(8,128)(2,1)}), bf16[768,6144]{0,1:T(8,128)(2,1)}) %reduce-scatter.10.cloned.1.call-update) | async-done | bytes 9437200 | tf_op jit(solution)/shard_map/reduce_scatter | solution.py:349
  2180.2 632.7 %all-reduce.9 = f32[768,6144]{0,1:T(8,128)} all-reduce(bf16[768,6144]{0,1:T(8,128)(2,1)} %reduce-scatter.10.cloned.1.call-done), channel_id=1, replica_groups=mesh['fsdp'=8,'sp'=4] {'sp'}, use_global_device_ids=true, to_apply=%region_33.34 | all-reduce | flops 4718592 | bytes 28311552 | tf_op jit(solution)/shard_map/psum | solution.py:372
  2812.9 13.7 fusion.95
  (386 shorter events, 420.1 us)
Async XLA Ops:
  7.2 95.3 %all-gather.11.cloned.1.call-start = ((), (), s32[]{:S(2)}) async-start(), calls=%async_computation.11 | async-start | bytes 18874368 | tf_op jit(solution)/shard_map/all_gather | solution.py:95
  7.9 155.0 %all-gather.13.cloned.1.call-start = ((), (), s32[]{:S(2)}) async-start(), calls=%async_computation.12 | async-start | bytes 2359296 | tf_op jit(solution)/shard_map/all_gather | solution.py:136
  18.8 230.8 %copy-start.41 = (f32[8,1,256]{2,1,0:T(1,128)}, f32[8,1,256]{2,1,0:T(1,128)S(1)}, u32[]{:S(2)}) copy-start(f32[8,1,256]{2,1,0:T(1,128)S(1)} %convert_element_type.248) | copy-start | bytes 24580
  37.7 212.0 %copy-start.56 = (f32[128]{0:T(128)}, f32[128]{0:T(128)S(1)}, u32[]{:S(2)}) copy-start(f32[128]{0:T(128)S(1)} %get-tuple-element.1106) | copy-start | bytes 1540
  37.9 104.7 %copy-start.33 = (f32[128,64]{0,1:T(8,128)}, f32[128,64]{0,1:T(8,128)S(1)}, u32[]{:S(2)}) copy-start(f32[128,64]{0,1:T(8,128)S(1)} %get-tuple-element.1101) | copy-start | bytes 98308
  127.8 58.5 %all-gather.15.cloned.1.call-start = ((), (), s32[]{:S(2)}) async-start(), calls=%async_computation.13 | async-start | bytes 2359296 | tf_op jit(solution)/shard_map/all_gather | solution.py:137
  138.1 124.8 %all-gather.17.cloned.1.call-start = ((), (), s32[]{:S(2)}) async-start(), calls=%async_computation.14 | async-start | bytes 9437184 | tf_op jit(solution)/shard_map/all_gather | solution.py:96
  138.7 230.9 %all-gather.19.cloned.1.call-start = ((), (), s32[]{:S(2)}) async-start(), calls=%async_computation.15 | async-start | bytes 28311552 | tf_op jit(solution)/shard_map/all_gather | solution.py:207
  139.3 357.4 %all-gather.21.cloned.1.call-start = ((), (), s32[]{:S(2)}) async-start(), calls=%async_computation.16 | async-start | bytes 28311552 | tf_op jit(solution)/shard_map/all_gather | solution.py:208
  139.9 484.1 %all-gather.23.cloned.1.call-start = ((), (), s32[]{:S(2)}) async-start(), calls=%async_computation.17 | async-start | bytes 28311552 | tf_op jit(solution)/shard_map/all_gather | solution.py:209
  143.6 18.8 all-to-all-start.1
  221.2 38.3 %all-to-all-start.3 = ((bf16[4,128,512]{2,1,0:T(8,128)(2,1)}), bf16[4,128,512]{2,1,0:T(8,128)(2,1)}, u32[]{:S(2)}, u32[]{:S(2)}) async-start(bf16[4,128,512]{2,1,0:T(8,128)(2,1)} %convert_element_type.199), calls=%async_computation.3 | async-start | bytes 1048576 | tf_op jit(solution)/shard_map/all_to_all | solution.py:198
  269.0 392.4 %copy-start.3 = (f32[128,2048]{1,0:T(8,128)}, f32[128,2048]{1,0:T(8,128)S(1)}, u32[]{:S(2)}) copy-start(f32[128,2048]{1,0:T(8,128)S(1)} %get-tuple-element.1110) | copy-start | bytes 3145732
  384.9 239.0 %copy-start.28 = (bf16[128,2048]{1,0:T(8,128)(2,1)S(1)}, bf16[128,2048]{1,0:T(8,128)(2,1)}, u32[]{:S(2)}) copy-start(bf16[128,2048]{1,0:T(8,128)(2,1)} %param.22) | copy-start | bytes 1572868
  666.7 18.4 all-to-all-start.4
  671.0 143.2 %reduce-scatter.8.cloned.1.call-start = ((), (), s32[]{:S(2)}) async-start(), calls=%async_computation.19 | async-start | bytes 4718592 | tf_op jit(solution)/shard_map/reduce_scatter | solution.py:296
  737.3 132.6 %reduce-scatter.6.cloned.1.call-start = ((), (), s32[]{:S(2)}) async-start(), calls=%async_computation.18 | async-start | bytes 4718592 | tf_op jit(solution)/shard_map/reduce_scatter | solution.py:290
  767.1 18.2 all-to-all-start.5
  816.0 55.7 %all-to-all-start.7 = ((bf16[4,128,256]{2,1,0:T(8,128)(2,1)}), bf16[4,128,256]{2,1,0:T(8,128)(2,1)S(1)}, u32[]{:S(2)}, u32[]{:S(2)}) async-start(bf16[4,128,256]{2,1,0:T(8,128)(2,1)} %bitcast.54), calls=%async_computation.9 | async-start | bytes 524288 | tf_op jit(solution)/shard_map/all_to_all | solution.py:309
  871.7 11.9 all-to-all-start.6
  876.0 877.4 %all-reduce.8.cloned.1.call-start = ((), (), s32[]{:S(2)}) async-start(), calls=%async_computation.20 | async-start | bytes 12713984 | tf_op jit(solution)/shard_map/psum | solution.py:372
  985.6 506.0 %copy-start.17 = (bf16[128,6144]{1,0:T(8,128)(2,1)S(1)}, bf16[128,6144]{1,0:T(8,128)(2,1)}, u32[]{:S(2)}) copy-start(bf16[128,6144]{1,0:T(8,128)(2,1)} %copy-done.16) | copy-start | bytes 4718596
  1487.2 16.4 collective-permute-start
  1529.2 651.0 %reduce-scatter.10.cloned.1.call-start = ((), (), s32[]{:S(2)}) async-start(), calls=%async_computation.21 | async-start | bytes 84934656 | tf_op jit(solution)/shard_map/reduce_scatter | solution.py:349
  (64 other events, 1064.3 us)
Sparse Core Ops, SparseCore 0:
  9.9 92.4 all-gather.10
  127.9 28.5 all-gather.12
  158.4 27.8 all-gather.14
  188.1 54.3 all-gather.16
  244.2 125.3 all-gather.18
  371.3 125.3 all-gather.20
  498.6 125.3 all-gather.22
  737.4 76.7 reduce-scatter.7
  818.5 51.3 reduce-scatter.5
  1529.3 224.0 all-reduce.7
  1757.5 422.7 reduce-scatter.9
where the time goes:
time: 2860 us; the launch traced here: 2850 us
  blocking collectives  1210 us (42%)
  waiting for transfers between devices  1070 us (37%)
  local copies, waits for them, and re-layouts  189 us (7%)
  matrix products  189 us (7%)
  other arithmetic  130 us (5%)
  starting transfers between devices  31.7 us (1%)
    psum x1, blocking collectives, local(): ffn_total, attn_total = lax.psum((ffn_partial, attn_partial), 'sp')  633 us
    unnamed x2, blocking collectives  511 us
    reduce_scatter x1, waiting for transfers between devices, local(): lax.psum_scatter(jnp.concatenate([mat_tn(grad_gate, normed_b), mat_tn(gra...  415 us
    psum x1, waiting for transfers between devices, local(): ffn_total, attn_total = lax.psum((ffn_partial, attn_partial), 'sp')  146 us
    all_gather x1, waiting for transfers between devices, local(): down_piece = lax.all_gather(w_down, 'fsdp', axis=0, tiled=True)  112 us
    all_gather x1, waiting for transfers between devices, local(): up_piece = lax.all_gather(w_up, 'fsdp', axis=0, tiled=True)  112 us
    all_gather x1, waiting for transfers between devices, local(): gate_piece = lax.all_gather(w_gate, 'fsdp', axis=0, tiled=True)  100 us
    unnamed x155, local copies, waits for them, and re-layouts  69.4 us
  transfers between devices with their start and end apart: 18, of which 13 were waited for; matrix products, arithmetic and copies ran while one was open for 8% of the time, Pallas kernels for 0%

commit v1 on v0

--- a/solution.py
+++ b/solution.py
@@ -1,8 +1,11 @@
+import functools
 import math
 
 import jax
 import jax.numpy as jnp
 from jax import lax
+from jax.experimental import pallas as pl
+from jax.experimental.pallas import tpu as pltpu
 from jax.sharding import PartitionSpec as P
 
 HEADS = 16
@@ -401,9 +404,1305 @@
     )
 
 
+MESH = pl.DeviceIdType.MESH
+VMEM_LIMIT = 60 * 1024 * 1024
+
+
+def peer_copy(src, dst, send_sem, recv_sem, rank, plane):
+    return pltpu.make_async_remote_copy(
+        src_ref=src,
+        dst_ref=dst,
+        send_sem=send_sem,
+        recv_sem=recv_sem,
+        device_id=(rank, plane),
+        device_id_type=MESH,
+    )
+
+
+def greet(peers):
+    barrier = pltpu.get_barrier_semaphore()
+    for peer in peers:
+        pl.semaphore_signal(barrier, inc=1, device_id=peer, device_id_type=MESH)
+    pl.semaphore_wait(barrier, len(peers))
+
+
+def gather_gains_kernel(x_ref, s_ref, o_ref, so_ref, send_sem, recv_sem, sib_send, sib_recv, own_sem, small_send, small_recv):
+    rank, plane = lax.axis_index("fsdp"), lax.axis_index("sp")
+    greet([(rank ^ k, plane) for k in range(1, 8)])
+    small = []
+    for k in range(1, 8):
+        copy = peer_copy(
+            s_ref, so_ref.at[rank], small_send.at[k - 1], small_recv.at[k - 1], rank ^ k, plane
+        )
+        copy.start()
+        small.append(copy)
+    so_ref[rank] = s_ref[...]
+    gather_blocks(x_ref, o_ref, send_sem, recv_sem, sib_send, sib_recv, own_sem)
+    for copy in small:
+        copy.wait()
+
+
+def gather_kernel(x_ref, o_ref, *sems):
+    rank, plane = lax.axis_index("fsdp"), lax.axis_index("sp")
+    greet([(rank ^ k, plane) for k in (1, 2, 4, 6)])
+    gather_blocks(x_ref, o_ref, *sems)
+
+
+def gather_blocks(x_ref, o_ref, send_sem, recv_sem, sib_send, sib_recv, own_sem):
+    rank, plane = lax.axis_index("fsdp"), lax.axis_index("sp")
+    half = x_ref.shape[0] // 2
+    own = pltpu.make_async_copy(x_ref, o_ref.at[rank], own_sem)
+    own.start()
+    far = {}
+    for h in range(2):
+        rows = pl.ds(h * half, half)
+        for i, k in enumerate((6, 2, 4)):
+            far[h, i] = peer_copy(
+                x_ref.at[rows],
+                o_ref.at[rank, rows],
+                send_sem.at[h, i],
+                recv_sem.at[h, i],
+                rank ^ k,
+                plane,
+            )
+            far[h, i].start()
+    near = []
+    first = peer_copy(
+        x_ref, o_ref.at[rank], sib_send.at[0, 3], sib_recv.at[0, 3], rank ^ 1, plane
+    )
+    first.start()
+    near.append(first)
+    for h in range(2):
+        rows = pl.ds(h * half, half)
+        for i, k in enumerate((6, 2, 4)):
+            far[h, i].wait_recv()
+            block = o_ref.at[rank ^ k, rows]
+            forward = peer_copy(
+                block, block, sib_send.at[h, i], sib_recv.at[h, i], rank ^ 1, plane
+            )
+            forward.start()
+            near.append(forward)
+    for copy in near:
+        copy.wait()
+    for copy in far.values():
+        copy.wait_send()
+    own.wait()
+
+
+def gather_plane(x, collective_id, small=None):
+    rows, width = x.shape
+    ranks = lax.axis_size("fsdp")
+    big = pl.BlockSpec(memory_space=pl.ANY)
+    sems = [
+        pltpu.SemaphoreType.DMA((2, 3)),
+        pltpu.SemaphoreType.DMA((2, 3)),
+        pltpu.SemaphoreType.DMA((2, 4)),
+        pltpu.SemaphoreType.DMA((2, 4)),
+        pltpu.SemaphoreType.DMA,
+    ]
+    out = jax.ShapeDtypeStruct((ranks, rows, width), x.dtype)
+    if small is not None:
+        vmem = pl.BlockSpec(memory_space=pltpu.VMEM)
+        return pl.pallas_call(
+            gather_gains_kernel,
+            out_shape=(out, jax.ShapeDtypeStruct((ranks,) + small.shape, small.dtype)),
+            in_specs=[big, vmem],
+            out_specs=(big, vmem),
+            scratch_shapes=sems + [pltpu.SemaphoreType.DMA((7,)), pltpu.SemaphoreType.DMA((7,))],
+            compiler_params=pltpu.CompilerParams(
+                collective_id=collective_id, has_side_effects=True, vmem_limit_bytes=VMEM_LIMIT
+            ),
+            name="gather_gains",
+        )(x, small)
+    return pl.pallas_call(
+        gather_kernel,
+        out_shape=out,
+        in_specs=[big],
+        out_specs=big,
+        scratch_shapes=sems,
+        compiler_params=pltpu.CompilerParams(
+            collective_id=collective_id, has_side_effects=True, vmem_limit_bytes=VMEM_LIMIT
+        ),
+        name="gather_plane",
+    )(x)
+
+
+def scatter_gains_kernel(planes, p_ref, s_ref, g_ref, o_ref, so_ref, go_ref, small_buf, line_out, line_buf, small_send, small_recv, line_send, line_recv, *rest):
+    rank, plane = lax.axis_index("fsdp"), lax.axis_index("sp")
+    others = [lax.rem(plane + k, planes) for k in range(1, planes)]
+    greet([(rank ^ k, plane) for k in range(1, 8)] + [(rank, other) for other in others])
+    small = []
+    for k in range(1, 8):
+        copy = peer_copy(
+            s_ref.at[rank ^ k],
+            small_buf.at[k - 1],
+            small_send.at[k - 1],
+            small_recv.at[k - 1],
+            rank ^ k,
+            plane,
+        )
+        copy.start()
+        small.append(copy)
+    scatter_blocks(p_ref, o_ref, *rest)
+    total = s_ref[rank]
+    for k in range(1, 8):
+        small[k - 1].wait()
+        total = total + small_buf[k - 1]
+    tail = total.shape[0]
+    line_out[:tail] = total
+    line_out[tail:] = g_ref[...]
+    line = []
+    for k in range(1, planes):
+        copy = peer_copy(
+            line_out,
+            line_buf.at[k - 1],
+            line_send.at[k - 1],
+            line_recv.at[k - 1],
+            rank,
+            others[k - 1],
+        )
+        copy.start()
+        line.append(copy)
+    final = line_out[...]
+    for k in range(1, planes):
+        line[k - 1].wait()
+        final = final + line_buf[k - 1]
+    so_ref[...] = final[:tail]
+    go_ref[...] = final[tail:]
+
+
+def scatter_kernel(*refs):
+    rank, plane = lax.axis_index("fsdp"), lax.axis_index("sp")
+    greet([(rank ^ k, plane) for k in (1, 2, 4, 6)])
+    scatter_blocks(*refs)
+
+
+def scatter_blocks(p_ref, o_ref, near_buf, out_buf, far_buf, sib_send, sib_recv, send_sem, recv_sem):
+    rank, plane = lax.axis_index("fsdp"), lax.axis_index("sp")
+    order = (6, 2, 4, 0)
+    near = []
+    for i, k in enumerate(order):
+        copy = peer_copy(
+            p_ref.at[rank ^ 1 ^ k], near_buf.at[i], sib_send.at[i], sib_recv.at[i], rank ^ 1, plane
+        )
+        copy.start()
+        near.append(copy)
+    far = []
+    for i, k in enumerate(order):
+        near[i].wait_recv()
+        joined = p_ref[rank ^ k].astype(jnp.float32) + near_buf[i].astype(jnp.float32)
+        if k:
+            out_buf[i] = joined.astype(out_buf.dtype)
+            copy = peer_copy(
+                out_buf.at[i], far_buf.at[i], send_sem.at[i], recv_sem.at[i], rank ^ k, plane
+            )
+            copy.start()
+            far.append(copy)
+        else:
+            o_ref[...] = joined
+    for i in (1, 2, 0):
+        far[i].wait_recv()
+        o_ref[...] += far_buf[i].astype(jnp.float32)
+    for copy in near + far:
+        copy.wait_send()
+
+
+def scatter_plane(p, collective_id, small=None, gate=None):
+    ranks, rows, width = p.shape
+    vmem = pl.BlockSpec(memory_space=pltpu.VMEM)
+    scratch = [
+        pltpu.VMEM((4, rows, width), p.dtype),
+        pltpu.VMEM((3, rows, width), p.dtype),
+        pltpu.VMEM((3, rows, width), p.dtype),
+        pltpu.SemaphoreType.DMA((4,)),
+        pltpu.SemaphoreType.DMA((4,)),
+        pltpu.SemaphoreType.DMA((3,)),
+        pltpu.SemaphoreType.DMA((3,)),
+    ]
+    out = jax.ShapeDtypeStruct((rows, width), jnp.float32)
+    params = pltpu.CompilerParams(
+        collective_id=collective_id, has_side_effects=True, vmem_limit_bytes=VMEM_LIMIT
+    )
+    if small is not None:
+        planes = lax.axis_size("sp")
+        joint = (small.shape[1] + gate.shape[0], small.shape[2])
+        return pl.pallas_call(
+            functools.partial(scatter_gains_kernel, planes),
+            out_shape=(
+                out,
+                jax.ShapeDtypeStruct(small.shape[1:], small.dtype),
+                jax.ShapeDtypeStruct(gate.shape, gate.dtype),
+            ),
+            in_specs=[vmem, vmem, vmem],
+            out_specs=(vmem, vmem, vmem),
+            scratch_shapes=[
+                pltpu.VMEM((7,) + small.shape[1:], small.dtype),
+                pltpu.VMEM(joint, small.dtype),
+                pltpu.VMEM((planes - 1,) + joint, small.dtype),
+                pltpu.SemaphoreType.DMA((7,)),
+                pltpu.SemaphoreType.DMA((7,)),
+                pltpu.SemaphoreType.DMA((planes - 1,)),
+                pltpu.SemaphoreType.DMA((planes - 1,)),
+            ]
+            + scratch,
+            compiler_params=params,
+            name="scatter_gains",
+        )(p, small, gate)
+    return pl.pallas_call(
+        scatter_kernel,
+        out_shape=out,
+        in_specs=[vmem],
+        out_specs=vmem,
+        scratch_shapes=scratch,
+        compiler_params=params,
+        name="scatter_plane",
+    )(p)
+
+
+def greet_line(ranks, planes):
+    rank, plane = lax.axis_index("fsdp"), lax.axis_index("sp")
+    barrier = pltpu.get_barrier_semaphore()
+    for k in range(1, ranks):
+        pl.semaphore_signal(
+            barrier, inc=1, device_id=(rank ^ k, plane), device_id_type=MESH
+        )
+
+    @pl.when(plane > 0)
+    def _():
+        pl.semaphore_signal(barrier, inc=1, device_id=(rank, plane - 1), device_id_type=MESH)
+
+    @pl.when(plane < planes - 1)
+    def _():
+        pl.semaphore_signal(barrier, inc=1, device_id=(rank, plane + 1), device_id_type=MESH)
+
+    lower = (plane > 0).astype(jnp.int32)
+    upper = (plane < planes - 1).astype(jnp.int32)
+    pl.semaphore_wait(barrier, ranks - 1 + lower + upper)
+
+
+def heads_kernel(planes, n_ref, q_ref, kv_ref, own_sem, q_send, q_recv, kv_send, kv_recv, line_send, line_recv):
+    rank, plane = lax.axis_index("fsdp"), lax.axis_index("sp")
+    greet_line(8, planes)
+
+    def q_copy(m, to):
+        return peer_copy(n_ref.at[pl.ds(2 * m, 2)], q_ref, q_send.at[m], q_recv, to, plane)
+
+    def kv_copy(m, which, to):
+        return peer_copy(
+            n_ref.at[m], kv_ref.at[plane, which], kv_send.at[m], kv_recv.at[which], to, plane
+        )
+
+    def q_local():
+        return pltpu.make_async_copy(n_ref.at[pl.ds(0, 2)], q_ref, own_sem)
+
+    def kv_local(m, which):
+        return pltpu.make_async_copy(n_ref.at[m], kv_ref.at[plane, which], own_sem)
+
+    @pl.when(rank < 4)
+    def _():
+        for m in range(2):
+            @pl.when(2 * rank + m != rank)
+            def _():
+                q_copy(m, 2 * rank + m).start()
+
+    @pl.when(rank == 0)
+    def _():
+        q_local().start()
+
+    for which in range(2):
+        first = 4 + 2 * which
+        own_m = (first + 1) % 4
+
+        @pl.when((rank == first) | (rank == first + 1))
+        def _():
+            for m in range(4):
+                to = 4 * (rank - first) + m
+
+                @pl.when(to != rank)
+                def _():
+                    kv_copy(m, which, to).start()
+
+        @pl.when(rank == first + 1)
+        def _():
+            kv_local(own_m, which).start()
+
+    for which in range(2):
+        first = 4 + 2 * which
+        own_m = (first + 1) % 4
+
+        @pl.when(rank == first + 1)
+        def _():
+            kv_local(own_m, which).wait()
+
+        @pl.when(rank != first + 1)
+        def _():
+            kv_copy(0, which, 0).wait_recv()
+
+        line_step(planes, kv_ref, which, 0, line_send, line_recv)
+    for j in range(1, planes):
+        for which in range(2):
+            line_step(planes, kv_ref, which, j, line_send, line_recv)
+
+    @pl.when(rank == 0)
+    def _():
+        q_local().wait()
+
+    @pl.when(rank != 0)
+    def _():
+        q_copy(0, 0).wait_recv()
+
+    @pl.when(rank < 4)
+    def _():
+        for m in range(2):
+            @pl.when(2 * rank + m != rank)
+            def _():
+                q_copy(m, 0).wait_send()
+
+    for which in range(2):
+        first = 4 + 2 * which
+
+        @pl.when((rank == first) | (rank == first + 1))
+        def _():
+            for m in range(4):
+                @pl.when(4 * (rank - first) + m != rank)
+                def _():
+                    kv_copy(m, which, 0).wait_send()
+
+    for j in range(planes - 1):
+        for which in range(2):
+            for side in range(2):
+                @pl.when(line_sends(planes, plane, j, side))
+                def _():
+                    line_copy(kv_ref, which, j, side, line_send, line_recv).wait_send()
+
+
+def line_sends(planes, plane, j, side):
+    if side == 0:
+        return (plane >= j) & (plane < planes - 1)
+    return (plane + j <= planes - 1) & (plane > 0)
+
+
+def line_copy(kv_ref, which, j, side, line_send, line_recv):
+    rank, plane = lax.axis_index("fsdp"), lax.axis_index("sp")
+    origin = plane - j if side == 0 else plane + j
+    block = kv_ref.at[origin, which]
+    to = plane + 1 if side == 0 else plane - 1
+    return peer_copy(
+        block, block, line_send.at[side, j, which], line_recv.at[side, j, which], rank, to
+    )
+
+
+def line_step(planes, kv_ref, which, j, line_send, line_recv):
+    rank, plane = lax.axis_index("fsdp"), lax.axis_index("sp")
+    for side in range(2):
+        if j:
+            arrives = (plane >= j) if side == 0 else (plane + j <= planes - 1)
+
+            @pl.when(arrives)
+            def _():
+                origin = plane - j if side == 0 else plane + j
+                block = kv_ref.at[origin, which]
+                peer_copy(
+                    block,
+                    block,
+                    line_send.at[side, j - 1, which],
+                    line_recv.at[side, j - 1, which],
+                    rank,
+                    plane,
+                ).wait_recv()
+
+        if j < planes - 1:
+            @pl.when(line_sends(planes, plane, j, side))
+            def _():
+                line_copy(kv_ref, which, j, side, line_send, line_recv).start()
+
+
+def exchange_heads(natural, collective_id):
+    _, tokens, width = natural.shape
+    planes = lax.axis_size("sp")
+    return pl.pallas_call(
+        functools.partial(heads_kernel, planes),
+        out_shape=(
+            jax.ShapeDtypeStruct((2, tokens, width), natural.dtype),
+            jax.ShapeDtypeStruct((planes, 2, tokens, width), natural.dtype),
+        ),
+        in_specs=[pl.BlockSpec(memory_space=pl.ANY)],
+        out_specs=(pl.BlockSpec(memory_space=pl.ANY), pl.BlockSpec(memory_space=pl.ANY)),
+        scratch_shapes=[
+            pltpu.SemaphoreType.DMA,
+            pltpu.SemaphoreType.DMA((2,)),
+            pltpu.SemaphoreType.DMA,
+            pltpu.SemaphoreType.DMA((4,)),
+            pltpu.SemaphoreType.DMA((2,)),
+            pltpu.SemaphoreType.DMA((2, planes - 1, 2)),
+            pltpu.SemaphoreType.DMA((2, planes - 1, 2)),
+        ],
+        compiler_params=pltpu.CompilerParams(
+            collective_id=collective_id, has_side_effects=True, vmem_limit_bytes=VMEM_LIMIT
+        ),
+        name="exchange_heads",
+    )(natural)
+
+
+def unheads_kernel(planes, dq_ref, dkv_ref, n_ref, line_out, line_in, done, own_sem, q_send, q_recv, kv_send, kv_recv, line_send, line_recv):
+    rank, plane = lax.axis_index("fsdp"), lax.axis_index("sp")
+    greet_line(8, planes)
+
+    def q_copy(m, to):
+        return peer_copy(dq_ref, n_ref.at[pl.ds(2 * m, 2)], q_send, q_recv.at[m], to, plane)
+
+    def kv_copy(m, which, to):
+        return peer_copy(done.at[which], n_ref.at[m], kv_send.at[which], kv_recv.at[m], to, plane)
+
+    def q_local():
+        return pltpu.make_async_copy(dq_ref, n_ref.at[pl.ds(0, 2)], own_sem)
+
+    def kv_local(m, which):
+        return pltpu.make_async_copy(done.at[which], n_ref.at[m], own_sem)
+
+    @pl.when(rank == 0)
+    def _():
+        q_local().start()
+
+    for m in range(2):
+        @pl.when((rank % 2 == m) & (rank != 0))
+        def _():
+            q_copy(m, rank // 2).start()
+
+    def step_copy(j, which, side):
+        to = plane + 1 if side == 0 else plane - 1
+        return peer_copy(
+            line_out.at[side, j, which],
+            line_in.at[side, j, which],
+            line_send.at[side, j, which],
+            line_recv.at[side, j, which],
+            rank,
+            to,
+        )
+
+    def sends(j, side):
+        return plane < planes - 1 - j if side == 0 else plane > j
+
+    def target(j, side):
+        return planes - 1 - j if side == 0 else j
+
+    for j in range(planes - 1):
+        for which in range(2):
+            for side in range(2):
+                inner = plane > 0 if side == 0 else plane < planes - 1
+
+                @pl.when(sends(j, side) & inner)
+                def _():
+                    step_copy(j, which, side).wait_recv()
+                    total = dkv_ref[target(j, side), which].astype(jnp.float32) + line_in[
+                        side, j, which
+                    ].astype(jnp.float32)
+                    line_out[side, j, which] = total.astype(line_out.dtype)
+
+                @pl.when(sends(j, side) & jnp.logical_not(inner))
+                def _():
+                    line_out[side, j, which] = dkv_ref[target(j, side), which]
+
+                @pl.when(sends(j, side))
+                def _():
+                    step_copy(j, which, side).start()
+
+    for which in range(2):
+        total = dkv_ref[plane, which].astype(jnp.float32)
+        done32 = total
+        for j in range(planes - 1):
+            for side in range(2):
+                @pl.when(plane == target(j, side))
+                def _():
+                    step_copy(j, which, side).wait_recv()
+        low = jnp.minimum(planes - 1 - plane, planes - 2)
+        high = jnp.minimum(plane, planes - 2)
+        below = line_in[0, low, which].astype(jnp.float32)
+        above = line_in[1, high, which].astype(jnp.float32)
+        done32 = done32 + jnp.where(plane > 0, below, 0.0) + jnp.where(plane < planes - 1, above, 0.0)
+        done[which] = done32.astype(done.dtype)
+        first = 4 + 2 * which
+        to = first + rank // 4
+        for m in range(4):
+            @pl.when((rank % 4 == m) & (to != rank))
+            def _():
+                kv_copy(m, which, to).start()
+
+            @pl.when((rank % 4 == m) & (to == rank))
+            def _():
+                kv_local(m, which).start()
+
+    @pl.when(rank < 4)
+    def _():
+        for m in range(2):
+            @pl.when(2 * rank + m != rank)
+            def _():
+                q_copy(m, 0).wait_recv()
+
+            @pl.when(2 * rank + m == rank)
+            def _():
+                q_local().wait()
+
+    for which in range(2):
+        first = 4 + 2 * which
+
+        @pl.when((rank == first) | (rank == first + 1))
+        def _():
+            for m in range(4):
+                @pl.when(4 * (rank - first) + m != rank)
+                def _():
+                    kv_copy(m, which, 0).wait_recv()
+
+                @pl.when(4 * (rank - first) + m == rank)
+                def _():
+                    kv_local(m, which).wait()
+
+    @pl.when(rank != 0)
+    def _():
+        q_copy(0, 0).wait_send()
+
+    for which in range(2):
+        @pl.when(4 + 2 * which + rank // 4 != rank)
+        def _():
+            kv_copy(0, which, 0).wait_send()
+
+    for j in range(planes - 1):
+        for which in range(2):
+            for side in range(2):
+                @pl.when(sends(j, side))
+                def _():
+                    step_copy(j, which, side).wait_send()
+
+
+def return_heads(grad_query, grad_kv, collective_id):
+    _, tokens, width = grad_query.shape
+    planes = lax.axis_size("sp")
+    vmem = pl.BlockSpec(memory_space=pltpu.VMEM)
+    return pl.pallas_call(
+        functools.partial(unheads_kernel, planes),
+        out_shape=jax.ShapeDtypeStruct((4, tokens, width), grad_query.dtype),
+        in_specs=[vmem, vmem],
+        out_specs=vmem,
+        scratch_shapes=[
+            pltpu.VMEM((2, planes - 1, 2, tokens, width), grad_query.dtype),
+            pltpu.VMEM((2, planes - 1, 2, tokens, width), grad_query.dtype),
+            pltpu.VMEM((2, tokens, width), grad_query.dtype),
+            pltpu.SemaphoreType.DMA,
+            pltpu.SemaphoreType.DMA,
+            pltpu.SemaphoreType.DMA((2,)),
+            pltpu.SemaphoreType.DMA((2,)),
+            pltpu.SemaphoreType.DMA((4,)),
+            pltpu.SemaphoreType.DMA((2, planes - 1, 2)),
+            pltpu.SemaphoreType.DMA((2, planes - 1, 2)),
+        ],
+        compiler_params=pltpu.CompilerParams(
+            collective_id=collective_id, has_side_effects=True, vmem_limit_bytes=VMEM_LIMIT
+        ),
+        name="return_heads",
+    )(grad_query, grad_kv)
+
+
+def stack_heads(ref):
+    return ref[...].reshape(ref.shape[0] * ref.shape[1], ref.shape[2])
+
+
+def block_bounds(lengths_ref, ranks, planes, rows):
+    block = pl.program_id(0)
+    span = planes * rows
+    first = block * span + lax.axis_index("sp") * rows
+    start, end = jnp.int32(0), jnp.int32(0)
+    for item in range(lengths_ref.shape[0]):
+        end = end + lengths_ref[item]
+        start = jnp.where(first >= end, end, start)
+    return start // span, block, first
+
+
+def row_starts(lengths_ref, tokens):
+    start, end = jnp.zeros_like(tokens), jnp.int32(0)
+    for item in range(lengths_ref.shape[0]):
+        end = end + lengths_ref[item]
+        start = jnp.where(tokens >= end, end, start)
+    return start
+
+
+def chunk_weights(query, key, scale, tokens, starts, first_key):
+    scores = mat_nt(query, key) * scale
+    columns = first_key + lax.broadcasted_iota(jnp.int32, scores.shape, 1)
+    allowed = (columns <= tokens) & (columns >= starts)
+    return jnp.where(allowed, jnp.exp(scores), 0.0)
+
+
+def query_tokens(first, rows, group):
+    row = lax.broadcasted_iota(jnp.int32, (group * rows, 1), 0)
+    return first + lax.rem(row, rows)
+
+
+def attend_kernel(ranks, planes, lengths_ref, q_ref, kv_ref, gate_ref, att_ref, total_ref, gated_ref):
+    group, rows, width = q_ref.shape
+    scale = HEAD_DIM ** (-0.5)
+    low, high, first = block_bounds(lengths_ref, ranks, planes, rows)
+    tokens = query_tokens(first, rows, group)
+    starts = row_starts(lengths_ref, tokens)
+    query = stack_heads(q_ref)
+    span = planes * rows
+
+    def step(chunk, running):
+        total, unnorm = running
+        key = kv_ref[:, 0, chunk].reshape(span, width)
+        value = kv_ref[:, 1, chunk].reshape(span, width)
+        weights = chunk_weights(query, key, scale, tokens, starts, chunk * span)
+        total = total + jnp.sum(weights, axis=1, keepdims=True)
+        unnorm = unnorm + jnp.dot(
+            weights.astype(jnp.bfloat16), value, preferred_element_type=jnp.float32
+        )
+        return total, unnorm
+
+    total, unnorm = lax.fori_loop(
+        low,
+        high + 1,
+        step,
+        (
+            jnp.zeros((group * rows, 1), jnp.float32),
+            jnp.zeros((group * rows, width), jnp.float32),
+        ),
+    )
+    attended = unnorm / total
+    att_ref[...] = attended.reshape(group, rows, width)
+    total_ref[...] = total.reshape(group, rows, 1)
+    sent = attended.astype(jnp.bfloat16).astype(jnp.float32)
+    for head in range(group):
+        gated = sent[head * rows : (head + 1) * rows] * jax.nn.sigmoid(gate_ref[head])
+        gated_ref[:, head * width : (head + 1) * width] = gated.astype(jnp.bfloat16)
+
+
+def attend(lengths, query, kv, gate_logit, rows):
+    group, tokens, width = query.shape
+    planes = kv.shape[0]
+    ranks = tokens // rows
+    kv_blocks = kv.reshape(planes, 2, ranks, rows, width)
+    block = pl.BlockSpec((group, rows, width), lambda i, *_: (0, i, 0))
+    thin = pl.BlockSpec((group, rows, 1), lambda i, *_: (0, i, 0))
+    return pl.pallas_call(
+        functools.partial(attend_kernel, ranks, planes),
+        grid_spec=pltpu.PrefetchScalarGridSpec(
+            num_scalar_prefetch=1,
+            grid=(ranks,),
+            in_specs=[
+                block,
+                pl.BlockSpec((planes, 2, ranks, rows, width), lambda i, *_: (0, 0, 0, 0, 0)),
+                thin,
+            ],
+            out_specs=(
+                block,
+                thin,
+                pl.BlockSpec((rows, group * width), lambda i, *_: (i, 0)),
+            ),
+        ),
+        out_shape=(
+            jax.ShapeDtypeStruct((group, tokens, width), jnp.float32),
+            jax.ShapeDtypeStruct((group, tokens, 1), jnp.float32),
+            jax.ShapeDtypeStruct((tokens, group * width), jnp.bfloat16),
+        ),
+        compiler_params=pltpu.CompilerParams(vmem_limit_bytes=VMEM_LIMIT),
+        name="attend",
+    )(lengths, query, kv_blocks, gate_logit)
+
+
+def attend_back_kernel(
+    ranks, planes, lengths_ref, q_ref, kv_ref, gate_ref, att_ref, total_ref, dgated_ref, dq_ref, dkv_ref, dgate_ref, sums
+):
+    group, rows, width = q_ref.shape
+    scale = HEAD_DIM ** (-0.5)
+    low, high, first = block_bounds(lengths_ref, ranks, planes, rows)
+    tokens = query_tokens(first, rows, group)
+    starts = row_starts(lengths_ref, tokens)
+    query = stack_heads(q_ref)
+    span = planes * rows
+
+    @pl.when(pl.program_id(0) == 0)
+    def _():
+        sums[...] = jnp.zeros_like(sums)
+
+    attended = stack_heads(att_ref)
+    sent = attended.astype(jnp.bfloat16).astype(jnp.float32)
+    total = stack_heads(total_ref)
+    logit = stack_heads(gate_ref)
+    prob = jax.nn.sigmoid(logit)
+    dgated = jnp.concatenate(
+        [dgated_ref[:, head * width : (head + 1) * width] for head in range(group)], axis=0
+    )
+    dattended = (dgated * prob).astype(jnp.bfloat16)
+    dlogit = jnp.sum(dgated * sent, axis=1, keepdims=True) * prob * (1.0 - prob)
+    dgate_ref[...] = dlogit.astype(jnp.bfloat16).reshape(group, rows, 1)
+    dattended = dattended.astype(jnp.float32)
+    scaled = (dattended / total).astype(jnp.bfloat16)
+    delta = jnp.sum(dattended * attended, axis=1, keepdims=True) / total
+
+    def step(chunk, dquery):
+        key = kv_ref[:, 0, chunk].reshape(span, width)
+        value = kv_ref[:, 1, chunk].reshape(span, width)
+        weights = chunk_weights(query, key, scale, tokens, starts, chunk * span)
+        dprob = mat_nt(scaled, value)
+        dscore = (weights * (dprob - delta)).astype(jnp.bfloat16)
+        dquery = dquery + jnp.dot(dscore, key, preferred_element_type=jnp.float32)
+        dkey = mat_tn(dscore, query)
+        dvalue = mat_tn(weights.astype(jnp.bfloat16), scaled)
+        sums[:, 0, chunk] += dkey.reshape(planes, rows, width)
+        sums[:, 1, chunk] += dvalue.reshape(planes, rows, width)
+        return dquery
+
+    dquery = lax.fori_loop(
+        low, high + 1, step, jnp.zeros((group * rows, width), jnp.float32)
+    )
+    dq_ref[...] = (dquery * scale).astype(jnp.bfloat16).reshape(group, rows, width)
+
+    @pl.when(pl.program_id(0) == ranks - 1)
+    def _():
+        for chunk in range(ranks):
+            dkv_ref[:, 0, chunk] = (sums[:, 0, chunk] * scale).astype(jnp.bfloat16)
+            dkv_ref[:, 1, chunk] = sums[:, 1, chunk].astype(jnp.bfloat16)
+
+
+def attend_back(lengths, query, kv, gate_logit, attended, total, dgated, rows):
+    group, tokens, width = query.shape
+    planes = kv.shape[0]
+    ranks = tokens // rows
+    kv_blocks = kv.reshape(planes, 2, ranks, rows, width)
+    block = pl.BlockSpec((group, rows, width), lambda i, *_: (0, i, 0))
+    thin = pl.BlockSpec((group, rows, 1), lambda i, *_: (0, i, 0))
+    whole = pl.BlockSpec((planes, 2, ranks, rows, width), lambda i, *_: (0, 0, 0, 0, 0))
+    dquery, dkv, dgate = pl.pallas_call(
+        functools.partial(attend_back_kernel, ranks, planes),
+        grid_spec=pltpu.PrefetchScalarGridSpec(
+            num_scalar_prefetch=1,
+            grid=(ranks,),
+            in_specs=[
+                block,
+                whole,
+                thin,
+                block,
+                thin,
+                pl.BlockSpec((rows, group * width), lambda i, *_: (i, 0)),
+            ],
+            out_specs=(block, whole, thin),
+            scratch_shapes=[pltpu.VMEM((planes, 2, ranks, rows, width), jnp.float32)],
+        ),
+        out_shape=(
+            jax.ShapeDtypeStruct((group, tokens, width), jnp.bfloat16),
+            jax.ShapeDtypeStruct((planes, 2, ranks, rows, width), jnp.bfloat16),
+            jax.ShapeDtypeStruct((group, tokens, 1), jnp.bfloat16),
+        ),
+        compiler_params=pltpu.CompilerParams(vmem_limit_bytes=VMEM_LIMIT),
+        name="attend_back",
+    )(lengths, query, kv_blocks, gate_logit, attended, total, dgated)
+    return dquery, dkv.reshape(planes, 2, tokens, width), dgate
+
+
+GATHER_COPIES = 13
+
+
+def gather_copy(buf, i, send_sem, recv_sem):
+    rank, plane = lax.axis_index("fsdp"), lax.axis_index("sp")
+    rows = buf.shape[1]
+    top, low = pl.ds(0, rows // 2), pl.ds(rows // 2, rows // 2)
+    block, part, to = (
+        (0, top, 2),
+        (0, low, 2),
+        (0, low, 4),
+        (0, top, 4),
+        (2, top, 4),
+        (4, low, 2),
+        (0, pl.ds(0, rows), 1),
+        (2, top, 1),
+        (2, low, 1),
+        (4, low, 1),
+        (4, top, 1),
+        (6, top, 1),
+        (6, low, 1),
+    )[i]
+    piece = buf.at[rank ^ block, part]
+    return peer_copy(piece, piece, send_sem.at[i], recv_sem.at[i], rank ^ to, plane)
+
+
+def gather_start(buf, send_sem, recv_sem):
+    for i in (6, 0, 2, 1, 3):
+        gather_copy(buf, i, send_sem, recv_sem).start()
+
+
+def gather_pass(buf, send_sem, recv_sem, pairs):
+    for arrived, onward in pairs:
+        gather_copy(buf, arrived, send_sem, recv_sem).wait_recv()
+        for i in onward:
+            gather_copy(buf, i, send_sem, recv_sem).start()
+
+
+def gather_wait(buf, send_sem, recv_sem, copies):
+    for i in copies:
+        gather_copy(buf, i, send_sem, recv_sem).wait_recv()
+
+
+NEIGHBOURS_FIRST = ((0, (4, 7)), (2, (5, 9)), (1, (8,)), (3, (10,)))
+DIAGONAL = ((4, (11,)), (5, (12,)))
+
+
+def middle_kernel(
+    gated_ref,
+    wout_ref,
+    x_ref,
+    scale_ref,
+    dy_hbm,
+    wg_hbm,
+    wu_hbm,
+    wd_hbm,
+    xb_ref,
+    down_hbm,
+    mid_ref,
+    dmid_ref,
+    gain_ref,
+    pm_ref,
+    dgated_ref,
+    wg,
+    wu,
+    wd,
+    dy,
+    dhid,
+    xg,
+    near_out,
+    near_in,
+    far_out,
+    far_in,
+    keep,
+    down_buf,
+    load_sem,
+    dy_sem,
+    down_sem,
+    near_send,
+    near_recv,
+    far_send,
+    far_recv,
+    ag_send,
+    ag_recv,
+):
+    rank, plane = lax.axis_index("fsdp"), lax.axis_index("sp")
+    ranks, rows, width = xg.shape
+    loads = [
+        pltpu.make_async_copy(wd_hbm, wd, load_sem.at[0]),
+        pltpu.make_async_copy(wg_hbm, wg, load_sem.at[1]),
+        pltpu.make_async_copy(wu_hbm, wu, load_sem.at[2]),
+    ]
+    dy_loads = [
+        pltpu.make_async_copy(dy_hbm.at[r, plane], dy.at[r], dy_sem.at[r]) for r in range(ranks)
+    ]
+    greet([(rank ^ k, plane) for k in (1, 2, 4, 6)])
+
+    def near(phase, i):
+        return peer_copy(
+            near_out.at[phase, i],
+            near_in.at[phase, i],
+            near_send.at[phase, i],
+            near_recv.at[phase, i],
+            rank ^ 1,
+            plane,
+        )
+
+    def far(phase, i, k):
+        return peer_copy(
+            far_out.at[phase, i],
+            far_in.at[phase, i],
+            far_send.at[phase, i],
+            far_recv.at[phase, i],
+            rank ^ k,
+            plane,
+        )
+
+    order = (6, 2, 4, 0)
+    for i, k in enumerate(order):
+        part = jnp.dot(
+            gated_ref[rank ^ 1 ^ k], wout_ref[...], preferred_element_type=jnp.float32
+        )
+        near_out[0, i] = part.astype(jnp.bfloat16)
+        near(0, i).start()
+    for copy in dy_loads + loads:
+        copy.start()
+    for i, k in enumerate(order):
+        part = jnp.dot(gated_ref[rank ^ k], wout_ref[...], preferred_element_type=jnp.float32)
+        near(0, i).wait_recv()
+        part = part + near_in[0, i].astype(jnp.float32)
+        if k:
+            far_out[0, i] = part.astype(jnp.bfloat16)
+            far(0, i, k).start()
+        else:
+            keep[...] = part
+
+    for copy in dy_loads:
+        copy.wait()
+    loads[0].wait()
+
+    @pl.loop(0, ranks // 2)
+    def _(p):
+        pair = dy[pl.ds(2 * p, 2)].reshape(2 * rows, width)
+        dhid[p] = mat_nt(pair, wd[...])
+
+    loads[1].wait()
+    loads[2].wait()
+    middle = x_ref[...].astype(jnp.float32) + keep[...]
+    for i in (1, 2, 0):
+        far(0, i, order[i]).wait_recv()
+        middle = middle + far_in[0, i].astype(jnp.float32)
+    inverse = inv_rms(middle)
+    mid_ref[...] = middle
+    normed = (middle * inverse * scale_ref[...]).astype(jnp.bfloat16)
+    xb_ref[...] = normed
+    xg[rank] = normed
+    sems = (ag_send.at[0], ag_recv.at[0])
+    gather_start(xg, *sems)
+
+    slots = {2: 0, 4: 1, 6: 2, 0: 3}
+
+    def down_copy(p, slot):
+        return pltpu.make_async_copy(
+            down_buf.at[slot], down_hbm.at[pl.ds(2 * p, 2)], down_sem.at[slot]
+        )
+
+    def feed(k):
+        p = (rank ^ k) // 2
+        slot = (0, 2, 4, 6).index(k) % 2
+        pair = xg[pl.ds(2 * p, 2)].reshape(2 * rows, width)
+        gate_pre = mat_nt(pair, wg[...])
+        up_pre = mat_nt(pair, wu[...])
+        grad_hidden = dhid[p]
+        sigma = jax.nn.sigmoid(gate_pre)
+        swish = gate_pre * sigma
+        grad_gate = (grad_hidden * up_pre * sigma * (1.0 + gate_pre * (1.0 - sigma))).astype(
+            jnp.bfloat16
+        )
+        grad_up = (grad_hidden * swish).astype(jnp.bfloat16)
+        part = jnp.dot(grad_gate, wg[...], preferred_element_type=jnp.float32) + jnp.dot(
+            grad_up, wu[...], preferred_element_type=jnp.float32
+        )
+        i = slots[k]
+        halves = part.reshape(2, rows, width)
+        mine_first = lax.rem(rank, 2) == 0
+        mine = jnp.where(mine_first, halves[0], halves[1])
+        theirs = jnp.where(mine_first, halves[1], halves[0])
+        near_out[1, i] = theirs.astype(jnp.bfloat16)
+        near(1, i).start()
+        hidden = (swish * up_pre).astype(jnp.bfloat16)
+        down = jnp.dot(hidden, wd[...], preferred_element_type=jnp.float32)
+        if k in (4, 6):
+            down_copy(p, slot).wait()
+        down_buf[slot] = down.astype(jnp.bfloat16).reshape(2, rows, width)
+        down_copy(p, slot).start()
+        near(1, i).wait_recv()
+        mine = mine + near_in[1, i].astype(jnp.float32)
+        if k:
+            far_out[1, i] = mine.astype(jnp.bfloat16)
+            far(1, i, k).start()
+        else:
+            keep[...] = mine
+
+    gather_wait(xg, *sems, (6,))
+    feed(0)
+    gather_pass(xg, *sems, NEIGHBOURS_FIRST)
+    gather_wait(xg, *sems, (7, 8))
+    feed(2)
+    gather_pass(xg, *sems, DIAGONAL)
+    gather_wait(xg, *sems, (9, 10))
+    feed(4)
+    gather_wait(xg, *sems, (11, 12))
+    feed(6)
+
+    grad = keep[...]
+    for i, k in enumerate((2, 4, 6)):
+        far(1, i, k).wait_recv()
+        grad = grad + far_in[1, i].astype(jnp.float32)
+    middle = mid_ref[...]
+    inverse = inv_rms(middle)
+    gain_ref[...] = jnp.sum(grad * middle * inverse, axis=0, keepdims=True)
+    grad_middle = dy[rank].astype(jnp.float32) + norm_back(
+        grad, middle, inverse, scale_ref[...]
+    )
+    dmid_ref[...] = grad_middle
+    pm_ref[rank] = grad_middle.astype(jnp.bfloat16)
+    sems2 = (ag_send.at[1], ag_recv.at[1])
+    gather_start(pm_ref, *sems2)
+
+    def gated_grad(k):
+        p = (rank ^ k) // 2
+        pair = pm_ref[pl.ds(2 * p, 2)].reshape(2 * rows, width)
+        dgated_ref[pl.ds(2 * p, 2)] = mat_nt(pair, wout_ref[...]).reshape(
+            2, rows, wout_ref.shape[0]
+        )
+
+    gather_wait(pm_ref, *sems2, (6,))
+    gated_grad(0)
+    gather_pass(pm_ref, *sems2, NEIGHBOURS_FIRST)
+    gather_wait(pm_ref, *sems2, (7, 8))
+    gated_grad(2)
+    gather_wait(pm_ref, *sems2, (9, 10))
+    gated_grad(4)
+    gather_pass(pm_ref, *sems2, DIAGONAL)
+    gather_wait(pm_ref, *sems2, (11, 12))
+    gated_grad(6)
+
+    for i in range(GATHER_COPIES):
+        gather_copy(xg, i, *sems).wait_send()
+        gather_copy(pm_ref, i, *sems2).wait_send()
+    for phase in range(2):
+        for i in range(4):
+            near(phase, i).wait_send()
+        for i in range(3):
+            far(phase, i, 2).wait_send()
+    down_copy(0, 0).wait()
+    down_copy(0, 1).wait()
+
+
+def middle_layer(gated, w_out, x, scale, grad_all, w_gate, w_up, w_down, collective_id):
+    ranks, rows, _ = gated.shape
+    width = x.shape[1]
+    hidden = w_gate.shape[0]
+    features = w_out.shape[0]
+    vmem = pl.BlockSpec(memory_space=pltpu.VMEM)
+    hbm = pl.BlockSpec(memory_space=pl.ANY)
+    half, full = jnp.bfloat16, jnp.float32
+    return pl.pallas_call(
+        middle_kernel,
+        out_shape=(
+            jax.ShapeDtypeStruct((rows, width), half),
+            jax.ShapeDtypeStruct((ranks, rows, width), half),
+            jax.ShapeDtypeStruct((rows, width), full),
+            jax.ShapeDtypeStruct((rows, width), full),
+            jax.ShapeDtypeStruct((1, width), full),
+            jax.ShapeDtypeStruct((ranks, rows, width), half),
+            jax.ShapeDtypeStruct((ranks, rows, features), full),
+        ),
+        in_specs=[vmem, vmem, vmem, vmem, hbm, hbm, hbm, hbm],
+        out_specs=(vmem, hbm, vmem, vmem, vmem, vmem, vmem),
+        scratch_shapes=[
+            pltpu.VMEM((hidden, width), half),
+            pltpu.VMEM((hidden, width), half),
+            pltpu.VMEM((hidden, width), half),
+            pltpu.VMEM((ranks, rows, width), half),
+            pltpu.VMEM((ranks // 2, 2 * rows, hidden), full),
+            pltpu.VMEM((ranks, rows, width), half),
+            pltpu.VMEM((2, 4, rows, width), half),
+            pltpu.VMEM((2, 4, rows, width), half),
+            pltpu.VMEM((2, 3, rows, width), half),
+            pltpu.VMEM((2, 3, rows, width), half),
+            pltpu.VMEM((rows, width), full),
+            pltpu.VMEM((2, 2, rows, width), half),
+            pltpu.SemaphoreType.DMA((3,)),
+            pltpu.SemaphoreType.DMA((ranks,)),
+            pltpu.SemaphoreType.DMA((2,)),
+            pltpu.SemaphoreType.DMA((2, 4)),
+            pltpu.SemaphoreType.DMA((2, 4)),
+            pltpu.SemaphoreType.DMA((2, 3)),
+            pltpu.SemaphoreType.DMA((2, 3)),
+            pltpu.SemaphoreType.DMA((2, GATHER_COPIES)),
+            pltpu.SemaphoreType.DMA((2, GATHER_COPIES)),
+        ],
+        compiler_params=pltpu.CompilerParams(
+            collective_id=collective_id, has_side_effects=True, vmem_limit_bytes=VMEM_LIMIT
+        ),
+        name="middle_layer",
+    )(gated, w_out, x, scale, grad_all, w_gate, w_up, w_down)
+
+
+def feed_weights_kernel(x_ref, g_ref, wg_ref, wu_ref, wd_ref, og_ref, ou_ref, od_ref):
+    normed, grad = x_ref[...], g_ref[...]
+    gate_pre = mat_nt(normed, wg_ref[...])
+    up_pre = mat_nt(normed, wu_ref[...])
+    grad_hidden = mat_nt(grad, wd_ref[...])
+    sigma = jax.nn.sigmoid(gate_pre)
+    swish = gate_pre * sigma
+    hidden = (swish * up_pre).astype(jnp.bfloat16)
+    grad_gate = (grad_hidden * up_pre * sigma * (1.0 + gate_pre * (1.0 - sigma))).astype(
+        jnp.bfloat16
+    )
+    grad_up = (grad_hidden * swish).astype(jnp.bfloat16)
+
+    @pl.when(pl.program_id(0) == 0)
+    def _():
+        for ref in (og_ref, ou_ref, od_ref):
+            ref[...] = jnp.zeros_like(ref)
+
+    og_ref[...] += mat_tn(grad_gate, normed)
+    ou_ref[...] += mat_tn(grad_up, normed)
+    od_ref[...] += mat_tn(hidden, grad)
+
+
+def feed_weights(normed, grad, w_gate, w_up, w_down):
+    tokens, width = normed.shape
+    chunk = 512
+    moving = pl.BlockSpec((chunk, width), lambda i: (i, 0))
+    still = pl.BlockSpec(w_gate.shape, lambda i: (0, 0), pipeline_mode=pl.Buffered(1))
+    flops = 12 * tokens * w_gate.size
+    return pl.pallas_call(
+        feed_weights_kernel,
+        grid=(tokens // chunk,),
+        in_specs=[moving, moving, still, still, still],
+        out_specs=(still, still, still),
+        out_shape=[jax.ShapeDtypeStruct(w_gate.shape, jnp.float32)] * 3,
+        cost_estimate=pl.CostEstimate(
+            flops=flops,
+            bytes_accessed=4 * normed.size + 18 * w_gate.size,
+            transcendentals=tokens * w_gate.shape[0],
+        ),
+        compiler_params=pltpu.CompilerParams(vmem_limit_bytes=VMEM_LIMIT),
+        name="feed_weights",
+    )(normed, grad, w_gate, w_up, w_down)
+
+
+def local_planes(
+    hidden_in,
+    grad_out,
+    lengths,
+    attn_gain,
+    w_qkv,
+    w_head_gate,
+    q_gain,
+    k_gain,
+    w_out,
+    ffn_gain,
+    w_gate,
+    w_up,
+    w_down,
+):
+    ranks, planes = lax.axis_size("fsdp"), lax.axis_size("sp")
+    rank, plane = lax.axis_index("fsdp"), lax.axis_index("sp")
+    rows, model_width = hidden_in.shape
+    tokens = ranks * rows
+    both = ("fsdp", "sp")
+    own_heads = w_qkv.shape[0] // HEAD_DIM
+    local_heads = HEADS // ranks
+
+    wide, thin = attn_gain.shape[0], q_gain.shape[0]
+    used = 2 * wide + 2 * thin
+    own_gains = jnp.concatenate(
+        [attn_gain, ffn_gain, q_gain, k_gain, jnp.zeros((8 * HEAD_DIM - used,), attn_gain.dtype)]
+    ).astype(jnp.float32)
+    gathered, gains = gather_plane(hidden_in, 0, own_gains.reshape(8, HEAD_DIM))
+    gains = gains.reshape(ranks, 8 * HEAD_DIM)
+    attn_scale = gains[:, :wide].reshape(-1)
+    ffn_scale = gains[:, wide : 2 * wide].reshape(-1)
+    query_scale = gains[:, 2 * wide : 2 * wide + thin].reshape(-1)
+    key_scale = gains[:, 2 * wide + thin : used].reshape(-1)
+
+    grad_later, gathered = lax.optimization_barrier((grad_out, gathered))
+    grad_all = lax.all_gather(grad_later, both, axis=0, tiled=True)
+
+    token_block = jnp.arange(ranks, dtype=jnp.int32) * (planes * rows) + plane * rows
+    plane_tokens = (token_block[:, None] + jnp.arange(rows, dtype=jnp.int32)[None]).reshape(-1)
+    cosine, sine = rope_tables(plane_tokens - item_starts(plane_tokens, lengths))
+
+    inputs = gathered.reshape(tokens, model_width).astype(jnp.float32)
+    inv_first = inv_rms(inputs)
+    normed_a = (inputs * inv_first * attn_scale).astype(jnp.bfloat16)
+    projected = mat_nt(normed_a, w_qkv)
+    gate_logit = mat_nt(w_head_gate, normed_a)[:, :, None]
+    raw = projected.reshape(tokens, own_heads, HEAD_DIM)
+    raw_inv = inv_rms(raw)
+    is_query, is_value = rank < ranks // 2, rank >= 3 * ranks // 4
+    head_scale = jnp.where(is_query, query_scale, key_scale)
+    turned = rotate(raw * raw_inv * head_scale, cosine, sine)
+    natural = jnp.where(is_value, raw, turned).astype(jnp.bfloat16)
+    query, kv = exchange_heads(jnp.transpose(natural, (1, 0, 2)), 1)
+
+    attended, total, gated = attend(lengths, query, kv, gate_logit, rows)
+    own_inputs = hidden_in.astype(jnp.float32)
+    normed_b, down_part, middle, grad_middle, grad_ffn_gain_local, plane_mid, grad_gated = middle_layer(
+        gated.reshape(ranks, rows, -1),
+        w_out,
+        hidden_in,
+        ffn_scale.reshape(1, -1),
+        grad_all.reshape(ranks, planes, rows, model_width),
+        w_gate,
+        w_up,
+        w_down,
+        2,
+    )
+    plane_mid = plane_mid.reshape(tokens, model_width)
+    grad_gated = grad_gated.reshape(tokens, -1)
+    all_b = lax.all_gather(normed_b, both, axis=0, tiled=True)
+    grad_query, grad_kv, gate_grad = attend_back(
+        lengths, query, kv, gate_logit, attended, total, grad_gated, rows
+    )
+    back = return_heads(grad_query, grad_kv, 6)
+    back = jnp.transpose(back, (1, 0, 2))
+    turned_back = rotate_back(back.astype(jnp.float32), cosine, sine)
+    gain_terms = jnp.sum(turned_back * raw * raw_inv, axis=(0, 1))
+    raw_back = norm_back(turned_back, raw, raw_inv, head_scale).astype(jnp.bfloat16)
+    grad_proj = jnp.where(is_value, back, raw_back).reshape(tokens, own_heads * HEAD_DIM)
+    gate_grad = gate_grad.reshape(local_heads, tokens)
+    grad_a_part = jnp.dot(grad_proj, w_qkv, preferred_element_type=jnp.float32) + mat_tn(
+        gate_grad, w_head_gate
+    )
+    nothing = jnp.zeros((HEAD_DIM,), jnp.float32)
+    gain_parts = jnp.concatenate(
+        [
+            jnp.sum(grad_a_part * inputs * inv_first, axis=0).reshape(ranks, wide),
+            grad_ffn_gain_local.reshape(ranks, wide),
+            jnp.where(is_query, gain_terms, nothing).reshape(ranks, thin),
+            jnp.where(is_query | is_value, nothing, gain_terms).reshape(ranks, thin),
+            jnp.zeros((ranks, 8 * HEAD_DIM - used), jnp.float32),
+        ],
+        axis=1,
+    )
+    grad_a_part, grad_proj, down_part, plane_mid, all_b = lax.optimization_barrier(
+        (grad_a_part, grad_proj, down_part, plane_mid, all_b)
+    )
+    ffn_out = lax.psum_scatter(
+        down_part.reshape(tokens, model_width), "fsdp", scatter_dimension=0, tiled=True
+    )
+    hidden_out = (middle + ffn_out.astype(jnp.float32)).astype(jnp.bfloat16)
+    gate_rows_part = jnp.dot(gate_grad, normed_a, preferred_element_type=jnp.float32)
+    grad_a, gain_total, gate_total = scatter_plane(
+        grad_a_part.astype(jnp.bfloat16).reshape(ranks, rows, model_width),
+        7,
+        gain_parts.reshape(ranks, 8, HEAD_DIM),
+        gate_rows_part.reshape(-1, HEAD_DIM),
+    )
+    own_inv = inv_rms(own_inputs)
+    grad_in = grad_middle + norm_back(grad_a, own_inputs, own_inv, attn_scale)
+
+    def over_planes(part):
+        reduced = lax.psum_scatter(
+            part.astype(jnp.bfloat16), "sp", scatter_dimension=0, tiled=True
+        )
+        return lax.all_gather(reduced, "sp", axis=0, tiled=True).astype(jnp.float32)
+
+    grad_w_out = over_planes(mat_tn(gated, plane_mid))
+    grad_w_qkv = over_planes(mat_tn(grad_proj, normed_a))
+    grad_w_head_gate = gate_total.reshape(w_head_gate.shape)
+
+    all_b, grad_a = lax.optimization_barrier((all_b, grad_a))
+    grad_w_gate, grad_w_up, grad_w_down = feed_weights(all_b, grad_all, w_gate, w_up, w_down)
+
+    gain_total = gain_total.reshape(-1)
+    grad_attn_gain = gain_total[:wide]
+    grad_ffn_gain = gain_total[wide : 2 * wide]
+    grad_q_gain = gain_total[2 * wide : 2 * wide + thin]
+    grad_k_gain = gain_total[2 * wide + thin : used]
+    return (
+        hidden_out,
+        grad_in,
+        grad_attn_gain,
+        grad_w_qkv,
+        grad_w_head_gate,
+        grad_q_gain,
+        grad_k_gain,
+        grad_w_out,
+        grad_ffn_gain,
+        grad_w_gate,
+        grad_w_up,
+        grad_w_down,
+    )
+
+
 def solution(mesh):
+    planar = mesh.shape["fsdp"] == 8 and mesh.shape["sp"] == 4
     return jax.shard_map(
-        local,
+        local_planes if planar else local,
         mesh=mesh,
         in_specs=(
             P(("fsdp", "sp"), None),

time: 2860 us -> 671 us (0.23)
  blocking collectives: 1210 us -> 0 us
  waiting for transfers between devices: 1070 us -> 89.9 us
  Pallas kernels: 0 us -> 479 us
  local copies, waits for them, and re-layouts: 189 us -> 17.5 us
  matrix products: 189 us -> 25.7 us
  other arithmetic: 130 us -> 35.2 us
  starting transfers between devices: 31.7 us -> 0.28 us
    psum x1 -> x0, blocking collectives: 633 us -> none  [local(): ffn_total, attn_total = lax.psum((ffn_partial, attn_partial), 'sp')]
    unnamed x2 -> x0, blocking collectives: 511 us -> none
    pallas_call x0 -> x8, Pallas kernels: none -> 479 us  [the longest x1 107 us: exchange_heads(): pl.pallas_call(functools.partial(heads_kernel, planes), out_shape=(jax.Sh...]
    reduce_scatter x3, waiting for transfers between devices: 485 us -> 30.4 us  [the longest x2 30.4 us: over_planes(): lax.psum_scatter(part.astype(jnp.bfloat16), 'sp', scatter_dimension=0, ti...]
    all_gather x7 -> x4, waiting for transfers between devices: 407 us -> 58.9 us  [the longest x1 35.8 us: local_planes(): all_b = lax.all_gather(normed_b, both, axis=0, tiled=True)]
    psum x1 -> x0, waiting for transfers between devices: 146 us -> none  [local(): ffn_total, attn_total = lax.psum((ffn_partial, attn_partial), 'sp')]
    concatenate x8 -> x0, other arithmetic: 89.5 us -> none  [the longest x1 50.9 us: local(): jnp.concatenate([mat_tn(grad_gate, normed_b), mat_tn(grad_up, normed_b),...]
    dot_general x16 -> x2, matrix products: 90.1 us -> 6.62 us  [the longest x1 3.78 us: local_planes(): jnp.dot(grad_proj, w_qkv, preferred_element_type=jnp.float32)]
  transfers between devices with their start and end apart: 18 -> 7, of which waited for: 13 -> 4; matrix products, arithmetic and copies ran while one was open for 8% -> 9% of each run, Pallas kernels for 0% -> 51%
where the time goes in v1:
time: 671 us; the launch traced here: 663 us
  Pallas kernels  479 us (71%)
  waiting for transfers between devices  89.9 us (13%)
  other arithmetic  35.2 us (5%)
  matrix products  25.7 us (4%)
  local copies, waits for them, and re-layouts  17.5 us (3%)
  between operations  15 us (2%)
    pallas_call x1, Pallas kernels, exchange_heads(): pl.pallas_call(functools.partial(heads_kernel, planes), out_shape=(jax.Sh...  107 us
    pallas_call x1, Pallas kernels, middle_layer(): pl.pallas_call(middle_kernel, out_shape=(jax.ShapeDtypeStruct((rows, widt...  107 us
    pallas_call x1, Pallas kernels, feed_weights(): pl.pallas_call(feed_weights_kernel, grid=(tokens // chunk,), in_specs=[mo...  98.8 us
    pallas_call x1, Pallas kernels, return_heads(): pl.pallas_call(functools.partial(unheads_kernel, planes), out_shape=jax.S...  60.1 us
    pallas_call x1, Pallas kernels, scatter_plane(): pl.pallas_call(functools.partial(scatter_gains_kernel, planes), out_shape...  38.8 us
    all_gather x1, waiting for transfers between devices, local_planes(): all_b = lax.all_gather(normed_b, both, axis=0, tiled=True)  35.8 us
    pallas_call x1, Pallas kernels, gather_plane(): pl.pallas_call(gather_gains_kernel, out_shape=(out, jax.ShapeDtypeStruct(...  32 us
    reduce_scatter x2, waiting for transfers between devices, over_planes(): lax.psum_scatter(part.astype(jnp.bfloat16), 'sp', scatter_dimension=0, ti...  30.4 us
  transfers between devices with their start and end apart: 7, of which 4 were waited for; matrix products, arithmetic and copies ran while one was open for 9% of the time, Pallas kernels for 51%

profile of v1, /device:TPU:1, one launch (start us, length us, event | category | flops | bytes accessed | tf_op | source)
XLA Modules:
  0.0 662.8 jit_solution(15554808276663067166)
XLA Ops:
  7.3 2.9 concatenate.12
  10.7 32.0 %gather_gains.1 = (bf16[8,128,2048]{2,1,0:T(8,128)(2,1)}, f32[8,8,128]{2,1,0:T(8,128)}) custom-call(bf16[128,2048]{1,0:T(8,128)(2,1)} %x_ref.3, f32[8,128]{1,0:T(8,128)} %bitcast_convert_fusion.1.s_ref), custom_call_target="tpu_custom_call" | custom-call | tf_op jit(solution)/shard_map/gather_gains/pallas_call | solution.py:506
  43.6 3.2 fusion
  48.1 3.7 multiply_reduce_fusion.2
  51.8 3.0 copy.39
  62.4 107.3 %exchange_heads.1 = (bf16[2,1024,128]{2,1,0:T(8,128)(2,1)}, bf16[4,2,1024,128]{3,2,1,0:T(8,128)(2,1)}) custom-call(bf16[4,1024,128]{2,1,0:T(8,128)(2,1)} %fusion.14.n_ref), custom_call_target="tpu_custom_call" | custom-call | tf_op jit(solution)/shard_map/exchange_heads/pallas_call | solution.py:823
  169.8 3.5 fusion.4
  178.5 14.1 %attend.1 = (f32[2,1024,128]{2,1,0:T(8,128)}, f32[2,1024,1]{2,1,0:T(8,128)}, bf16[1024,256]{1,0:T(8,128)(2,1)}) custom-call(s32[5]{0:T(128)} %lengths_ref.3, bf16[2,1024,128]{2,1,0:T(8,128)(2,1)} %get-tuple-element.46.q_ref, bf16[4,2,8,128,128]{4,3,2,1,0:T(8,128)(2,1)} %bitcast.84, f32[2,1024,1]{2,1,0:T(8,128)} %copy.40.gate_ref), custom_call_target="tpu_custom_call" | custom-call | tf_op jit(solution)/shard_map/attend/pallas_call | solution.py:1085
  192.5 106.9 %middle_layer.1 = (bf16[128,2048]{1,0:T(8,128)(2,1)}, bf16[8,128,2048]{2,1,0:T(8,128)(2,1)}, f32[128,2048]{1,0:T(8,128)}, f32[128,2048]{1,0:T(8,128)}, f32[1,204...) custom-call(bf16[8,128,256]{2,1,0:T(8,128)(2,1)} %bitcast.91, bf16[256,2048]{1,0:T(8,128)(2,1)} %wout_ref.1, ...), custom_call_target="tpu_custom_call" | custom-call | tf_op jit(solution)/shard_map/middle_layer/pallas_call | solution.py:1468
  299.5 21.4 %attend_back.1 = (bf16[2,1024,128]{2,1,0:T(8,128)(2,1)}, bf16[4,2,8,128,128]{4,3,2,1,0:T(8,128)(2,1)}, bf16[2,1024,1]{2,1,0:T(8,128)(2,1)}) custom-call(s32[5]{0:T(128)} %lengths_ref.3, bf16[2,1024,128]{2,1,0:T(8,128)(2,1)} %get-tuple-element.46.q_ref, bf16[4,2,8,128,128]{4,3,2,1,0:T(8,128)(2,1)} %bitcast.85, f32[2,1024,1]{2,1,0:T(8,128)} %copy.40.gate_ref, ...), custom_call_target="tpu_custom_call" | custom-call | tf_op jit(solution)/shard_map/attend_back/pallas_call | solution.py:1174
  320.9 60.1 %return_heads.1 = bf16[4,1024,128]{2,1,0:T(8,128)(2,1)} custom-call(bf16[2,1024,128]{2,1,0:T(8,128)(2,1)} %get-tuple-element.54.dq_ref, bf16[4,2,1024,128]{3,2,1,0:T(8,128)(2,1)} %bitcast.87), custom_call_target="tpu_custom_call" | custom-call | tf_op jit(solution)/shard_map/return_heads/pallas_call | solution.py:981
  386.2 2.5 fusion.13
  391.5 3.8 fusion.17
  395.3 3.8 fusion.6
  399.1 35.8 %all-gather.7.cloned.1.call-done.x_ref = bf16[4096,2048]{1,0:T(8,128)(2,1)} async-done(((bf16[128,2048]{1,0:T(8,128)(2,1)}), bf16[4096,2048]{1,0:T(8,128)(2,1)}) %all-gather.7.cloned.1.call-update) | async-done | bytes 16777232 | tf_op jit(solution)/shard_map/all_gather | solution.py:1626
  434.9 4.5 convolution_convert_fusion.1
  439.5 5.8 convolution_convert_fusion
  445.4 28.7 %reduce-scatter.8.cloned.1.call-done = bf16[64,2048]{1,0:T(8,128)(2,1)} async-done(((bf16[256,2048]{1,0:T(8,128)(2,1)}), bf16[64,2048]{1,0:T(8,128)(2,1)}) %reduce-scatter.8.cloned.1.call-update) | async-done | bytes 262160 | tf_op jit(solution)/shard_map/reduce_scatter | solution.py:1669
  476.9 2.8 fusion.18
  480.4 38.8 %scatter_gains.1 = (f32[128,2048]{1,0:T(8,128)}, f32[8,128]{1,0:T(8,128)}, f32[32,128]{1,0:T(8,128)}) custom-call(bf16[8,128,2048]{2,1,0:T(8,128)(2,1)} %bitcast.80, f32[8,8,128]{2,1,0:T(8,128)} %bitcast.96, f32[32,128]{1,0:T(8,128)} %reshape.310.g_ref), custom_call_target="tpu_custom_call" | custom-call | tf_op jit(solution)/shard_map/scatter_gains/pallas_call | solution.py:629
  520.9 98.8 %feed_weights.1 = (f32[768,2048]{1,0:T(8,128)}, f32[768,2048]{1,0:T(8,128)}, f32[768,2048]{1,0:T(8,128)}) custom-call(bf16[4096,2048]{1,0:T(8,128)(2,1)} %all-gather.7.cloned.1.call-done.x_ref, bf16[4096,2048]{1,0:T(8,128)(2,1)} %all-gather.5.cloned.1.call-done.g_ref, bf16[768,2048]{1,0:T(8,128)(2,1)} %wg_ref.1, bf16[768,2048]{1,0:T(8,128)(2,1)} %wu_ref.1, ...), custom_call_target="tpu_custom_call" | custom-call | flops 77309411328 | bytes 61865984 | tf_op jit(solution)/shard_map/feed_weights/pallas_call | solution.py:1540
  623.3 2.9 convert_element_type.86
  628.3 23.1 %all-gather.9.cloned.1.call-done = bf16[512,2048]{1,0:T(8,128)(2,1)} async-done(((bf16[128,2048]{1,0:T(8,128)(2,1)}), bf16[512,2048]{1,0:T(8,128)(2,1)}) %all-gather.9.cloned.1.call-update) | async-done | bytes 2097168 | tf_op jit(solution)/shard_map/all_gather | solution.py:1672
  651.4 4.1 convert_element_type.84
  (107 shorter events, 34.4 us)
Async XLA Ops:
  7.2 40.9 %copy-start = (bf16[512,2048]{1,0:T(8,128)(2,1)S(1)}, bf16[512,2048]{1,0:T(8,128)(2,1)}, u32[]{:S(2)}) copy-start(bf16[512,2048]{1,0:T(8,128)(2,1)} %param.17) | copy-start | bytes 6291460
  7.2 185.3 %all-gather.5.cloned.1.call-start = ((), (), s32[]{:S(2)}) async-start(), calls=%async_computation.3 | async-start | bytes 17301504 | tf_op jit(solution)/shard_map/all_gather | solution.py:1592
  42.7 392.2 %all-gather.7.cloned.1.call-start = ((), (), s32[]{:S(2)}) async-start(), calls=%async_computation.4 | async-start | bytes 17301504 | tf_op jit(solution)/shard_map/all_gather | solution.py:1626
  43.6 3.5 copy-start.2
  48.1 3.7 copy-start.7
  51.8 3.1 copy-start.19
  169.8 5.5 copy-start.15
  173.3 2.0 copy-start.6
  299.4 174.7 %reduce-scatter.8.cloned.1.call-start = ((), (), s32[]{:S(2)}) async-start(), calls=%async_computation.8 | async-start | bytes 1310720 | tf_op jit(solution)/shard_map/reduce_scatter | solution.py:1669
  384.2 2.0 copy-start.8
  391.5 3.8 copy-start.3
  395.3 39.6 %copy-start.14 = (bf16[1024,256]{1,0:T(8,128)(2,1)S(1)}, bf16[1024,256]{1,0:T(8,128)(2,1)}, u32[]{:S(2)}) copy-start(bf16[1024,256]{1,0:T(8,128)(2,1)} %get-tuple-element.48) | copy-start | bytes 1572868
  434.9 4.6 copy-start.13
  439.5 81.4 %reduce-scatter.6.cloned.1.call-start = ((), (), s32[]{:S(2)}) async-start(), calls=%async_computation.6 | async-start | bytes 2621440 | tf_op jit(solution)/shard_map/reduce_scatter | solution.py:1669
  445.4 177.9 %all-gather.11.cloned.1.call-start = ((), (), s32[]{:S(2)}) async-start(), calls=%async_computation.9 | async-start | bytes 1310720 | tf_op jit(solution)/shard_map/all_gather | solution.py:1672
  474.2 152.0 %reduce-scatter.4.cloned.1.call-start = ((), (), s32[]{:S(2)}) async-start(), calls=%async_computation.5 | async-start | bytes 4718592 | tf_op jit(solution)/shard_map/reduce_scatter | solution.py:1654
  474.8 176.7 %all-gather.9.cloned.1.call-start = ((), (), s32[]{:S(2)}) async-start(), calls=%async_computation.7 | async-start | bytes 2621440 | tf_op jit(solution)/shard_map/all_gather | solution.py:1672
  520.9 98.9 %copy-start.16 = (f32[32,128]{1,0:T(8,128)S(1)}, f32[32,128]{1,0:T(8,128)}, u32[]{:S(2)}) copy-start(f32[32,128]{1,0:T(8,128)} %get-tuple-element.67) | copy-start | bytes 49156
  520.9 99.5 %copy-start.9 = (bf16[128,2048]{1,0:T(8,128)(2,1)S(1)}, bf16[128,2048]{1,0:T(8,128)(2,1)}, u32[]{:S(2)}) copy-start(bf16[128,2048]{1,0:T(8,128)(2,1)} %x_ref.3) | copy-start | bytes 1572868
  520.9 99.5 %copy-start.10 = (f32[128,2048]{1,0:T(8,128)S(1)}, f32[128,2048]{1,0:T(8,128)}, u32[]{:S(2)}) copy-start(f32[128,2048]{1,0:T(8,128)} %get-tuple-element.64) | copy-start | bytes 3145732
  520.9 99.8 %copy-start.18 = (f32[8,128]{1,0:T(8,128)S(1)}, f32[8,128]{1,0:T(8,128)}, u32[]{:S(2)}) copy-start(f32[8,128]{1,0:T(8,128)} %get-tuple-element.65) | copy-start | bytes 12292
  619.8 2.1 copy-start.11
  623.3 2.9 copy-start.12
  626.2 29.4 %copy-start.1 = (bf16[512,2048]{1,0:T(8,128)(2,1)S(1)}, bf16[512,2048]{1,0:T(8,128)(2,1)}, u32[]{:S(2)}) copy-start(bf16[512,2048]{1,0:T(8,128)(2,1)} %param.17) | copy-start | bytes 6291460
  (3 other events, 4.3 us)
Sparse Core Ops, SparseCore 0:
  42.9 135.5 all-gather.4
  299.5 135.3 all-gather.6
  439.6 34.5 reduce-scatter.7
  477.0 43.8 reduce-scatter.5
  522.3 27.2 all-gather.10
  552.8 50.9 reduce-scatter.3
  605.4 45.9 all-gather.8

commit v2 on v1

--- a/solution.py
+++ b/solution.py
@@ -659,6 +659,60 @@
     )(p)
 
 
+GATHER_COPIES = 13
+
+
+def gather_copy(buf, i, send_sem, recv_sem, own=None):
+    rank, plane = lax.axis_index("fsdp"), lax.axis_index("sp")
+    rows = buf.shape[1]
+    top, low = pl.ds(0, rows // 2), pl.ds(rows // 2, rows // 2)
+    block, part, to = (
+        (0, top, 2),
+        (0, low, 2),
+        (0, low, 4),
+        (0, top, 4),
+        (2, top, 4),
+        (4, low, 2),
+        (0, pl.ds(0, rows), 1),
+        (2, top, 1),
+        (2, low, 1),
+        (4, low, 1),
+        (4, top, 1),
+        (6, top, 1),
+        (6, low, 1),
+    )[i]
+    piece = buf.at[rank ^ block, part]
+    source = piece if own is None or block else own.at[part]
+    return peer_copy(source, piece, send_sem.at[i], recv_sem.at[i], rank ^ to, plane)
+
+
+def gather_start(buf, send_sem, recv_sem, own=None):
+    for i in (6, 0, 2, 1, 3):
+        gather_copy(buf, i, send_sem, recv_sem, own).start()
+
+
+def gather_pass(buf, send_sem, recv_sem, pairs):
+    for arrived, onward in pairs:
+        gather_copy(buf, arrived, send_sem, recv_sem).wait_recv()
+        for i in onward:
+            gather_copy(buf, i, send_sem, recv_sem).start()
+
+
+def gather_wait(buf, send_sem, recv_sem, copies):
+    for i in copies:
+        gather_copy(buf, i, send_sem, recv_sem).wait_recv()
+
+
+def gather_sent(buf, send_sem, recv_sem):
+    for i in range(GATHER_COPIES):
+        gather_copy(buf, i, send_sem, recv_sem).wait_send()
+
+
+NEIGHBOURS_FIRST = ((0, (4, 7)), (2, (5, 9)), (1, (8,)), (3, (10,)))
+DIAGONAL = ((4, (11,)), (5, (12,)))
+FROM_SIBLING = (6, 7, 8, 9, 10, 11, 12)
+
+
 def greet_line(ranks, planes):
     rank, plane = lax.axis_index("fsdp"), lax.axis_index("sp")
     barrier = pltpu.get_barrier_semaphore()
@@ -680,9 +734,11 @@
     pl.semaphore_wait(barrier, ranks - 1 + lower + upper)
 
 
-def heads_kernel(planes, n_ref, q_ref, kv_ref, own_sem, q_send, q_recv, kv_send, kv_recv, line_send, line_recv):
+def heads_kernel(planes, n_ref, g_ref, q_ref, kv_ref, dy_ref, g_sem, ag_send, ag_recv, own_sem, q_send, q_recv, kv_send, kv_recv, line_send, line_recv):
     rank, plane = lax.axis_index("fsdp"), lax.axis_index("sp")
     greet_line(8, planes)
+    own_block = pltpu.make_async_copy(g_ref, dy_ref.at[rank], g_sem)
+    own_block.start()
 
     def q_copy(m, to):
         return peer_copy(n_ref.at[pl.ds(2 * m, 2)], q_ref, q_send.at[m], q_recv, to, plane)
@@ -739,9 +795,17 @@
             kv_copy(0, which, 0).wait_recv()
 
         line_step(planes, kv_ref, which, 0, line_send, line_recv)
+    gather_start(dy_ref, ag_send, ag_recv, g_ref)
     for j in range(1, planes):
         for which in range(2):
             line_step(planes, kv_ref, which, j, line_send, line_recv)
+        if j == 1:
+            gather_pass(dy_ref, ag_send, ag_recv, NEIGHBOURS_FIRST)
+        if j == 2:
+            gather_pass(dy_ref, ag_send, ag_recv, DIAGONAL)
+    gather_wait(dy_ref, ag_send, ag_recv, FROM_SIBLING)
+    gather_sent(dy_ref, ag_send, ag_recv)
+    own_block.wait()
 
     @pl.when(rank == 0)
     def _():
@@ -817,18 +881,24 @@
                 line_copy(kv_ref, which, j, side, line_send, line_recv).start()
 
 
-def exchange_heads(natural, collective_id):
+def exchange_heads(natural, grad, collective_id):
     _, tokens, width = natural.shape
     planes = lax.axis_size("sp")
+    ranks = lax.axis_size("fsdp")
+    hbm = pl.BlockSpec(memory_space=pl.ANY)
     return pl.pallas_call(
         functools.partial(heads_kernel, planes),
         out_shape=(
             jax.ShapeDtypeStruct((2, tokens, width), natural.dtype),
             jax.ShapeDtypeStruct((planes, 2, tokens, width), natural.dtype),
+            jax.ShapeDtypeStruct((ranks,) + grad.shape, grad.dtype),
         ),
-        in_specs=[pl.BlockSpec(memory_space=pl.ANY)],
-        out_specs=(pl.BlockSpec(memory_space=pl.ANY), pl.BlockSpec(memory_space=pl.ANY)),
+        in_specs=[hbm, hbm],
+        out_specs=(hbm, hbm, hbm),
         scratch_shapes=[
+            pltpu.SemaphoreType.DMA,
+            pltpu.SemaphoreType.DMA((GATHER_COPIES,)),
+            pltpu.SemaphoreType.DMA((GATHER_COPIES,)),
             pltpu.SemaphoreType.DMA,
             pltpu.SemaphoreType.DMA((2,)),
             pltpu.SemaphoreType.DMA,
@@ -841,12 +911,21 @@
             collective_id=collective_id, has_side_effects=True, vmem_limit_bytes=VMEM_LIMIT
         ),
         name="exchange_heads",
-    )(natural)
-
-
-def unheads_kernel(planes, dq_ref, dkv_ref, n_ref, line_out, line_in, done, own_sem, q_send, q_recv, kv_send, kv_recv, line_send, line_recv):
+    )(natural, grad)
+
+
+def unheads_kernel(planes, dq_ref, dkv_ref, dz_ref, n_ref, dy_ref, g_sem, ag_send, ag_recv, line_out, line_in, done, own_sem, q_send, q_recv, kv_send, kv_recv, line_send, line_recv):
     rank, plane = lax.axis_index("fsdp"), lax.axis_index("sp")
     greet_line(8, planes)
+    own_blocks = [
+        pltpu.make_async_copy(dz_ref.at[j], dy_ref.at[j, rank], g_sem.at[j])
+        for j in range(planes - 1)
+    ]
+    for copy in own_blocks:
+        copy.start()
+    gathers = [
+        (dy_ref.at[j], ag_send.at[j], ag_recv.at[j]) for j in range(planes - 1)
+    ]
 
     def q_copy(m, to):
         return peer_copy(dq_ref, n_ref.at[pl.ds(2 * m, 2)], q_send, q_recv.at[m], to, plane)
@@ -906,6 +985,12 @@
                 @pl.when(sends(j, side))
                 def _():
                     step_copy(j, which, side).start()
+
+        gather_start(*gathers[j], own=dz_ref.at[j])
+        if j:
+            gather_pass(*gathers[j - 1], NEIGHBOURS_FIRST)
+        if j > 1:
+            gather_pass(*gathers[j - 2], DIAGONAL)
 
     for which in range(2):
         total = dkv_ref[plane, which].astype(jnp.float32)
@@ -932,6 +1017,15 @@
             def _():
                 kv_local(m, which).start()
 
+    gather_pass(*gathers[planes - 2], NEIGHBOURS_FIRST)
+    for j in range(max(planes - 3, 0), planes - 1):
+        gather_pass(*gathers[j], DIAGONAL)
+    for gather in gathers:
+        gather_wait(*gather, FROM_SIBLING)
+        gather_sent(*gather)
+    for copy in own_blocks:
+        copy.wait()
+
     @pl.when(rank < 4)
     def _():
         for m in range(2):
@@ -974,16 +1068,24 @@
                     step_copy(j, which, side).wait_send()
 
 
-def return_heads(grad_query, grad_kv, collective_id):
+def return_heads(grad_query, grad_kv, grad_line, collective_id):
     _, tokens, width = grad_query.shape
     planes = lax.axis_size("sp")
+    ranks = lax.axis_size("fsdp")
     vmem = pl.BlockSpec(memory_space=pltpu.VMEM)
+    hbm = pl.BlockSpec(memory_space=pl.ANY)
     return pl.pallas_call(
         functools.partial(unheads_kernel, planes),
-        out_shape=jax.ShapeDtypeStruct((4, tokens, width), grad_query.dtype),
-        in_specs=[vmem, vmem],
-        out_specs=vmem,
+        out_shape=(
+            jax.ShapeDtypeStruct((4, tokens, width), grad_query.dtype),
+            jax.ShapeDtypeStruct((planes - 1, ranks) + grad_line.shape[1:], grad_line.dtype),
+        ),
+        in_specs=[vmem, vmem, hbm],
+        out_specs=(vmem, hbm),
         scratch_shapes=[
+            pltpu.SemaphoreType.DMA((planes - 1,)),
+            pltpu.SemaphoreType.DMA((planes - 1, GATHER_COPIES)),
+            pltpu.SemaphoreType.DMA((planes - 1, GATHER_COPIES)),
             pltpu.VMEM((2, planes - 1, 2, tokens, width), grad_query.dtype),
             pltpu.VMEM((2, planes - 1, 2, tokens, width), grad_query.dtype),
             pltpu.VMEM((2, tokens, width), grad_query.dtype),
@@ -999,7 +1101,7 @@
             collective_id=collective_id, has_side_effects=True, vmem_limit_bytes=VMEM_LIMIT
         ),
         name="return_heads",
-    )(grad_query, grad_kv)
+    )(grad_query, grad_kv, grad_line)
 
 
 def stack_heads(ref):
@@ -1198,54 +1300,8 @@
     return dquery, dkv.reshape(planes, 2, tokens, width), dgate
 
 
-GATHER_COPIES = 13
-
-
-def gather_copy(buf, i, send_sem, recv_sem):
-    rank, plane = lax.axis_index("fsdp"), lax.axis_index("sp")
-    rows = buf.shape[1]
-    top, low = pl.ds(0, rows // 2), pl.ds(rows // 2, rows // 2)
-    block, part, to = (
-        (0, top, 2),
-        (0, low, 2),
-        (0, low, 4),
-        (0, top, 4),
-        (2, top, 4),
-        (4, low, 2),
-        (0, pl.ds(0, rows), 1),
-        (2, top, 1),
-        (2, low, 1),
-        (4, low, 1),
-        (4, top, 1),
-        (6, top, 1),
-        (6, low, 1),
-    )[i]
-    piece = buf.at[rank ^ block, part]
-    return peer_copy(piece, piece, send_sem.at[i], recv_sem.at[i], rank ^ to, plane)
-
-
-def gather_start(buf, send_sem, recv_sem):
-    for i in (6, 0, 2, 1, 3):
-        gather_copy(buf, i, send_sem, recv_sem).start()
-
-
-def gather_pass(buf, send_sem, recv_sem, pairs):
-    for arrived, onward in pairs:
-        gather_copy(buf, arrived, send_sem, recv_sem).wait_recv()
-        for i in onward:
-            gather_copy(buf, i, send_sem, recv_sem).start()
-
-
-def gather_wait(buf, send_sem, recv_sem, copies):
-    for i in copies:
-        gather_copy(buf, i, send_sem, recv_sem).wait_recv()
-
-
-NEIGHBOURS_FIRST = ((0, (4, 7)), (2, (5, 9)), (1, (8,)), (3, (10,)))
-DIAGONAL = ((4, (11,)), (5, (12,)))
-
-
 def middle_kernel(
+    planes,
     gated_ref,
     wout_ref,
     x_ref,
@@ -1254,7 +1310,9 @@
     wg_hbm,
     wu_hbm,
     wd_hbm,
-    xb_ref,
+    xg,
+    xz_hbm,
+    dz_hbm,
     down_hbm,
     mid_ref,
     dmid_ref,
@@ -1266,7 +1324,6 @@
     wd,
     dy,
     dhid,
-    xg,
     near_out,
     near_in,
     far_out,
@@ -1282,6 +1339,8 @@
     far_recv,
     ag_send,
     ag_recv,
+    line_send,
+    line_recv,
 ):
     rank, plane = lax.axis_index("fsdp"), lax.axis_index("sp")
     ranks, rows, width = xg.shape
@@ -1290,10 +1349,22 @@
         pltpu.make_async_copy(wg_hbm, wg, load_sem.at[1]),
         pltpu.make_async_copy(wu_hbm, wu, load_sem.at[2]),
     ]
-    dy_loads = [
-        pltpu.make_async_copy(dy_hbm.at[r, plane], dy.at[r], dy_sem.at[r]) for r in range(ranks)
-    ]
-    greet([(rank ^ k, plane) for k in (1, 2, 4, 6)])
+    dy_load = pltpu.make_async_copy(dy_hbm, dy, dy_sem)
+    others = [lax.rem(plane + k, planes) for k in range(1, planes)]
+    greet([(rank ^ k, plane) for k in (1, 2, 4, 6)] + [(rank, other) for other in others])
+
+    def along(source, target, which):
+        return [
+            peer_copy(
+                source,
+                target.at[j - 1],
+                line_send.at[which, j - 1],
+                line_recv.at[which, j - 1],
+                rank,
+                lax.rem(plane + planes - j, planes),
+            )
+            for j in range(1, planes)
+        ]
 
     def near(phase, i):
         return peer_copy(
@@ -1322,7 +1393,11 @@
         )
         near_out[0, i] = part.astype(jnp.bfloat16)
         near(0, i).start()
-    for copy in dy_loads + loads:
+    dy_load.start()
+    for copy in loads:
+        copy.start()
+    dy_line = along(dy_hbm.at[rank], dz_hbm, 0)
+    for copy in dy_line:
         copy.start()
     for i, k in enumerate(order):
         part = jnp.dot(gated_ref[rank ^ k], wout_ref[...], preferred_element_type=jnp.float32)
@@ -1334,8 +1409,7 @@
         else:
             keep[...] = part
 
-    for copy in dy_loads:
-        copy.wait()
+    dy_load.wait()
     loads[0].wait()
 
     @pl.loop(0, ranks // 2)
@@ -1352,10 +1426,12 @@
     inverse = inv_rms(middle)
     mid_ref[...] = middle
     normed = (middle * inverse * scale_ref[...]).astype(jnp.bfloat16)
-    xb_ref[...] = normed
     xg[rank] = normed
     sems = (ag_send.at[0], ag_recv.at[0])
     gather_start(xg, *sems)
+    xb_line = along(xg.at[rank], xz_hbm, 1)
+    for copy in xb_line:
+        copy.start()
 
     slots = {2: 0, 4: 1, 6: 2, 0: 3}
 
@@ -1445,9 +1521,10 @@
     gather_wait(pm_ref, *sems2, (11, 12))
     gated_grad(6)
 
-    for i in range(GATHER_COPIES):
-        gather_copy(xg, i, *sems).wait_send()
-        gather_copy(pm_ref, i, *sems2).wait_send()
+    gather_sent(xg, *sems)
+    gather_sent(pm_ref, *sems2)
+    for copy in dy_line + xb_line:
+        copy.wait()
     for phase in range(2):
         for i in range(4):
             near(phase, i).wait_send()
@@ -1457,8 +1534,9 @@
     down_copy(0, 1).wait()
 
 
-def middle_layer(gated, w_out, x, scale, grad_all, w_gate, w_up, w_down, collective_id):
+def middle_layer(gated, w_out, x, scale, grad_plane, w_gate, w_up, w_down, collective_id):
     ranks, rows, _ = gated.shape
+    planes = lax.axis_size("sp")
     width = x.shape[1]
     hidden = w_gate.shape[0]
     features = w_out.shape[0]
@@ -1466,9 +1544,11 @@
     hbm = pl.BlockSpec(memory_space=pl.ANY)
     half, full = jnp.bfloat16, jnp.float32
     return pl.pallas_call(
-        middle_kernel,
+        functools.partial(middle_kernel, planes),
         out_shape=(
-            jax.ShapeDtypeStruct((rows, width), half),
+            jax.ShapeDtypeStruct((ranks, rows, width), half),
+            jax.ShapeDtypeStruct((planes - 1, rows, width), half),
+            jax.ShapeDtypeStruct((planes - 1, rows, width), half),
             jax.ShapeDtypeStruct((ranks, rows, width), half),
             jax.ShapeDtypeStruct((rows, width), full),
             jax.ShapeDtypeStruct((rows, width), full),
@@ -1477,14 +1557,13 @@
             jax.ShapeDtypeStruct((ranks, rows, features), full),
         ),
         in_specs=[vmem, vmem, vmem, vmem, hbm, hbm, hbm, hbm],
-        out_specs=(vmem, hbm, vmem, vmem, vmem, vmem, vmem),
+        out_specs=(vmem, hbm, hbm, hbm, vmem, vmem, vmem, vmem, vmem),
         scratch_shapes=[
             pltpu.VMEM((hidden, width), half),
             pltpu.VMEM((hidden, width), half),
             pltpu.VMEM((hidden, width), half),
             pltpu.VMEM((ranks, rows, width), half),
             pltpu.VMEM((ranks // 2, 2 * rows, hidden), full),
-            pltpu.VMEM((ranks, rows, width), half),
             pltpu.VMEM((2, 4, rows, width), half),
             pltpu.VMEM((2, 4, rows, width), half),
             pltpu.VMEM((2, 3, rows, width), half),
@@ -1492,7 +1571,7 @@
             pltpu.VMEM((rows, width), full),
             pltpu.VMEM((2, 2, rows, width), half),
             pltpu.SemaphoreType.DMA((3,)),
-            pltpu.SemaphoreType.DMA((ranks,)),
+            pltpu.SemaphoreType.DMA,
             pltpu.SemaphoreType.DMA((2,)),
             pltpu.SemaphoreType.DMA((2, 4)),
             pltpu.SemaphoreType.DMA((2, 4)),
@@ -1500,57 +1579,137 @@
             pltpu.SemaphoreType.DMA((2, 3)),
             pltpu.SemaphoreType.DMA((2, GATHER_COPIES)),
             pltpu.SemaphoreType.DMA((2, GATHER_COPIES)),
+            pltpu.SemaphoreType.DMA((2, planes - 1)),
+            pltpu.SemaphoreType.DMA((2, planes - 1)),
         ],
         compiler_params=pltpu.CompilerParams(
             collective_id=collective_id, has_side_effects=True, vmem_limit_bytes=VMEM_LIMIT
         ),
         name="middle_layer",
-    )(gated, w_out, x, scale, grad_all, w_gate, w_up, w_down)
-
-
-def feed_weights_kernel(x_ref, g_ref, wg_ref, wu_ref, wd_ref, og_ref, ou_ref, od_ref):
-    normed, grad = x_ref[...], g_ref[...]
-    gate_pre = mat_nt(normed, wg_ref[...])
-    up_pre = mat_nt(normed, wu_ref[...])
-    grad_hidden = mat_nt(grad, wd_ref[...])
-    sigma = jax.nn.sigmoid(gate_pre)
-    swish = gate_pre * sigma
-    hidden = (swish * up_pre).astype(jnp.bfloat16)
-    grad_gate = (grad_hidden * up_pre * sigma * (1.0 + gate_pre * (1.0 - sigma))).astype(
-        jnp.bfloat16
-    )
-    grad_up = (grad_hidden * swish).astype(jnp.bfloat16)
-
-    @pl.when(pl.program_id(0) == 0)
-    def _():
-        for ref in (og_ref, ou_ref, od_ref):
-            ref[...] = jnp.zeros_like(ref)
-
-    og_ref[...] += mat_tn(grad_gate, normed)
-    ou_ref[...] += mat_tn(grad_up, normed)
-    od_ref[...] += mat_tn(hidden, grad)
-
-
-def feed_weights(normed, grad, w_gate, w_up, w_down):
-    tokens, width = normed.shape
-    chunk = 512
-    moving = pl.BlockSpec((chunk, width), lambda i: (i, 0))
-    still = pl.BlockSpec(w_gate.shape, lambda i: (0, 0), pipeline_mode=pl.Buffered(1))
-    flops = 12 * tokens * w_gate.size
+    )(gated, w_out, x, scale, grad_plane, w_gate, w_up, w_down)
+
+
+def feed_weights_kernel(
+    planes, xp_hbm, dp_hbm, xz_hbm, dy_hbm, wg_ref, wu_ref, wd_ref, og_ref, ou_ref, od_ref, xo_hbm, xbuf, dbuf, x_sem, d_sem, own_sem, ag_send, ag_recv
+):
+    rank, plane = lax.axis_index("fsdp"), lax.axis_index("sp")
+    ranks, rows, width = xp_hbm.shape
+    part = ranks // 2
+    greet([(rank ^ k, plane) for k in (1, 2, 4)])
+    own_blocks = [
+        pltpu.make_async_copy(xz_hbm.at[j], xo_hbm.at[j, rank], own_sem.at[j])
+        for j in range(planes - 1)
+    ]
+    gathers = [(xo_hbm.at[j], ag_send.at[j], ag_recv.at[j]) for j in range(planes - 1)]
+
+    def load(step, start):
+        slot = lax.rem(step, 2)
+        block = pl.ds(part * lax.rem(step, 2), part)
+        group = step // 2
+
+        def go(x_from, d_from):
+            for copy in (
+                pltpu.make_async_copy(x_from, xbuf.at[slot], x_sem.at[slot]),
+                pltpu.make_async_copy(d_from, dbuf.at[slot], d_sem.at[slot]),
+            ):
+                if start:
+                    copy.start()
+                else:
+                    copy.wait()
+
+        @pl.when(group == 0)
+        def _():
+            go(xp_hbm.at[block], dp_hbm.at[block])
+
+        @pl.when(group > 0)
+        def _():
+            go(xo_hbm.at[group - 1, block], dy_hbm.at[group - 1, block])
+
+    load(0, True)
+    for copy in own_blocks:
+        copy.start()
+    gather_start(*gathers[0], own=xz_hbm.at[0])
+
+    @pl.loop(0, 2 * planes)
+    def _(step):
+        for j in range(planes - 1):
+            @pl.when(step == 2 * j + 1)
+            def _():
+                gather_pass(*gathers[j], NEIGHBOURS_FIRST)
+                if j < planes - 2:
+                    gather_start(*gathers[j + 1], own=xz_hbm.at[j + 1])
+
+            @pl.when(step == 2 * j + 2)
+            def _():
+                gather_pass(*gathers[j], DIAGONAL)
+                gather_wait(*gathers[j], FROM_SIBLING)
+                own_blocks[j].wait()
+                load(step, True)
+
+        load(step, False)
+
+        @pl.when(lax.rem(step, 2) == 0)
+        def _():
+            load(step + 1, True)
+
+        slot = lax.rem(step, 2)
+        normed = xbuf[slot].reshape(part * rows, width)
+        grad = dbuf[slot].reshape(part * rows, width)
+        gate_pre = mat_nt(normed, wg_ref[...])
+        up_pre = mat_nt(normed, wu_ref[...])
+        grad_hidden = mat_nt(grad, wd_ref[...])
+        sigma = jax.nn.sigmoid(gate_pre)
+        swish = gate_pre * sigma
+        hidden = (swish * up_pre).astype(jnp.bfloat16)
+        grad_gate = (grad_hidden * up_pre * sigma * (1.0 + gate_pre * (1.0 - sigma))).astype(
+            jnp.bfloat16
+        )
+        grad_up = (grad_hidden * swish).astype(jnp.bfloat16)
+
+        @pl.when(step == 0)
+        def _():
+            for ref in (og_ref, ou_ref, od_ref):
+                ref[...] = jnp.zeros_like(ref)
+
+        og_ref[...] += mat_tn(grad_gate, normed)
+        ou_ref[...] += mat_tn(grad_up, normed)
+        od_ref[...] += mat_tn(hidden, grad)
+
+    for gather in gathers:
+        gather_sent(*gather)
+
+
+def feed_weights(plane_x, plane_grad, line_x, other_grad, w_gate, w_up, w_down, collective_id):
+    ranks, rows, width = plane_x.shape
+    planes = lax.axis_size("sp")
+    vmem = pl.BlockSpec(memory_space=pltpu.VMEM)
+    hbm = pl.BlockSpec(memory_space=pl.ANY)
+    tokens = planes * ranks * rows
     return pl.pallas_call(
-        feed_weights_kernel,
-        grid=(tokens // chunk,),
-        in_specs=[moving, moving, still, still, still],
-        out_specs=(still, still, still),
-        out_shape=[jax.ShapeDtypeStruct(w_gate.shape, jnp.float32)] * 3,
+        functools.partial(feed_weights_kernel, planes),
+        in_specs=[hbm, hbm, hbm, hbm, vmem, vmem, vmem],
+        out_specs=(vmem, vmem, vmem, hbm),
+        out_shape=[jax.ShapeDtypeStruct(w_gate.shape, jnp.float32)] * 3
+        + [jax.ShapeDtypeStruct((planes - 1, ranks, rows, width), plane_x.dtype)],
+        scratch_shapes=[
+            pltpu.VMEM((2, ranks // 2, rows, width), plane_x.dtype),
+            pltpu.VMEM((2, ranks // 2, rows, width), plane_x.dtype),
+            pltpu.SemaphoreType.DMA((2,)),
+            pltpu.SemaphoreType.DMA((2,)),
+            pltpu.SemaphoreType.DMA((planes - 1,)),
+            pltpu.SemaphoreType.DMA((planes - 1, GATHER_COPIES)),
+            pltpu.SemaphoreType.DMA((planes - 1, GATHER_COPIES)),
+        ],
         cost_estimate=pl.CostEstimate(
-            flops=flops,
-            bytes_accessed=4 * normed.size + 18 * w_gate.size,
+            flops=12 * tokens * w_gate.size,
+            bytes_accessed=4 * tokens * width + 18 * w_gate.size,
             transcendentals=tokens * w_gate.shape[0],
         ),
-        compiler_params=pltpu.CompilerParams(vmem_limit_bytes=VMEM_LIMIT),
+        compiler_params=pltpu.CompilerParams(
+            collective_id=collective_id, has_side_effects=True, vmem_limit_bytes=VMEM_LIMIT
+        ),
         name="feed_weights",
-    )(normed, grad, w_gate, w_up, w_down)
+    )(plane_x, plane_grad, line_x, other_grad, w_gate, w_up, w_down)[:3]
 
 
 def local_planes(
@@ -1572,7 +1731,6 @@
     rank, plane = lax.axis_index("fsdp"), lax.axis_index("sp")
     rows, model_width = hidden_in.shape
     tokens = ranks * rows
-    both = ("fsdp", "sp")
     own_heads = w_qkv.shape[0] // HEAD_DIM
     local_heads = HEADS // ranks
 
@@ -1588,9 +1746,6 @@
     query_scale = gains[:, 2 * wide : 2 * wide + thin].reshape(-1)
     key_scale = gains[:, 2 * wide + thin : used].reshape(-1)
 
-    grad_later, gathered = lax.optimization_barrier((grad_out, gathered))
-    grad_all = lax.all_gather(grad_later, both, axis=0, tiled=True)
-
     token_block = jnp.arange(ranks, dtype=jnp.int32) * (planes * rows) + plane * rows
     plane_tokens = (token_block[:, None] + jnp.arange(rows, dtype=jnp.int32)[None]).reshape(-1)
     cosine, sine = rope_tables(plane_tokens - item_starts(plane_tokens, lengths))
@@ -1606,16 +1761,16 @@
     head_scale = jnp.where(is_query, query_scale, key_scale)
     turned = rotate(raw * raw_inv * head_scale, cosine, sine)
     natural = jnp.where(is_value, raw, turned).astype(jnp.bfloat16)
-    query, kv = exchange_heads(jnp.transpose(natural, (1, 0, 2)), 1)
+    query, kv, plane_grad = exchange_heads(jnp.transpose(natural, (1, 0, 2)), grad_out, 1)
 
     attended, total, gated = attend(lengths, query, kv, gate_logit, rows)
     own_inputs = hidden_in.astype(jnp.float32)
-    normed_b, down_part, middle, grad_middle, grad_ffn_gain_local, plane_mid, grad_gated = middle_layer(
+    plane_b, line_b, line_grad, down_part, middle, grad_middle, grad_ffn_gain_local, plane_mid, grad_gated = middle_layer(
         gated.reshape(ranks, rows, -1),
         w_out,
         hidden_in,
         ffn_scale.reshape(1, -1),
-        grad_all.reshape(ranks, planes, rows, model_width),
+        plane_grad,
         w_gate,
         w_up,
         w_down,
@@ -1623,11 +1778,10 @@
     )
     plane_mid = plane_mid.reshape(tokens, model_width)
     grad_gated = grad_gated.reshape(tokens, -1)
-    all_b = lax.all_gather(normed_b, both, axis=0, tiled=True)
     grad_query, grad_kv, gate_grad = attend_back(
         lengths, query, kv, gate_logit, attended, total, grad_gated, rows
     )
-    back = return_heads(grad_query, grad_kv, 6)
+    back, other_grad = return_heads(grad_query, grad_kv, line_grad, 6)
     back = jnp.transpose(back, (1, 0, 2))
     turned_back = rotate_back(back.astype(jnp.float32), cosine, sine)
     gain_terms = jnp.sum(turned_back * raw * raw_inv, axis=(0, 1))
@@ -1648,9 +1802,6 @@
         ],
         axis=1,
     )
-    grad_a_part, grad_proj, down_part, plane_mid, all_b = lax.optimization_barrier(
-        (grad_a_part, grad_proj, down_part, plane_mid, all_b)
-    )
     ffn_out = lax.psum_scatter(
         down_part.reshape(tokens, model_width), "fsdp", scatter_dimension=0, tiled=True
     )
@@ -1675,8 +1826,10 @@
     grad_w_qkv = over_planes(mat_tn(grad_proj, normed_a))
     grad_w_head_gate = gate_total.reshape(w_head_gate.shape)
 
-    all_b, grad_a = lax.optimization_barrier((all_b, grad_a))
-    grad_w_gate, grad_w_up, grad_w_down = feed_weights(all_b, grad_all, w_gate, w_up, w_down)
+    line_b, grad_a = lax.optimization_barrier((line_b, grad_a))
+    grad_w_gate, grad_w_up, grad_w_down = feed_weights(
+        plane_b, plane_grad, line_b, other_grad, w_gate, w_up, w_down, 4
+    )
 
     gain_total = gain_total.reshape(-1)
     grad_attn_gain = gain_total[:wide]

time: 671 us -> 605 us (0.902)
  waiting for transfers between devices: 89.9 us -> 7.29 us
  local copies, waits for them, and re-layouts: 17.5 us -> 27.9 us
  Pallas kernels: 479 us -> 487 us
    pallas_call x1, Pallas kernels: 107 us -> 47.6 us  [exchange_heads(): pl.pallas_call(functools.partial(heads_kernel, planes), out_shape=(jax.Sh...]
    pallas_call x3, Pallas kernels: 266 us -> 312 us  [the longest x1 123 us: feed_weights(): pl.pallas_call(functools.partial(feed_weights_kernel, planes), in_specs=[...]
    all_gather x2 -> x0, waiting for transfers between devices: 35.8 us -> none  [the longest x1 35.8 us: local_planes(): all_b = lax.all_gather(normed_b, both, axis=0, tiled=True)]
    reduce_scatter x2, waiting for transfers between devices: 30.4 us -> 0.04 us  [over_planes(): lax.psum_scatter(part.astype(jnp.bfloat16), 'sp', scatter_dimension=0, ti...]
    pallas_call x1, Pallas kernels: 38.8 us -> 57.4 us  [scatter_plane(): pl.pallas_call(functools.partial(scatter_gains_kernel, planes), out_shape...]
    all_gather x2, waiting for transfers between devices: 23.1 us -> 6.04 us  [over_planes(): return lax.all_gather(reduced, 'sp', axis=0, tiled=True).astype(jnp.float32)]
    unnamed x45 -> x54, local copies, waits for them, and re-layouts: 5.7 us -> 16.3 us
  transfers between devices with their start and end apart: 7 -> 5, of which waited for: 4 -> 1; matrix products, arithmetic and copies ran while one was open for 9% -> 6% of each run, Pallas kernels for 51% -> 47%
where the time goes in v2:
time: 605 us; the launch traced here: 596 us
  Pallas kernels  487 us (80%)
  other arithmetic  34.8 us (6%)
  local copies, waits for them, and re-layouts  27.9 us (5%)
  matrix products  24.7 us (4%)
  between operations  14.6 us (2%)
  waiting for transfers between devices  7.29 us (1%)
    pallas_call x1, Pallas kernels, feed_weights(): pl.pallas_call(functools.partial(feed_weights_kernel, planes), in_specs=[...  123 us
    pallas_call x1, Pallas kernels, middle_layer(): pl.pallas_call(functools.partial(middle_kernel, planes), out_shape=(jax.S...  113 us
    pallas_call x1, Pallas kernels, return_heads(): pl.pallas_call(functools.partial(unheads_kernel, planes), out_shape=(jax....  76.5 us
    pallas_call x1, Pallas kernels, scatter_plane(): pl.pallas_call(functools.partial(scatter_gains_kernel, planes), out_shape...  57.4 us
    pallas_call x1, Pallas kernels, exchange_heads(): pl.pallas_call(functools.partial(heads_kernel, planes), out_shape=(jax.Sh...  47.6 us
    pallas_call x1, Pallas kernels, gather_plane(): pl.pallas_call(gather_gains_kernel, out_shape=(out, jax.ShapeDtypeStruct(...  32 us
    pallas_call x1, Pallas kernels, attend_back(): pl.pallas_call(functools.partial(attend_back_kernel, ranks, planes), grid...  22.6 us
    unnamed x54, local copies, waits for them, and re-layouts  16.3 us
  transfers between devices with their start and end apart: 5, of which 1 were waited for; matrix products, arithmetic and copies ran while one was open for 6% of the time, Pallas kernels for 47%

profile of v2, /device:TPU:1, one launch (start us, length us, event | category | flops | bytes accessed | tf_op | source)
XLA Modules:
  0.0 596.0 jit_solution(2721530810875598037)
XLA Ops:
  8.9 2.8 concatenate.12
  12.5 32.0 %gather_gains.1 = (bf16[8,128,2048]{2,1,0:T(8,128)(2,1)}, f32[8,8,128]{2,1,0:T(8,128)}) custom-call(bf16[128,2048]{1,0:T(8,128)(2,1)} %x_ref.3, f32[8,128]{1,0:T(8,128)} %bitcast_convert_fusion.1.s_ref), custom_call_target="tpu_custom_call" | custom-call | tf_op jit(solution)/shard_map/gather_gains/pallas_call | solution.py:506
  46.0 3.2 fusion
  50.5 3.7 multiply_reduce_fusion.2
  54.2 2.9 copy.39
  57.1 3.2 fusion.4
  69.9 47.6 %exchange_heads.1 = (bf16[2,1024,128]{2,1,0:T(8,128)(2,1)}, bf16[4,2,1024,128]{3,2,1,0:T(8,128)(2,1)}, bf16[8,128,2048]{2,1,0:T(8,128)(2,1)}) custom-call(bf16[4,1024,128]{2,1,0:T(8,128)(2,1)} %fusion.14.n_ref, bf16[128,2048]{1,0:T(8,128)(2,1)} %g_ref.1), custom_call_target="tpu_custom_call" | custom-call | tf_op jit(solution)/shard_map/exchange_heads/pallas_call | solution.py:889
  117.6 14.6 %attend.1 = (f32[2,1024,128]{2,1,0:T(8,128)}, f32[2,1024,1]{2,1,0:T(8,128)}, bf16[1024,256]{1,0:T(8,128)(2,1)}) custom-call(s32[5]{0:T(128)} %lengths_ref.3, bf16[2,1024,128]{2,1,0:T(8,128)(2,1)} %get-tuple-element.43.q_ref, bf16[4,2,8,128,128]{4,3,2,1,0:T(8,128)(2,1)} %bitcast.83, f32[2,1024,1]{2,1,0:T(8,128)} %copy.40.gate_ref), custom_call_target="tpu_custom_call" | custom-call | tf_op jit(solution)/shard_map/attend/pallas_call | solution.py:1187
  132.2 113.0 %middle_layer.1 = (bf16[8,128,2048]{2,1,0:T(8,128)(2,1)}, bf16[3,128,2048]{2,1,0:T(8,128)(2,1)}, bf16[3,128,2048]{2,1,0:T(8,128)(2,1)}, bf16[8,128,2048]{2,1,0:T...) custom-call(bf16[8,128,256]{2,1,0:T(8,128)(2,1)} %bitcast.94, ...), custom_call_target="tpu_custom_call" | custom-call | tf_op jit(solution)/shard_map/middle_layer/pallas_call | solution.py:1546
  245.2 4.5 convolution_convert_fusion.1
  249.7 22.6 %attend_back.1 = (bf16[2,1024,128]{2,1,0:T(8,128)(2,1)}, bf16[4,2,8,128,128]{4,3,2,1,0:T(8,128)(2,1)}, bf16[2,1024,1]{2,1,0:T(8,128)(2,1)}) custom-call(s32[5]{0:T(128)} %lengths_ref.3, bf16[2,1024,128]{2,1,0:T(8,128)(2,1)} %get-tuple-element.43.q_ref, bf16[4,2,8,128,128]{4,3,2,1,0:T(8,128)(2,1)} %bitcast.84, f32[2,1024,1]{2,1,0:T(8,128)} %copy.40.gate_ref, ...), custom_call_target="tpu_custom_call" | custom-call | tf_op jit(solution)/shard_map/attend_back/pallas_call | solution.py:1276
  272.4 76.5 %return_heads.1 = (bf16[4,1024,128]{2,1,0:T(8,128)(2,1)}, bf16[3,8,128,2048]{3,2,1,0:T(8,128)(2,1)}) custom-call(bf16[2,1024,128]{2,1,0:T(8,128)(2,1)} %get-tuple-element.53.dq_ref, bf16[4,2,1024,128]{3,2,1,0:T(8,128)(2,1)} %bitcast.90, bf16[3,128,2048]{2,1,0:T(8,128)(2,1)} %get-tuple-element.55.dz_ref), custom_call_target="tpu_custom_call" | custom-call | tf_op jit(solution)/shard_map/return_heads/pallas_call | solution.py:1077
  353.6 2.5 fusion.13
  357.5 6.2 %convolution_convert_fusion = bf16[512,2048]{1,0:T(8,128)(2,1)} fusion(bf16[1024,512]{0,1:T(8,128)(2,1)} %bitcast.91, bf16[1024,2048]{1,0:T(8,128)(2,1)} %bitcast.81), kind=kOutput, calls=%fused_computation.12 | convolution fusion | flops 2148532224 | bytes 7340032 | tf_op jit(solution)/shard_map/dot_general | solution.py:27
  366.6 2.9 fusion.18
  372.7 3.8 fusion.6
  377.3 57.4 %scatter_gains.1 = (f32[128,2048]{1,0:T(8,128)}, f32[8,128]{1,0:T(8,128)}, f32[32,128]{1,0:T(8,128)}) custom-call(bf16[8,128,2048]{2,1,0:T(8,128)(2,1)} %bitcast.79, f32[8,8,128]{2,1,0:T(8,128)} %bitcast.99, f32[32,128]{1,0:T(8,128)} %reshape.316.g_ref), custom_call_target="tpu_custom_call" | custom-call | tf_op jit(solution)/shard_map/scatter_gains/pallas_call | solution.py:629
  434.8 122.8 %feed_weights.1 = (f32[768,2048]{1,0:T(8,128)}, f32[768,2048]{1,0:T(8,128)}, f32[768,2048]{1,0:T(8,128)}, bf16[3,8,128,2048]{3,2,1,0:T(8,128)(2,1)}) custom-call(bf16[8,128,2048]{2,1,0:T(8,128)(2,1)} %get-tuple-element.63.xp_hbm, bf16[8,128,2048]{2,1,0:T(8,128)(2,1)} %get-tuple-element.46.dy_hbm.dp_hbm, bf16[3,128,2048]{2,1,0:T(8,128)(2,1)} %get-tuple-element.65.xz_hbm, ...), custom_call_target="tpu_custom_call" | custom-call | flops 77309411328 | bytes 61865984 | tf_op jit(solution)/shard_map/feed_weights/pallas_call | solution.py:1688
  561.2 2.9 convert_element_type.88
  566.0 6.0 %all-gather.3.cloned.1.call-done = bf16[512,2048]{1,0:T(8,128)(2,1)} async-done(((bf16[128,2048]{1,0:T(8,128)(2,1)}), bf16[512,2048]{1,0:T(8,128)(2,1)}) %all-gather.3.cloned.1.call-update) | async-done | bytes 2097168 | tf_op jit(solution)/shard_map/all_gather | solution.py:1823
  572.1 4.3 convert_element_type.86
  576.3 6.4 %copy.57 = f32[768,2048]{1,0:T(8,128)} copy(f32[768,2048]{1,0:T(8,128)} %get-tuple-element.120) | data formatting | bytes 12582912
  582.8 2.8 copy.58
  585.9 2.8 copy.59
  (112 shorter events, 33.9 us)
Async XLA Ops:
  7.2 43.3 %copy-start = (bf16[512,2048]{1,0:T(8,128)(2,1)S(1)}, bf16[512,2048]{1,0:T(8,128)(2,1)}, u32[]{:S(2)}) copy-start(bf16[512,2048]{1,0:T(8,128)(2,1)} %param.17) | copy-start | bytes 6291460
  7.2 356.5 %reduce-scatter.8.cloned.1.call-start = ((), (), s32[]{:S(2)}) async-start(), calls=%async_computation.6 | async-start | bytes 1310720 | tf_op jit(solution)/shard_map/reduce_scatter | solution.py:1820
  46.0 3.4 copy-start.2
  50.5 3.7 copy-start.6
  57.1 3.2 copy-start.15
  132.2 113.0 %copy-start.13 = (bf16[1024,256]{1,0:T(8,128)(2,1)S(1)}, bf16[1024,256]{1,0:T(8,128)(2,1)}, u32[]{:S(2)}) copy-start(bf16[1024,256]{1,0:T(8,128)(2,1)} %get-tuple-element.45) | copy-start | bytes 1572868
  249.7 185.0 %reduce-scatter.6.cloned.1.call-start = ((), (), s32[]{:S(2)}) async-start(), calls=%async_computation.4 | async-start | bytes 2621440 | tf_op jit(solution)/shard_map/reduce_scatter | solution.py:1820
  351.8 1.8 copy-start.8
  363.7 197.5 %all-gather.5.cloned.1.call-start = ((), (), s32[]{:S(2)}) async-start(), calls=%async_computation.7 | async-start | bytes 1310720 | tf_op jit(solution)/shard_map/all_gather | solution.py:1823
  364.4 199.7 %reduce-scatter.4.cloned.1.call-start = ((), (), s32[]{:S(2)}) async-start(), calls=%async_computation.3 | async-start | bytes 4718592 | tf_op jit(solution)/shard_map/reduce_scatter | solution.py:1805
  365.0 207.1 %all-gather.3.cloned.1.call-start = ((), (), s32[]{:S(2)}) async-start(), calls=%async_computation.5 | async-start | bytes 2621440 | tf_op jit(solution)/shard_map/all_gather | solution.py:1823
  366.6 3.7 copy-start.12
  370.3 2.4 copy-start.3
  434.7 122.9 %copy-start.16 = (f32[32,128]{1,0:T(8,128)S(1)}, f32[32,128]{1,0:T(8,128)}, u32[]{:S(2)}) copy-start(f32[32,128]{1,0:T(8,128)} %get-tuple-element.61) | copy-start | bytes 49156
  434.8 123.5 %copy-start.7 = (bf16[128,2048]{1,0:T(8,128)(2,1)S(1)}, bf16[128,2048]{1,0:T(8,128)(2,1)}, u32[]{:S(2)}) copy-start(bf16[128,2048]{1,0:T(8,128)(2,1)} %x_ref.3) | copy-start | bytes 1572868
  434.8 123.5 %copy-start.9 = (f32[128,2048]{1,0:T(8,128)S(1)}, f32[128,2048]{1,0:T(8,128)}, u32[]{:S(2)}) copy-start(f32[128,2048]{1,0:T(8,128)} %get-tuple-element.59) | copy-start | bytes 3145732
  434.8 123.8 %copy-start.18 = (f32[8,128]{1,0:T(8,128)S(1)}, f32[8,128]{1,0:T(8,128)}, u32[]{:S(2)}) copy-start(f32[8,128]{1,0:T(8,128)} %get-tuple-element.60) | copy-start | bytes 12292
  557.6 2.1 copy-start.10
  561.2 2.9 copy-start.11
  572.1 10.7 %slice-start.2 = ((s8[6291456]{0:T(1024)(128)(4,1)}), s8[4194304]{0:T(1024)(128)(4,1)S(1)}, s32[]{:S(2)}) async-start(s8[6291456]{0:T(1024)(128)(4,1)} %bitcast.87), calls=%async_computation.10 | async-start | bytes 8388608
  576.3 6.4 %slice-start.3 = ((s8[6291456]{0:T(1024)(128)(4,1)}), s8[2097152]{0:T(1024)(128)(4,1)S(1)}, s32[]{:S(2)}) async-start(s8[6291456]{0:T(1024)(128)(4,1)} %bitcast.87), calls=%async_computation.11 | async-start | bytes 4194304
  576.3 9.3 %slice-start = ((s8[6291456]{0:T(1024)(128)(4,1)}), s8[4194304]{0:T(1024)(128)(4,1)S(1)}, s32[]{:S(2)}) async-start(s8[6291456]{0:T(1024)(128)(4,1)} %bitcast.85), calls=%async_computation.8 | async-start | bytes 8388608
  582.8 3.1 slice-start.1
  585.9 3.1 copy-start.1
  (4 other events, 6.1 us)
Sparse Core Ops, SparseCore 0:
  249.8 25.5 reduce-scatter.7
  363.8 63.4 reduce-scatter.5
  428.9 27.2 all-gather.4
  459.4 66.4 reduce-scatter.3
  527.4 44.5 all-gather.2

commit v3 on v2

--- a/solution.py
+++ b/solution.py
@@ -405,7 +405,7 @@
 
 
 MESH = pl.DeviceIdType.MESH
-VMEM_LIMIT = 60 * 1024 * 1024
+VMEM_LIMIT = 62 * 1024 * 1024
 
 
 def peer_copy(src, dst, send_sem, recv_sem, rank, plane):
@@ -426,115 +426,31 @@
     pl.semaphore_wait(barrier, len(peers))
 
 
-def gather_gains_kernel(x_ref, s_ref, o_ref, so_ref, send_sem, recv_sem, sib_send, sib_recv, own_sem, small_send, small_recv):
+def scatter_gains_kernel(
+    p_ref, attn_ref, ffn_ref, head_ref, x_ref, scale_ref, dmid_ref, blocks_ref, o_ref, so_ref, next_ref, parts, small_buf, grad, small_send, small_recv, ag_send, ag_recv, own_sem, *rest
+):
     rank, plane = lax.axis_index("fsdp"), lax.axis_index("sp")
+    ranks = p_ref.shape[0]
     greet([(rank ^ k, plane) for k in range(1, 8)])
+    block = blocks_ref.at[1, 1]
+    own = pltpu.make_async_copy(block, next_ref.at[rank], own_sem)
+    own.start()
+    for i in range(4):
+        scatter_near(p_ref, i, rest[0], rest[3], rest[4]).start()
+    for r in range(ranks):
+        for i in range(2):
+            columns = slice((2 * r + i) * HEAD_DIM, (2 * r + i + 1) * HEAD_DIM)
+            parts[r, i : i + 1] = attn_ref[:, columns]
+            parts[r, 2 + i : 3 + i] = ffn_ref[:, columns]
+        parts[r, 4:5] = jnp.where(rank < ranks // 2, head_ref[...], 0.0)
+        parts[r, 5:6] = jnp.where(
+            (rank >= ranks // 2) & (rank < 3 * ranks // 4), head_ref[...], 0.0
+        )
+        parts[r, 6:8] = jnp.zeros((2, HEAD_DIM), jnp.float32)
     small = []
     for k in range(1, 8):
         copy = peer_copy(
-            s_ref, so_ref.at[rank], small_send.at[k - 1], small_recv.at[k - 1], rank ^ k, plane
-        )
-        copy.start()
-        small.append(copy)
-    so_ref[rank] = s_ref[...]
-    gather_blocks(x_ref, o_ref, send_sem, recv_sem, sib_send, sib_recv, own_sem)
-    for copy in small:
-        copy.wait()
-
-
-def gather_kernel(x_ref, o_ref, *sems):
-    rank, plane = lax.axis_index("fsdp"), lax.axis_index("sp")
-    greet([(rank ^ k, plane) for k in (1, 2, 4, 6)])
-    gather_blocks(x_ref, o_ref, *sems)
-
-
-def gather_blocks(x_ref, o_ref, send_sem, recv_sem, sib_send, sib_recv, own_sem):
-    rank, plane = lax.axis_index("fsdp"), lax.axis_index("sp")
-    half = x_ref.shape[0] // 2
-    own = pltpu.make_async_copy(x_ref, o_ref.at[rank], own_sem)
-    own.start()
-    far = {}
-    for h in range(2):
-        rows = pl.ds(h * half, half)
-        for i, k in enumerate((6, 2, 4)):
-            far[h, i] = peer_copy(
-                x_ref.at[rows],
-                o_ref.at[rank, rows],
-                send_sem.at[h, i],
-                recv_sem.at[h, i],
-                rank ^ k,
-                plane,
-            )
-            far[h, i].start()
-    near = []
-    first = peer_copy(
-        x_ref, o_ref.at[rank], sib_send.at[0, 3], sib_recv.at[0, 3], rank ^ 1, plane
-    )
-    first.start()
-    near.append(first)
-    for h in range(2):
-        rows = pl.ds(h * half, half)
-        for i, k in enumerate((6, 2, 4)):
-            far[h, i].wait_recv()
-            block = o_ref.at[rank ^ k, rows]
-            forward = peer_copy(
-                block, block, sib_send.at[h, i], sib_recv.at[h, i], rank ^ 1, plane
-            )
-            forward.start()
-            near.append(forward)
-    for copy in near:
-        copy.wait()
-    for copy in far.values():
-        copy.wait_send()
-    own.wait()
-
-
-def gather_plane(x, collective_id, small=None):
-    rows, width = x.shape
-    ranks = lax.axis_size("fsdp")
-    big = pl.BlockSpec(memory_space=pl.ANY)
-    sems = [
-        pltpu.SemaphoreType.DMA((2, 3)),
-        pltpu.SemaphoreType.DMA((2, 3)),
-        pltpu.SemaphoreType.DMA((2, 4)),
-        pltpu.SemaphoreType.DMA((2, 4)),
-        pltpu.SemaphoreType.DMA,
-    ]
-    out = jax.ShapeDtypeStruct((ranks, rows, width), x.dtype)
-    if small is not None:
-        vmem = pl.BlockSpec(memory_space=pltpu.VMEM)
-        return pl.pallas_call(
-            gather_gains_kernel,
-            out_shape=(out, jax.ShapeDtypeStruct((ranks,) + small.shape, small.dtype)),
-            in_specs=[big, vmem],
-            out_specs=(big, vmem),
-            scratch_shapes=sems + [pltpu.SemaphoreType.DMA((7,)), pltpu.SemaphoreType.DMA((7,))],
-            compiler_params=pltpu.CompilerParams(
-                collective_id=collective_id, has_side_effects=True, vmem_limit_bytes=VMEM_LIMIT
-            ),
-            name="gather_gains",
-        )(x, small)
-    return pl.pallas_call(
-        gather_kernel,
-        out_shape=out,
-        in_specs=[big],
-        out_specs=big,
-        scratch_shapes=sems,
-        compiler_params=pltpu.CompilerParams(
-            collective_id=collective_id, has_side_effects=True, vmem_limit_bytes=VMEM_LIMIT
-        ),
-        name="gather_plane",
-    )(x)
-
-
-def scatter_gains_kernel(planes, p_ref, s_ref, g_ref, o_ref, so_ref, go_ref, small_buf, line_out, line_buf, small_send, small_recv, line_send, line_recv, *rest):
-    rank, plane = lax.axis_index("fsdp"), lax.axis_index("sp")
-    others = [lax.rem(plane + k, planes) for k in range(1, planes)]
-    greet([(rank ^ k, plane) for k in range(1, 8)] + [(rank, other) for other in others])
-    small = []
-    for k in range(1, 8):
-        copy = peer_copy(
-            s_ref.at[rank ^ k],
+            parts.at[rank ^ k],
             small_buf.at[k - 1],
             small_send.at[k - 1],
             small_recv.at[k - 1],
@@ -543,120 +459,207 @@
         )
         copy.start()
         small.append(copy)
-    scatter_blocks(p_ref, o_ref, *rest)
-    total = s_ref[rank]
+    scatter_begin(p_ref, grad, *rest, started=True)
+    gather_start(next_ref, ag_send, ag_recv, own=block)
+    total = parts[rank]
     for k in range(1, 8):
         small[k - 1].wait()
         total = total + small_buf[k - 1]
-    tail = total.shape[0]
-    line_out[:tail] = total
-    line_out[tail:] = g_ref[...]
-    line = []
-    for k in range(1, planes):
-        copy = peer_copy(
-            line_out,
-            line_buf.at[k - 1],
-            line_send.at[k - 1],
-            line_recv.at[k - 1],
-            rank,
-            others[k - 1],
-        )
-        copy.start()
-        line.append(copy)
-    final = line_out[...]
-    for k in range(1, planes):
-        line[k - 1].wait()
-        final = final + line_buf[k - 1]
-    so_ref[...] = final[:tail]
-    go_ref[...] = final[tail:]
-
-
-def scatter_kernel(*refs):
+    so_ref[...] = total
+    gather_pass(next_ref, ag_send, ag_recv, NEIGHBOURS_FIRST)
+    scatter_end(p_ref, grad, *rest)
+    gather_pass(next_ref, ag_send, ag_recv, DIAGONAL)
+    inputs = x_ref[...].astype(jnp.float32)
+    o_ref[...] = dmid_ref[...] + norm_back(grad[...], inputs, inv_rms(inputs), scale_ref[...])
+    gather_wait(next_ref, ag_send, ag_recv, FROM_SIBLING)
+    gather_sent(next_ref, ag_send, ag_recv)
+    own.wait()
+
+
+SCATTER_ORDER = (6, 2, 4, 0)
+
+
+def scatter_far(i, out_buf, far_buf, send_sem, recv_sem):
     rank, plane = lax.axis_index("fsdp"), lax.axis_index("sp")
-    greet([(rank ^ k, plane) for k in (1, 2, 4, 6)])
-    scatter_blocks(*refs)
-
-
-def scatter_blocks(p_ref, o_ref, near_buf, out_buf, far_buf, sib_send, sib_recv, send_sem, recv_sem):
+    return peer_copy(
+        out_buf.at[i],
+        far_buf.at[i],
+        send_sem.at[i],
+        recv_sem.at[i],
+        rank ^ SCATTER_ORDER[i],
+        plane,
+    )
+
+
+def scatter_near(p_ref, i, near_buf, sib_send, sib_recv):
     rank, plane = lax.axis_index("fsdp"), lax.axis_index("sp")
-    order = (6, 2, 4, 0)
-    near = []
-    for i, k in enumerate(order):
-        copy = peer_copy(
-            p_ref.at[rank ^ 1 ^ k], near_buf.at[i], sib_send.at[i], sib_recv.at[i], rank ^ 1, plane
-        )
-        copy.start()
-        near.append(copy)
-    far = []
-    for i, k in enumerate(order):
-        near[i].wait_recv()
+    return peer_copy(
+        p_ref.at[rank ^ 1 ^ SCATTER_ORDER[i]],
+        near_buf.at[i],
+        sib_send.at[i],
+        sib_recv.at[i],
+        rank ^ 1,
+        plane,
+    )
+
+
+def scatter_begin(p_ref, o_ref, near_buf, out_buf, far_buf, sib_send, sib_recv, send_sem, recv_sem, started=False):
+    rank = lax.axis_index("fsdp")
+    for i in range(0 if started else 4):
+        scatter_near(p_ref, i, near_buf, sib_send, sib_recv).start()
+    for i, k in enumerate(SCATTER_ORDER):
+        scatter_near(p_ref, i, near_buf, sib_send, sib_recv).wait_recv()
         joined = p_ref[rank ^ k].astype(jnp.float32) + near_buf[i].astype(jnp.float32)
         if k:
             out_buf[i] = joined.astype(out_buf.dtype)
-            copy = peer_copy(
-                out_buf.at[i], far_buf.at[i], send_sem.at[i], recv_sem.at[i], rank ^ k, plane
-            )
-            copy.start()
-            far.append(copy)
+            scatter_far(i, out_buf, far_buf, send_sem, recv_sem).start()
         else:
             o_ref[...] = joined
+
+
+def scatter_end(p_ref, o_ref, near_buf, out_buf, far_buf, sib_send, sib_recv, send_sem, recv_sem):
     for i in (1, 2, 0):
-        far[i].wait_recv()
+        scatter_far(i, out_buf, far_buf, send_sem, recv_sem).wait_recv()
         o_ref[...] += far_buf[i].astype(jnp.float32)
-    for copy in near + far:
-        copy.wait_send()
-
-
-def scatter_plane(p, collective_id, small=None, gate=None):
-    ranks, rows, width = p.shape
-    vmem = pl.BlockSpec(memory_space=pltpu.VMEM)
-    scratch = [
-        pltpu.VMEM((4, rows, width), p.dtype),
-        pltpu.VMEM((3, rows, width), p.dtype),
-        pltpu.VMEM((3, rows, width), p.dtype),
+    for i in range(4):
+        scatter_near(p_ref, i, near_buf, sib_send, sib_recv).wait_send()
+    for i in range(3):
+        scatter_far(i, out_buf, far_buf, send_sem, recv_sem).wait_send()
+
+
+def scatter_scratch(rows, width, dtype):
+    return [
+        pltpu.VMEM((4, rows, width), dtype),
+        pltpu.VMEM((3, rows, width), dtype),
+        pltpu.VMEM((3, rows, width), dtype),
         pltpu.SemaphoreType.DMA((4,)),
         pltpu.SemaphoreType.DMA((4,)),
         pltpu.SemaphoreType.DMA((3,)),
         pltpu.SemaphoreType.DMA((3,)),
     ]
-    out = jax.ShapeDtypeStruct((rows, width), jnp.float32)
-    params = pltpu.CompilerParams(
-        collective_id=collective_id, has_side_effects=True, vmem_limit_bytes=VMEM_LIMIT
-    )
-    if small is not None:
-        planes = lax.axis_size("sp")
-        joint = (small.shape[1] + gate.shape[0], small.shape[2])
-        return pl.pallas_call(
-            functools.partial(scatter_gains_kernel, planes),
-            out_shape=(
-                out,
-                jax.ShapeDtypeStruct(small.shape[1:], small.dtype),
-                jax.ShapeDtypeStruct(gate.shape, gate.dtype),
-            ),
-            in_specs=[vmem, vmem, vmem],
-            out_specs=(vmem, vmem, vmem),
-            scratch_shapes=[
-                pltpu.VMEM((7,) + small.shape[1:], small.dtype),
-                pltpu.VMEM(joint, small.dtype),
-                pltpu.VMEM((planes - 1,) + joint, small.dtype),
-                pltpu.SemaphoreType.DMA((7,)),
-                pltpu.SemaphoreType.DMA((7,)),
-                pltpu.SemaphoreType.DMA((planes - 1,)),
-                pltpu.SemaphoreType.DMA((planes - 1,)),
-            ]
-            + scratch,
-            compiler_params=params,
-            name="scatter_gains",
-        )(p, small, gate)
+
+
+def scatter_gains(p, attn, ffn, head, x, scale, grad_middle, blocks, collective_id):
+    ranks, rows, width = p.shape
+    vmem = pl.BlockSpec(memory_space=pltpu.VMEM)
+    hbm = pl.BlockSpec(memory_space=pl.ANY)
+    small = (8, HEAD_DIM)
     return pl.pallas_call(
-        scatter_kernel,
-        out_shape=out,
-        in_specs=[vmem],
-        out_specs=vmem,
-        scratch_shapes=scratch,
-        compiler_params=params,
-        name="scatter_plane",
-    )(p)
+        scatter_gains_kernel,
+        out_shape=(
+            jax.ShapeDtypeStruct((rows, width), jnp.float32),
+            jax.ShapeDtypeStruct(small, jnp.float32),
+            jax.ShapeDtypeStruct(p.shape, blocks.dtype),
+        ),
+        in_specs=[vmem] * 7 + [hbm],
+        out_specs=(vmem, vmem, hbm),
+        scratch_shapes=[
+            pltpu.VMEM((ranks,) + small, jnp.float32),
+            pltpu.VMEM((7,) + small, jnp.float32),
+            pltpu.VMEM((rows, width), jnp.float32),
+            pltpu.SemaphoreType.DMA((7,)),
+            pltpu.SemaphoreType.DMA((7,)),
+            pltpu.SemaphoreType.DMA((GATHER_COPIES,)),
+            pltpu.SemaphoreType.DMA((GATHER_COPIES,)),
+            pltpu.SemaphoreType.DMA,
+        ]
+        + scatter_scratch(rows, width, p.dtype),
+        compiler_params=pltpu.CompilerParams(
+            collective_id=collective_id, has_side_effects=True, vmem_limit_bytes=VMEM_LIMIT
+        ),
+        name="scatter_gains",
+    )(p, attn, ffn, head, x, scale, grad_middle, blocks)
+
+
+def projection_back_kernel(
+    back_ref, raw_ref, cos_ref, sin_ref, xa_ref, x_ref, dgate_ref, gated_ref, pm_ref, w_ref, wg_ref, head_ref, dxa_ref, pieces_ref, gate_ref, attn_ref, terms_ref, sums
+):
+    rank = lax.axis_index("fsdp")
+    group, rows, width = back_ref.shape
+    out_rows = gated_ref.shape[1]
+
+    @pl.when(pl.program_id(0) == 0)
+    def _():
+        for ref in (sums, gate_ref, attn_ref, terms_ref):
+            ref[...] = jnp.zeros_like(ref)
+
+    cosine, sine = cos_ref[...], sin_ref[...]
+    columns = []
+    for m in range(group):
+        back = back_ref[m]
+        grad = back.astype(jnp.float32)
+        turned = grad * cosine - pltpu.roll(grad, width // 2, 1) * sine
+        raw = raw_ref[:, m * width : (m + 1) * width]
+        inverse = inv_rms(raw)
+        terms_ref[...] += jnp.sum(turned * raw * inverse, axis=0, keepdims=True)
+        grad_raw = norm_back(turned, raw, inverse, head_ref[...])
+        columns.append(jnp.where(rank >= 6, grad, grad_raw).astype(jnp.bfloat16))
+    grad_proj = jnp.concatenate(columns, axis=1)
+    grad_a = jnp.dot(grad_proj, w_ref[...], preferred_element_type=jnp.float32)
+    normed = xa_ref[...].reshape(rows, -1)
+    normed32 = normed.astype(jnp.float32)
+    for head in range(dgate_ref.shape[0]):
+        gate = dgate_ref[head].astype(jnp.float32)
+        grad_a = grad_a + gate * wg_ref[head : head + 1].astype(jnp.float32)
+        gate_ref[head : head + 1] += jnp.sum(gate * normed32, axis=0, keepdims=True)
+    inputs = x_ref[...].reshape(rows, -1).astype(jnp.float32)
+    attn_ref[...] += jnp.sum(grad_a * inputs * inv_rms(inputs), axis=0, keepdims=True)
+    dxa_ref[...] = grad_a.astype(jnp.bfloat16).reshape(dxa_ref.shape)
+    sums[:out_rows] += mat_tn(gated_ref[...], pm_ref[...].reshape(rows, -1))
+    sums[out_rows:] += mat_tn(grad_proj, normed)
+
+    @pl.when(pl.program_id(0) == pl.num_programs(0) - 1)
+    def _():
+        pieces_ref[...] = sums[...].astype(jnp.bfloat16)
+
+
+def projection_back(back, raw, cosine, sine, normed, inputs, gate_grad, gated, plane_mid, w_qkv, w_head_gate, head_scale):
+    ranks, rows, model_width = normed.shape
+    group, tokens, width = back.shape
+    pair = 2 * rows
+    blocks = pl.BlockSpec((2, rows, model_width), lambda i: (i, 0, 0))
+    thin = pl.BlockSpec((pair, width), lambda i: (i, 0))
+    heads, out_rows = gate_grad.shape[0], gated.shape[1]
+
+    def still(shape):
+        return pl.BlockSpec(shape, lambda i: (0, 0))
+
+    total = (out_rows + w_qkv.shape[0], model_width)
+    return pl.pallas_call(
+        projection_back_kernel,
+        grid=(tokens // pair,),
+        in_specs=[
+            pl.BlockSpec((group, pair, width), lambda i: (0, i, 0)),
+            pl.BlockSpec((pair, group * width), lambda i: (i, 0)),
+            thin,
+            thin,
+            blocks,
+            blocks,
+            pl.BlockSpec((heads, pair, 1), lambda i: (0, i, 0)),
+            pl.BlockSpec((pair, out_rows), lambda i: (i, 0)),
+            blocks,
+            still(w_qkv.shape),
+            still(w_head_gate.shape),
+            still(head_scale.shape),
+        ],
+        out_specs=(
+            blocks,
+            still(total),
+            still(w_head_gate.shape),
+            still((1, model_width)),
+            still((1, width)),
+        ),
+        out_shape=(
+            jax.ShapeDtypeStruct(normed.shape, jnp.bfloat16),
+            jax.ShapeDtypeStruct(total, jnp.bfloat16),
+            jax.ShapeDtypeStruct(w_head_gate.shape, jnp.float32),
+            jax.ShapeDtypeStruct((1, model_width), jnp.float32),
+            jax.ShapeDtypeStruct((1, width), jnp.float32),
+        ),
+        scratch_shapes=[pltpu.VMEM(total, jnp.float32)],
+        compiler_params=pltpu.CompilerParams(vmem_limit_bytes=VMEM_LIMIT),
+        name="projection_back",
+    )(back, raw, cosine, sine, normed, inputs, gate_grad, gated, plane_mid, w_qkv, w_head_gate, head_scale)
 
 
 GATHER_COPIES = 13
@@ -734,198 +737,22 @@
     pl.semaphore_wait(barrier, ranks - 1 + lower + upper)
 
 
-def heads_kernel(planes, n_ref, g_ref, q_ref, kv_ref, dy_ref, g_sem, ag_send, ag_recv, own_sem, q_send, q_recv, kv_send, kv_recv, line_send, line_recv):
-    rank, plane = lax.axis_index("fsdp"), lax.axis_index("sp")
-    greet_line(8, planes)
-    own_block = pltpu.make_async_copy(g_ref, dy_ref.at[rank], g_sem)
-    own_block.start()
-
-    def q_copy(m, to):
-        return peer_copy(n_ref.at[pl.ds(2 * m, 2)], q_ref, q_send.at[m], q_recv, to, plane)
-
-    def kv_copy(m, which, to):
-        return peer_copy(
-            n_ref.at[m], kv_ref.at[plane, which], kv_send.at[m], kv_recv.at[which], to, plane
-        )
-
-    def q_local():
-        return pltpu.make_async_copy(n_ref.at[pl.ds(0, 2)], q_ref, own_sem)
-
-    def kv_local(m, which):
-        return pltpu.make_async_copy(n_ref.at[m], kv_ref.at[plane, which], own_sem)
-
-    @pl.when(rank < 4)
-    def _():
-        for m in range(2):
-            @pl.when(2 * rank + m != rank)
-            def _():
-                q_copy(m, 2 * rank + m).start()
-
-    @pl.when(rank == 0)
-    def _():
-        q_local().start()
-
-    for which in range(2):
-        first = 4 + 2 * which
-        own_m = (first + 1) % 4
-
-        @pl.when((rank == first) | (rank == first + 1))
-        def _():
-            for m in range(4):
-                to = 4 * (rank - first) + m
-
-                @pl.when(to != rank)
-                def _():
-                    kv_copy(m, which, to).start()
-
-        @pl.when(rank == first + 1)
-        def _():
-            kv_local(own_m, which).start()
-
-    for which in range(2):
-        first = 4 + 2 * which
-        own_m = (first + 1) % 4
-
-        @pl.when(rank == first + 1)
-        def _():
-            kv_local(own_m, which).wait()
-
-        @pl.when(rank != first + 1)
-        def _():
-            kv_copy(0, which, 0).wait_recv()
-
-        line_step(planes, kv_ref, which, 0, line_send, line_recv)
-    gather_start(dy_ref, ag_send, ag_recv, g_ref)
-    for j in range(1, planes):
-        for which in range(2):
-            line_step(planes, kv_ref, which, j, line_send, line_recv)
-        if j == 1:
-            gather_pass(dy_ref, ag_send, ag_recv, NEIGHBOURS_FIRST)
-        if j == 2:
-            gather_pass(dy_ref, ag_send, ag_recv, DIAGONAL)
-    gather_wait(dy_ref, ag_send, ag_recv, FROM_SIBLING)
-    gather_sent(dy_ref, ag_send, ag_recv)
-    own_block.wait()
-
-    @pl.when(rank == 0)
-    def _():
-        q_local().wait()
-
-    @pl.when(rank != 0)
-    def _():
-        q_copy(0, 0).wait_recv()
-
-    @pl.when(rank < 4)
-    def _():
-        for m in range(2):
-            @pl.when(2 * rank + m != rank)
-            def _():
-                q_copy(m, 0).wait_send()
-
-    for which in range(2):
-        first = 4 + 2 * which
-
-        @pl.when((rank == first) | (rank == first + 1))
-        def _():
-            for m in range(4):
-                @pl.when(4 * (rank - first) + m != rank)
-                def _():
-                    kv_copy(m, which, 0).wait_send()
-
-    for j in range(planes - 1):
-        for which in range(2):
-            for side in range(2):
-                @pl.when(line_sends(planes, plane, j, side))
-                def _():
-                    line_copy(kv_ref, which, j, side, line_send, line_recv).wait_send()
-
-
 def line_sends(planes, plane, j, side):
     if side == 0:
         return (plane >= j) & (plane < planes - 1)
     return (plane + j <= planes - 1) & (plane > 0)
 
 
-def line_copy(kv_ref, which, j, side, line_send, line_recv):
-    rank, plane = lax.axis_index("fsdp"), lax.axis_index("sp")
-    origin = plane - j if side == 0 else plane + j
-    block = kv_ref.at[origin, which]
-    to = plane + 1 if side == 0 else plane - 1
-    return peer_copy(
-        block, block, line_send.at[side, j, which], line_recv.at[side, j, which], rank, to
-    )
-
-
-def line_step(planes, kv_ref, which, j, line_send, line_recv):
-    rank, plane = lax.axis_index("fsdp"), lax.axis_index("sp")
-    for side in range(2):
-        if j:
-            arrives = (plane >= j) if side == 0 else (plane + j <= planes - 1)
-
-            @pl.when(arrives)
-            def _():
-                origin = plane - j if side == 0 else plane + j
-                block = kv_ref.at[origin, which]
-                peer_copy(
-                    block,
-                    block,
-                    line_send.at[side, j - 1, which],
-                    line_recv.at[side, j - 1, which],
-                    rank,
-                    plane,
-                ).wait_recv()
-
-        if j < planes - 1:
-            @pl.when(line_sends(planes, plane, j, side))
-            def _():
-                line_copy(kv_ref, which, j, side, line_send, line_recv).start()
-
-
-def exchange_heads(natural, grad, collective_id):
-    _, tokens, width = natural.shape
-    planes = lax.axis_size("sp")
-    ranks = lax.axis_size("fsdp")
-    hbm = pl.BlockSpec(memory_space=pl.ANY)
-    return pl.pallas_call(
-        functools.partial(heads_kernel, planes),
-        out_shape=(
-            jax.ShapeDtypeStruct((2, tokens, width), natural.dtype),
-            jax.ShapeDtypeStruct((planes, 2, tokens, width), natural.dtype),
-            jax.ShapeDtypeStruct((ranks,) + grad.shape, grad.dtype),
-        ),
-        in_specs=[hbm, hbm],
-        out_specs=(hbm, hbm, hbm),
-        scratch_shapes=[
-            pltpu.SemaphoreType.DMA,
-            pltpu.SemaphoreType.DMA((GATHER_COPIES,)),
-            pltpu.SemaphoreType.DMA((GATHER_COPIES,)),
-            pltpu.SemaphoreType.DMA,
-            pltpu.SemaphoreType.DMA((2,)),
-            pltpu.SemaphoreType.DMA,
-            pltpu.SemaphoreType.DMA((4,)),
-            pltpu.SemaphoreType.DMA((2,)),
-            pltpu.SemaphoreType.DMA((2, planes - 1, 2)),
-            pltpu.SemaphoreType.DMA((2, planes - 1, 2)),
-        ],
-        compiler_params=pltpu.CompilerParams(
-            collective_id=collective_id, has_side_effects=True, vmem_limit_bytes=VMEM_LIMIT
-        ),
-        name="exchange_heads",
-    )(natural, grad)
-
-
-def unheads_kernel(planes, dq_ref, dkv_ref, dz_ref, n_ref, dy_ref, g_sem, ag_send, ag_recv, line_out, line_in, done, own_sem, q_send, q_recv, kv_send, kv_recv, line_send, line_recv):
+def unheads_kernel(planes, dq_ref, dkv_ref, blocks_ref, n_ref, next_ref, ag_send, ag_recv, own_sem2, line_out, line_in, done, own_sem, q_send, q_recv, kv_send, kv_recv, line_send, line_recv):
     rank, plane = lax.axis_index("fsdp"), lax.axis_index("sp")
     greet_line(8, planes)
+    gathers = [(next_ref.at[which], ag_send.at[which], ag_recv.at[which]) for which in range(2)]
     own_blocks = [
-        pltpu.make_async_copy(dz_ref.at[j], dy_ref.at[j, rank], g_sem.at[j])
-        for j in range(planes - 1)
+        pltpu.make_async_copy(blocks_ref.at[which, 0], next_ref.at[which, rank], own_sem2.at[which])
+        for which in range(2)
     ]
     for copy in own_blocks:
         copy.start()
-    gathers = [
-        (dy_ref.at[j], ag_send.at[j], ag_recv.at[j]) for j in range(planes - 1)
-    ]
 
     def q_copy(m, to):
         return peer_copy(dq_ref, n_ref.at[pl.ds(2 * m, 2)], q_send, q_recv.at[m], to, plane)
@@ -986,11 +813,12 @@
                 def _():
                     step_copy(j, which, side).start()
 
-        gather_start(*gathers[j], own=dz_ref.at[j])
-        if j:
-            gather_pass(*gathers[j - 1], NEIGHBOURS_FIRST)
-        if j > 1:
-            gather_pass(*gathers[j - 2], DIAGONAL)
+        if j == 0:
+            gather_start(*gathers[0], own=blocks_ref.at[0, 0])
+            gather_start(*gathers[1], own=blocks_ref.at[1, 0])
+        if j == 2:
+            gather_pass(*gathers[0], NEIGHBOURS_FIRST)
+            gather_pass(*gathers[1], NEIGHBOURS_FIRST)
 
     for which in range(2):
         total = dkv_ref[plane, which].astype(jnp.float32)
@@ -1017,9 +845,8 @@
             def _():
                 kv_local(m, which).start()
 
-    gather_pass(*gathers[planes - 2], NEIGHBOURS_FIRST)
-    for j in range(max(planes - 3, 0), planes - 1):
-        gather_pass(*gathers[j], DIAGONAL)
+    for gather in gathers:
+        gather_pass(*gather, DIAGONAL)
     for gather in gathers:
         gather_wait(*gather, FROM_SIBLING)
         gather_sent(*gather)
@@ -1068,7 +895,7 @@
                     step_copy(j, which, side).wait_send()
 
 
-def return_heads(grad_query, grad_kv, grad_line, collective_id):
+def return_heads(grad_query, grad_kv, line_blocks, collective_id):
     _, tokens, width = grad_query.shape
     planes = lax.axis_size("sp")
     ranks = lax.axis_size("fsdp")
@@ -1078,14 +905,14 @@
         functools.partial(unheads_kernel, planes),
         out_shape=(
             jax.ShapeDtypeStruct((4, tokens, width), grad_query.dtype),
-            jax.ShapeDtypeStruct((planes - 1, ranks) + grad_line.shape[1:], grad_line.dtype),
+            jax.ShapeDtypeStruct((2, ranks) + line_blocks.shape[2:], line_blocks.dtype),
         ),
         in_specs=[vmem, vmem, hbm],
         out_specs=(vmem, hbm),
         scratch_shapes=[
-            pltpu.SemaphoreType.DMA((planes - 1,)),
-            pltpu.SemaphoreType.DMA((planes - 1, GATHER_COPIES)),
-            pltpu.SemaphoreType.DMA((planes - 1, GATHER_COPIES)),
+            pltpu.SemaphoreType.DMA((2, GATHER_COPIES)),
+            pltpu.SemaphoreType.DMA((2, GATHER_COPIES)),
+            pltpu.SemaphoreType.DMA((2,)),
             pltpu.VMEM((2, planes - 1, 2, tokens, width), grad_query.dtype),
             pltpu.VMEM((2, planes - 1, 2, tokens, width), grad_query.dtype),
             pltpu.VMEM((2, tokens, width), grad_query.dtype),
@@ -1101,7 +928,7 @@
             collective_id=collective_id, has_side_effects=True, vmem_limit_bytes=VMEM_LIMIT
         ),
         name="return_heads",
-    )(grad_query, grad_kv, grad_line)
+    )(grad_query, grad_kv, line_blocks)
 
 
 def stack_heads(ref):
@@ -1311,14 +1138,14 @@
     wu_hbm,
     wd_hbm,
     xg,
-    xz_hbm,
-    dz_hbm,
+    line_hbm,
     down_hbm,
     mid_ref,
     dmid_ref,
     gain_ref,
     pm_ref,
     dgated_ref,
+    act_ref,
     wg,
     wu,
     wd,
@@ -1353,11 +1180,11 @@
     others = [lax.rem(plane + k, planes) for k in range(1, planes)]
     greet([(rank ^ k, plane) for k in (1, 2, 4, 6)] + [(rank, other) for other in others])
 
-    def along(source, target, which):
+    def along(source, which):
         return [
             peer_copy(
                 source,
-                target.at[j - 1],
+                line_hbm.at[which, j - 1],
                 line_send.at[which, j - 1],
                 line_recv.at[which, j - 1],
                 rank,
@@ -1396,7 +1223,7 @@
     dy_load.start()
     for copy in loads:
         copy.start()
-    dy_line = along(dy_hbm.at[rank], dz_hbm, 0)
+    dy_line = along(dy_hbm.at[rank], 1)
     for copy in dy_line:
         copy.start()
     for i, k in enumerate(order):
@@ -1429,7 +1256,7 @@
     xg[rank] = normed
     sems = (ag_send.at[0], ag_recv.at[0])
     gather_start(xg, *sems)
-    xb_line = along(xg.at[rank], xz_hbm, 1)
+    xb_line = along(xg.at[rank], 0)
     for copy in xb_line:
         copy.start()
 
@@ -1464,6 +1291,8 @@
         near_out[1, i] = theirs.astype(jnp.bfloat16)
         near(1, i).start()
         hidden = (swish * up_pre).astype(jnp.bfloat16)
+        for kept, value in enumerate((grad_gate, grad_up, hidden)):
+            act_ref[kept, pl.ds(pl.multiple_of(2 * rows * p, 2 * rows), 2 * rows)] = value
         down = jnp.dot(hidden, wd[...], preferred_element_type=jnp.float32)
         if k in (4, 6):
             down_copy(p, slot).wait()
@@ -1547,17 +1376,17 @@
         functools.partial(middle_kernel, planes),
         out_shape=(
             jax.ShapeDtypeStruct((ranks, rows, width), half),
-            jax.ShapeDtypeStruct((planes - 1, rows, width), half),
-            jax.ShapeDtypeStruct((planes - 1, rows, width), half),
+            jax.ShapeDtypeStruct((2, planes - 1, rows, width), half),
             jax.ShapeDtypeStruct((ranks, rows, width), half),
             jax.ShapeDtypeStruct((rows, width), full),
             jax.ShapeDtypeStruct((rows, width), full),
             jax.ShapeDtypeStruct((1, width), full),
             jax.ShapeDtypeStruct((ranks, rows, width), half),
             jax.ShapeDtypeStruct((ranks, rows, features), full),
+            jax.ShapeDtypeStruct((3, ranks * rows, hidden), half),
         ),
         in_specs=[vmem, vmem, vmem, vmem, hbm, hbm, hbm, hbm],
-        out_specs=(vmem, hbm, hbm, hbm, vmem, vmem, vmem, vmem, vmem),
+        out_specs=(vmem, hbm, hbm, vmem, vmem, vmem, vmem, vmem, vmem),
         scratch_shapes=[
             pltpu.VMEM((hidden, width), half),
             pltpu.VMEM((hidden, width), half),
@@ -1590,116 +1419,259 @@
 
 
 def feed_weights_kernel(
-    planes, xp_hbm, dp_hbm, xz_hbm, dy_hbm, wg_ref, wu_ref, wd_ref, og_ref, ou_ref, od_ref, xo_hbm, xbuf, dbuf, x_sem, d_sem, own_sem, ag_send, ag_recv
+    planes,
+    xp_hbm,
+    dp_hbm,
+    act_hbm,
+    blocks_hbm,
+    first_hbm,
+    second_hbm,
+    down_hbm,
+    mid_ref,
+    small_ref,
+    rows_ref,
+    wg_ref,
+    wu_ref,
+    wd_ref,
+    og_ref,
+    ou_ref,
+    od_ref,
+    h_ref,
+    so_ref,
+    go_ref,
+    more_hbm,
+    xbuf,
+    dbuf,
+    act,
+    parts,
+    small_buf,
+    rows_buf,
+    x_sem,
+    d_sem,
+    act_sem,
+    part_sem,
+    own_sem,
+    ag_send,
+    ag_recv,
+    line_send,
+    line_recv,
+    near_buf,
+    out_buf,
+    far_buf,
+    sib_send,
+    sib_recv,
+    send_sem,
+    recv_sem,
 ):
     rank, plane = lax.axis_index("fsdp"), lax.axis_index("sp")
     ranks, rows, width = xp_hbm.shape
     part = ranks // 2
-    greet([(rank ^ k, plane) for k in (1, 2, 4)])
+    chunk = part * rows
+    others = [lax.rem(plane + k, planes) for k in range(1, planes)]
+    greet([(rank ^ k, plane) for k in (1, 2, 4, 6)] + [(rank, other) for other in others])
+
+    picks = ((0, 1), (1, 2), (0, 2))
+    gathers = [(more_hbm.at[g], ag_send.at[g], ag_recv.at[g]) for g in range(3)]
     own_blocks = [
-        pltpu.make_async_copy(xz_hbm.at[j], xo_hbm.at[j, rank], own_sem.at[j])
-        for j in range(planes - 1)
+        pltpu.make_async_copy(blocks_hbm.at[pick], more_hbm.at[g, rank], own_sem.at[g])
+        for g, pick in enumerate(picks)
     ]
-    gathers = [(xo_hbm.at[j], ag_send.at[j], ag_recv.at[j]) for j in range(planes - 1)]
+
+    def begin(g):
+        gather_start(*gathers[g], own=blocks_hbm.at[picks[g]])
 
     def load(step, start):
         slot = lax.rem(step, 2)
         block = pl.ds(part * lax.rem(step, 2), part)
         group = step // 2
-
-        def go(x_from, d_from):
-            for copy in (
-                pltpu.make_async_copy(x_from, xbuf.at[slot], x_sem.at[slot]),
-                pltpu.make_async_copy(d_from, dbuf.at[slot], d_sem.at[slot]),
-            ):
-                if start:
-                    copy.start()
-                else:
-                    copy.wait()
-
-        @pl.when(group == 0)
-        def _():
-            go(xp_hbm.at[block], dp_hbm.at[block])
-
-        @pl.when(group > 0)
-        def _():
-            go(xo_hbm.at[group - 1, block], dy_hbm.at[group - 1, block])
+        sources = (
+            (first_hbm.at[0, block], first_hbm.at[1, block]),
+            (xp_hbm.at[block], dp_hbm.at[block]),
+            (more_hbm.at[0, block], second_hbm.at[block]),
+            (more_hbm.at[2, block], more_hbm.at[1, block]),
+        )
+        for index, (x_from, d_from) in enumerate(sources):
+            @pl.when(group == index)
+            def _():
+                for copy in (
+                    pltpu.make_async_copy(x_from, xbuf.at[slot], x_sem.at[slot]),
+                    pltpu.make_async_copy(d_from, dbuf.at[slot], d_sem.at[slot]),
+                ):
+                    if start:
+                        copy.start()
+                    else:
+                        copy.wait()
+
+    def kept(step):
+        where = pl.ds(pl.multiple_of(step * chunk, chunk), chunk)
+        return pltpu.make_async_copy(act_hbm.at[:, where], act, act_sem)
+
+    scatter = (near_buf, sib_send, sib_recv)
+    own_parts = [
+        pltpu.make_async_copy(down_hbm.at[rank ^ k], parts.at[i], part_sem.at[i])
+        for i, k in enumerate(SCATTER_ORDER)
+    ]
+    small = [
+        peer_copy(
+            source,
+            buffer.at[k],
+            line_send.at[which, k],
+            line_recv.at[which, k],
+            rank,
+            others[k],
+        )
+        for which, (source, buffer) in enumerate(((small_ref, small_buf), (rows_ref, rows_buf)))
+        for k in range(planes - 1)
+    ]
 
     load(0, True)
-    for copy in own_blocks:
+    for copy in own_blocks + small + own_parts:
         copy.start()
-    gather_start(*gathers[0], own=xz_hbm.at[0])
+    begin(0)
+    for i in range(4):
+        scatter_near(down_hbm, i, *scatter).start()
 
     @pl.loop(0, 2 * planes)
     def _(step):
-        for j in range(planes - 1):
-            @pl.when(step == 2 * j + 1)
-            def _():
-                gather_pass(*gathers[j], NEIGHBOURS_FIRST)
-                if j < planes - 2:
-                    gather_start(*gathers[j + 1], own=xz_hbm.at[j + 1])
-
-            @pl.when(step == 2 * j + 2)
-            def _():
-                gather_pass(*gathers[j], DIAGONAL)
-                gather_wait(*gathers[j], FROM_SIBLING)
-                own_blocks[j].wait()
-                load(step, True)
+        @pl.when(step == 1)
+        def _():
+            gather_pass(*gathers[0], NEIGHBOURS_FIRST)
+            begin(1)
+
+        @pl.when(step == 2)
+        def _():
+            kept(0).start()
+            gather_pass(*gathers[0], DIAGONAL)
+            gather_pass(*gathers[1], NEIGHBOURS_FIRST)
+            begin(2)
+
+        @pl.when(step == 3)
+        def _():
+            kept(1).start()
+            for i, k in enumerate(SCATTER_ORDER):
+                own_parts[i].wait()
+                scatter_near(down_hbm, i, *scatter).wait_recv()
+                joined = parts[i].astype(jnp.float32) + near_buf[i].astype(jnp.float32)
+                if k:
+                    out_buf[i] = joined.astype(out_buf.dtype)
+                else:
+                    parts[i] = joined.astype(parts.dtype)
+
+        @pl.when(step == 4)
+        def _():
+            gather_wait(*gathers[0], FROM_SIBLING)
+            own_blocks[0].wait()
+            load(step, True)
+            gather_pass(*gathers[1], DIAGONAL)
+
+        @pl.when(step == 5)
+        def _():
+            gather_pass(*gathers[2], NEIGHBOURS_FIRST)
+            for i in range(3):
+                scatter_far(i, out_buf, far_buf, send_sem, recv_sem).start()
+
+        @pl.when(step == 6)
+        def _():
+            gather_pass(*gathers[2], DIAGONAL)
+            for g in (1, 2):
+                gather_wait(*gathers[g], FROM_SIBLING)
+                own_blocks[g].wait()
+            load(step, True)
 
         load(step, False)
 
-        @pl.when(lax.rem(step, 2) == 0)
+        @pl.when((lax.rem(step, 2) == 0) | (step == 1))
         def _():
             load(step + 1, True)
 
         slot = lax.rem(step, 2)
-        normed = xbuf[slot].reshape(part * rows, width)
-        grad = dbuf[slot].reshape(part * rows, width)
-        gate_pre = mat_nt(normed, wg_ref[...])
-        up_pre = mat_nt(normed, wu_ref[...])
-        grad_hidden = mat_nt(grad, wd_ref[...])
-        sigma = jax.nn.sigmoid(gate_pre)
-        swish = gate_pre * sigma
-        hidden = (swish * up_pre).astype(jnp.bfloat16)
-        grad_gate = (grad_hidden * up_pre * sigma * (1.0 + gate_pre * (1.0 - sigma))).astype(
-            jnp.bfloat16
-        )
-        grad_up = (grad_hidden * swish).astype(jnp.bfloat16)
+        normed = xbuf[slot].reshape(chunk, width)
+        grad = dbuf[slot].reshape(chunk, width)
+
+        own = step // 2 == 1
+
+        @pl.when(own)
+        def _():
+            kept(0).wait()
+
+        @pl.when(jnp.logical_not(own))
+        def _():
+            gate_pre = mat_nt(normed, wg_ref[...])
+            up_pre = mat_nt(normed, wu_ref[...])
+            grad_hidden = mat_nt(grad, wd_ref[...])
+            sigma = jax.nn.sigmoid(gate_pre)
+            swish = gate_pre * sigma
+            act[0] = (grad_hidden * up_pre * sigma * (1.0 + gate_pre * (1.0 - sigma))).astype(
+                jnp.bfloat16
+            )
+            act[1] = (grad_hidden * swish).astype(jnp.bfloat16)
+            act[2] = (swish * up_pre).astype(jnp.bfloat16)
 
         @pl.when(step == 0)
         def _():
             for ref in (og_ref, ou_ref, od_ref):
                 ref[...] = jnp.zeros_like(ref)
 
-        og_ref[...] += mat_tn(grad_gate, normed)
-        ou_ref[...] += mat_tn(grad_up, normed)
-        od_ref[...] += mat_tn(hidden, grad)
-
+        og_ref[...] += mat_tn(act[0], normed)
+        ou_ref[...] += mat_tn(act[1], normed)
+        od_ref[...] += mat_tn(act[2], grad)
+
+    output = mid_ref[...] + parts[3].astype(jnp.float32)
+    for i in range(3):
+        scatter_far(i, out_buf, far_buf, send_sem, recv_sem).wait()
+        output = output + far_buf[i].astype(jnp.float32)
+    h_ref[...] = output.astype(h_ref.dtype)
+    for copy in small:
+        copy.wait()
+    total, gate_rows = small_ref[...], rows_ref[...]
+    for k in range(planes - 1):
+        total = total + small_buf[k]
+        gate_rows = gate_rows + rows_buf[k]
+    so_ref[...] = total
+    go_ref[...] = gate_rows
+    for i in range(4):
+        scatter_near(down_hbm, i, *scatter).wait_send()
     for gather in gathers:
         gather_sent(*gather)
 
 
-def feed_weights(plane_x, plane_grad, line_x, other_grad, w_gate, w_up, w_down, collective_id):
+def feed_weights(plane_x, plane_grad, acts, blocks, first, second, down, middle, small, gate_rows, w_gate, w_up, w_down, collective_id):
     ranks, rows, width = plane_x.shape
     planes = lax.axis_size("sp")
+    hidden = w_gate.shape[0]
     vmem = pl.BlockSpec(memory_space=pltpu.VMEM)
     hbm = pl.BlockSpec(memory_space=pl.ANY)
     tokens = planes * ranks * rows
+    half, full = plane_x.dtype, jnp.float32
     return pl.pallas_call(
         functools.partial(feed_weights_kernel, planes),
-        in_specs=[hbm, hbm, hbm, hbm, vmem, vmem, vmem],
-        out_specs=(vmem, vmem, vmem, hbm),
-        out_shape=[jax.ShapeDtypeStruct(w_gate.shape, jnp.float32)] * 3
-        + [jax.ShapeDtypeStruct((planes - 1, ranks, rows, width), plane_x.dtype)],
+        in_specs=[hbm] * 7 + [vmem] * 6,
+        out_specs=(vmem,) * 6 + (hbm,),
+        out_shape=[jax.ShapeDtypeStruct(w_gate.shape, full)] * 3
+        + [
+            jax.ShapeDtypeStruct((rows, width), half),
+            jax.ShapeDtypeStruct(small.shape, full),
+            jax.ShapeDtypeStruct(gate_rows.shape, full),
+            jax.ShapeDtypeStruct((3, ranks, rows, width), half),
+        ],
         scratch_shapes=[
-            pltpu.VMEM((2, ranks // 2, rows, width), plane_x.dtype),
-            pltpu.VMEM((2, ranks // 2, rows, width), plane_x.dtype),
+            pltpu.VMEM((2, ranks // 2, rows, width), half),
+            pltpu.VMEM((2, ranks // 2, rows, width), half),
+            pltpu.VMEM((3, ranks // 2 * rows, hidden), half),
+            pltpu.VMEM((4, rows, width), half),
+            pltpu.VMEM((planes - 1,) + small.shape, full),
+            pltpu.VMEM((planes - 1,) + gate_rows.shape, full),
             pltpu.SemaphoreType.DMA((2,)),
             pltpu.SemaphoreType.DMA((2,)),
-            pltpu.SemaphoreType.DMA((planes - 1,)),
-            pltpu.SemaphoreType.DMA((planes - 1, GATHER_COPIES)),
-            pltpu.SemaphoreType.DMA((planes - 1, GATHER_COPIES)),
-        ],
+            pltpu.SemaphoreType.DMA,
+            pltpu.SemaphoreType.DMA((4,)),
+            pltpu.SemaphoreType.DMA((3,)),
+            pltpu.SemaphoreType.DMA((3, GATHER_COPIES)),
+            pltpu.SemaphoreType.DMA((3, GATHER_COPIES)),
+            pltpu.SemaphoreType.DMA((2, planes - 1)),
+            pltpu.SemaphoreType.DMA((2, planes - 1)),
+        ]
+        + scatter_scratch(rows, width, half),
         cost_estimate=pl.CostEstimate(
             flops=12 * tokens * w_gate.size,
             bytes_accessed=4 * tokens * width + 18 * w_gate.size,
@@ -1709,7 +1681,333 @@
             collective_id=collective_id, has_side_effects=True, vmem_limit_bytes=VMEM_LIMIT
         ),
         name="feed_weights",
-    )(plane_x, plane_grad, line_x, other_grad, w_gate, w_up, w_down)[:3]
+    )(plane_x, plane_grad, acts, blocks, first, second, down, middle, small, gate_rows, w_gate, w_up, w_down)[:6]
+
+
+def front_kernel(
+    planes,
+    lengths_ref,
+    x_ref,
+    small_ref,
+    w_ref,
+    wg_ref,
+    dyo_ref,
+    q_ref,
+    kv_ref,
+    dy_ref,
+    xg,
+    xa_ref,
+    raw_ref,
+    gate_ref,
+    attn_ref,
+    ffn_ref,
+    head_ref,
+    cos_ref,
+    sin_ref,
+    nat,
+    gains,
+    small_send,
+    small_recv,
+    ag_send,
+    ag_recv,
+    own_sem,
+    local_sem,
+    q_send,
+    q_recv,
+    kv_send,
+    kv_recv,
+    line_send,
+    line_recv,
+):
+    rank, plane = lax.axis_index("fsdp"), lax.axis_index("sp")
+    ranks, rows, width = xg.shape
+    pair_rows = 2 * rows
+    chip = rank // 2
+    greet_line(ranks, planes)
+    own_block = pltpu.make_async_copy(dyo_ref, dy_ref.at[rank], own_sem)
+    own_block.start()
+    small = []
+    for k in range(1, ranks):
+        copy = peer_copy(
+            small_ref, gains.at[rank], small_send.at[k - 1], small_recv.at[k - 1], rank ^ k, plane
+        )
+        copy.start()
+        small.append(copy)
+    sems = (ag_send.at[0], ag_recv.at[0])
+    gather_start(xg, *sems, own=x_ref)
+    xg[rank] = x_ref[...]
+    gains[rank] = small_ref[...]
+
+    half = HEAD_DIM // 2
+    lane = lax.broadcasted_iota(jnp.int32, (1, HEAD_DIM), 1)
+    step = lax.rem(lane, half).astype(jnp.float32)
+    frequency = jnp.exp(-math.log(ROPE_BASE) * 2.0 * step / HEAD_DIM)
+    sign = jnp.where(lane < half, -1.0, 1.0)
+
+    @pl.loop(0, ranks)
+    def _(block):
+        tokens = (block * planes + plane) * rows + lax.broadcasted_iota(jnp.int32, (rows, 1), 0)
+        position = tokens - row_starts(lengths_ref, tokens)
+        angles = position.astype(jnp.float32) * frequency
+        where = pl.ds(pl.multiple_of(block * rows, rows), rows)
+        cos_ref[where] = jnp.cos(angles)
+        sin_ref[where] = jnp.sin(angles) * sign
+
+    for copy in small:
+        copy.wait_recv()
+    head_q, head_k = gains[0, 4:5], gains[0, 5:6]
+    for r in range(1, ranks):
+        head_q = head_q + gains[r, 4:5]
+        head_k = head_k + gains[r, 5:6]
+    head_ref[...] = jnp.where(rank < ranks // 2, head_q, head_k)
+    for r in range(ranks):
+        for i in range(2):
+            columns = slice((2 * r + i) * HEAD_DIM, (2 * r + i + 1) * HEAD_DIM)
+            attn_ref[:, columns] = gains[r, i : i + 1]
+            ffn_ref[:, columns] = gains[r, 2 + i : 3 + i]
+
+    def token_rows(p):
+        return pl.ds(pl.multiple_of(p * pair_rows, pair_rows), pair_rows)
+
+    def q_copy(m, p, to):
+        return peer_copy(
+            nat.at[pl.ds(2 * m, 2), token_rows(p)],
+            q_ref.at[:, token_rows(p)],
+            q_send.at[m, p],
+            q_recv.at[p],
+            to,
+            plane,
+        )
+
+    def kv_copy(m, which, p, to):
+        return peer_copy(
+            nat.at[m, token_rows(p)],
+            kv_ref.at[plane, which, token_rows(p)],
+            kv_send.at[m, p],
+            kv_recv.at[which, p],
+            to,
+            plane,
+        )
+
+    def q_local(p):
+        return pltpu.make_async_copy(
+            nat.at[pl.ds(0, 2), token_rows(p)], q_ref.at[:, token_rows(p)], local_sem.at[p]
+        )
+
+    def kv_local(m, which, p):
+        return pltpu.make_async_copy(
+            nat.at[m, token_rows(p)], kv_ref.at[plane, which, token_rows(p)], local_sem.at[p]
+        )
+
+    def process(k):
+        p = chip ^ (k // 2)
+        inputs = xg[pl.ds(2 * p, 2)].reshape(pair_rows, width).astype(jnp.float32)
+        normed = (inputs * inv_rms(inputs) * attn_ref[...]).astype(jnp.bfloat16)
+        xa_ref[pl.ds(2 * p, 2)] = normed.reshape(2, rows, width)
+        projected = mat_nt(normed, w_ref[...])
+        raw_ref[token_rows(p)] = projected
+        logits = mat_nt(normed, wg_ref[...])
+        for head in range(gate_ref.shape[0]):
+            gate_ref[head, token_rows(p)] = logits[:, head : head + 1]
+        cosine, sine = cos_ref[token_rows(p)], sin_ref[token_rows(p)]
+        for m in range(4):
+            head = projected[:, m * HEAD_DIM : (m + 1) * HEAD_DIM]
+            scaled = head * inv_rms(head) * head_ref[...]
+            turned = scaled * cosine + pltpu.roll(scaled, half, 1) * sine
+            nat[m, token_rows(p)] = jnp.where(rank >= 6, head, turned).astype(jnp.bfloat16)
+
+        @pl.when(rank < 4)
+        def _():
+            for m in range(2):
+                @pl.when(2 * rank + m != rank)
+                def _():
+                    q_copy(m, p, 2 * rank + m).start()
+
+        @pl.when(rank == 0)
+        def _():
+            q_local(p).start()
+
+        for which in range(2):
+            first = 4 + 2 * which
+
+            @pl.when((rank == first) | (rank == first + 1))
+            def _():
+                for m in range(4):
+                    to = 4 * (rank - first) + m
+
+                    @pl.when(to != rank)
+                    def _():
+                        kv_copy(m, which, p, to).start()
+
+            @pl.when(rank == first + 1)
+            def _():
+                kv_local((first + 1) % 4, which, p).start()
+
+    def line_piece(origin, which, p, side, j, to):
+        piece = kv_ref.at[origin, which, token_rows(p)]
+        return peer_copy(
+            piece,
+            piece,
+            line_send.at[side, j, which, p],
+            line_recv.at[side, j, which, p],
+            rank,
+            to,
+        )
+
+    def origin_of(side, j):
+        return plane - j if side == 0 else plane + j
+
+    def next_of(side):
+        return plane + 1 if side == 0 else plane - 1
+
+    def line_go(which, p, j):
+        if j == 0:
+            @pl.when(rank == 5 + 2 * which)
+            def _():
+                kv_local((5 + 2 * which) % 4, which, p).wait()
+
+            @pl.when(rank != 5 + 2 * which)
+            def _():
+                kv_copy(0, which, p, 0).wait_recv()
+
+        for side in range(2):
+            if j:
+                arrives = (plane >= j) if side == 0 else (plane + j <= planes - 1)
+
+                @pl.when(arrives)
+                def _():
+                    line_piece(origin_of(side, j), which, p, side, j - 1, plane).wait_recv()
+
+            if j < planes - 1:
+                @pl.when(line_sends(planes, plane, j, side))
+                def _():
+                    line_piece(origin_of(side, j), which, p, side, j, next_of(side)).start()
+
+    slots = (((0, 2), (1, 3)), ((0, 3), (1, 2)), ((0, 0), (1, 1)), ((0, 1), (1, 0)))
+
+    def slot_go(slot, j):
+        for which, p in slots[slot]:
+            line_go(which, p, j)
+
+    gather_wait(xg, *sems, (6,))
+    process(0)
+    slot_go(0, 0)
+    gather_pass(xg, *sems, NEIGHBOURS_FIRST)
+    gather_wait(xg, *sems, (7, 8))
+    process(2)
+    slot_go(0, 1)
+    gather_wait(xg, *sems, (9, 10))
+    process(4)
+    gather_pass(xg, *sems, DIAGONAL)
+    slot_go(1, 0)
+    slot_go(0, 2)
+    gather_wait(xg, *sems, (11, 12))
+    process(6)
+    sems2 = (ag_send.at[1], ag_recv.at[1])
+    slot_go(2, 0)
+    slot_go(1, 1)
+    slot_go(3, 0)
+    gather_start(dy_ref, *sems2, own=dyo_ref)
+    slot_go(0, 3)
+    slot_go(1, 2)
+    slot_go(2, 1)
+    slot_go(3, 1)
+    slot_go(1, 3)
+    slot_go(2, 2)
+    gather_pass(dy_ref, *sems2, NEIGHBOURS_FIRST)
+    slot_go(3, 2)
+    slot_go(2, 3)
+    gather_pass(dy_ref, *sems2, DIAGONAL)
+    slot_go(3, 3)
+    gather_wait(dy_ref, *sems2, FROM_SIBLING)
+
+    for p in range(ranks // 2):
+        @pl.when(rank == 0)
+        def _():
+            q_local(p).wait()
+
+        @pl.when(rank != 0)
+        def _():
+            q_copy(0, p, 0).wait_recv()
+
+    for copy in small:
+        copy.wait_send()
+    gather_sent(xg, *sems)
+    gather_sent(dy_ref, *sems2)
+    own_block.wait()
+    for p in range(ranks // 2):
+        @pl.when(rank < 4)
+        def _():
+            for m in range(2):
+                @pl.when(2 * rank + m != rank)
+                def _():
+                    q_copy(m, p, 0).wait_send()
+
+        for which in range(2):
+            first = 4 + 2 * which
+
+            @pl.when((rank == first) | (rank == first + 1))
+            def _():
+                for m in range(4):
+                    @pl.when(4 * (rank - first) + m != rank)
+                    def _():
+                        kv_copy(m, which, p, 0).wait_send()
+
+            for j in range(planes - 1):
+                for side in range(2):
+                    @pl.when(line_sends(planes, plane, j, side))
+                    def _():
+                        line_piece(0, which, p, side, j, next_of(side)).wait_send()
+
+
+def front(lengths, x, small, w_qkv, w_head_gate, grad, collective_id):
+    rows, width = x.shape
+    ranks, planes = lax.axis_size("fsdp"), lax.axis_size("sp")
+    tokens = ranks * rows
+    heads = w_head_gate.shape[0]
+    vmem = pl.BlockSpec(memory_space=pltpu.VMEM)
+    hbm = pl.BlockSpec(memory_space=pl.ANY)
+    half, full = jnp.bfloat16, jnp.float32
+    pairs = ranks // 2
+    return pl.pallas_call(
+        functools.partial(front_kernel, planes),
+        out_shape=(
+            jax.ShapeDtypeStruct((2, tokens, HEAD_DIM), half),
+            jax.ShapeDtypeStruct((planes, 2, tokens, HEAD_DIM), half),
+            jax.ShapeDtypeStruct((ranks, rows, width), half),
+            jax.ShapeDtypeStruct((ranks, rows, width), half),
+            jax.ShapeDtypeStruct((ranks, rows, width), half),
+            jax.ShapeDtypeStruct((tokens, w_qkv.shape[0]), full),
+            jax.ShapeDtypeStruct((heads, tokens, 1), full),
+            jax.ShapeDtypeStruct((1, width), full),
+            jax.ShapeDtypeStruct((1, width), full),
+            jax.ShapeDtypeStruct((1, HEAD_DIM), full),
+            jax.ShapeDtypeStruct((tokens, HEAD_DIM), full),
+            jax.ShapeDtypeStruct((tokens, HEAD_DIM), full),
+        ),
+        in_specs=[pl.BlockSpec(memory_space=pltpu.SMEM), vmem, vmem, vmem, vmem, hbm],
+        out_specs=(hbm, hbm, hbm) + (vmem,) * 9,
+        scratch_shapes=[
+            pltpu.VMEM((4, tokens, HEAD_DIM), half),
+            pltpu.VMEM((ranks,) + small.shape, small.dtype),
+            pltpu.SemaphoreType.DMA((ranks - 1,)),
+            pltpu.SemaphoreType.DMA((ranks - 1,)),
+            pltpu.SemaphoreType.DMA((2, GATHER_COPIES)),
+            pltpu.SemaphoreType.DMA((2, GATHER_COPIES)),
+            pltpu.SemaphoreType.DMA,
+            pltpu.SemaphoreType.DMA((pairs,)),
+            pltpu.SemaphoreType.DMA((2, pairs)),
+            pltpu.SemaphoreType.DMA((pairs,)),
+            pltpu.SemaphoreType.DMA((4, pairs)),
+            pltpu.SemaphoreType.DMA((2, pairs)),
+            pltpu.SemaphoreType.DMA((2, planes - 1, 2, pairs)),
+            pltpu.SemaphoreType.DMA((2, planes - 1, 2, pairs)),
+        ],
+        compiler_params=pltpu.CompilerParams(
+            collective_id=collective_id, has_side_effects=True, vmem_limit_bytes=VMEM_LIMIT
+        ),
+        name="front",
+    )(lengths, x, small, w_qkv, w_head_gate, grad)
 
 
 def local_planes(
@@ -1734,108 +2032,99 @@
     own_heads = w_qkv.shape[0] // HEAD_DIM
     local_heads = HEADS // ranks
 
-    wide, thin = attn_gain.shape[0], q_gain.shape[0]
-    used = 2 * wide + 2 * thin
+    thin = q_gain.shape[0]
+    spread = jnp.zeros((2, HEAD_DIM), attn_gain.dtype)
+    spread = lax.dynamic_update_slice(
+        spread, jnp.stack([q_gain, k_gain]), (jnp.int32(0), rank * thin)
+    )
     own_gains = jnp.concatenate(
-        [attn_gain, ffn_gain, q_gain, k_gain, jnp.zeros((8 * HEAD_DIM - used,), attn_gain.dtype)]
+        [
+            attn_gain.reshape(-1, HEAD_DIM),
+            ffn_gain.reshape(-1, HEAD_DIM),
+            spread,
+            jnp.zeros((2, HEAD_DIM), attn_gain.dtype),
+        ],
+        axis=0,
     ).astype(jnp.float32)
-    gathered, gains = gather_plane(hidden_in, 0, own_gains.reshape(8, HEAD_DIM))
-    gains = gains.reshape(ranks, 8 * HEAD_DIM)
-    attn_scale = gains[:, :wide].reshape(-1)
-    ffn_scale = gains[:, wide : 2 * wide].reshape(-1)
-    query_scale = gains[:, 2 * wide : 2 * wide + thin].reshape(-1)
-    key_scale = gains[:, 2 * wide + thin : used].reshape(-1)
-
-    token_block = jnp.arange(ranks, dtype=jnp.int32) * (planes * rows) + plane * rows
-    plane_tokens = (token_block[:, None] + jnp.arange(rows, dtype=jnp.int32)[None]).reshape(-1)
-    cosine, sine = rope_tables(plane_tokens - item_starts(plane_tokens, lengths))
-
-    inputs = gathered.reshape(tokens, model_width).astype(jnp.float32)
-    inv_first = inv_rms(inputs)
-    normed_a = (inputs * inv_first * attn_scale).astype(jnp.bfloat16)
-    projected = mat_nt(normed_a, w_qkv)
-    gate_logit = mat_nt(w_head_gate, normed_a)[:, :, None]
-    raw = projected.reshape(tokens, own_heads, HEAD_DIM)
-    raw_inv = inv_rms(raw)
-    is_query, is_value = rank < ranks // 2, rank >= 3 * ranks // 4
-    head_scale = jnp.where(is_query, query_scale, key_scale)
-    turned = rotate(raw * raw_inv * head_scale, cosine, sine)
-    natural = jnp.where(is_value, raw, turned).astype(jnp.bfloat16)
-    query, kv, plane_grad = exchange_heads(jnp.transpose(natural, (1, 0, 2)), grad_out, 1)
-
+    (
+        query,
+        kv,
+        plane_grad,
+        gathered,
+        normed_a,
+        projected,
+        gate_logit,
+        attn_scale,
+        ffn_scale,
+        head_scale,
+        cosine,
+        sine,
+    ) = front(lengths, hidden_in, own_gains, w_qkv, w_head_gate, grad_out, 0)
     attended, total, gated = attend(lengths, query, kv, gate_logit, rows)
-    own_inputs = hidden_in.astype(jnp.float32)
-    plane_b, line_b, line_grad, down_part, middle, grad_middle, grad_ffn_gain_local, plane_mid, grad_gated = middle_layer(
+    plane_b, line_blocks, down_part, middle, grad_middle, grad_ffn_gain_local, plane_mid, grad_gated, acts = middle_layer(
         gated.reshape(ranks, rows, -1),
         w_out,
         hidden_in,
-        ffn_scale.reshape(1, -1),
+        ffn_scale,
         plane_grad,
         w_gate,
         w_up,
         w_down,
         2,
     )
-    plane_mid = plane_mid.reshape(tokens, model_width)
     grad_gated = grad_gated.reshape(tokens, -1)
     grad_query, grad_kv, gate_grad = attend_back(
         lengths, query, kv, gate_logit, attended, total, grad_gated, rows
     )
-    back, other_grad = return_heads(grad_query, grad_kv, line_grad, 6)
-    back = jnp.transpose(back, (1, 0, 2))
-    turned_back = rotate_back(back.astype(jnp.float32), cosine, sine)
-    gain_terms = jnp.sum(turned_back * raw * raw_inv, axis=(0, 1))
-    raw_back = norm_back(turned_back, raw, raw_inv, head_scale).astype(jnp.bfloat16)
-    grad_proj = jnp.where(is_value, back, raw_back).reshape(tokens, own_heads * HEAD_DIM)
-    gate_grad = gate_grad.reshape(local_heads, tokens)
-    grad_a_part = jnp.dot(grad_proj, w_qkv, preferred_element_type=jnp.float32) + mat_tn(
-        gate_grad, w_head_gate
-    )
-    nothing = jnp.zeros((HEAD_DIM,), jnp.float32)
-    gain_parts = jnp.concatenate(
-        [
-            jnp.sum(grad_a_part * inputs * inv_first, axis=0).reshape(ranks, wide),
-            grad_ffn_gain_local.reshape(ranks, wide),
-            jnp.where(is_query, gain_terms, nothing).reshape(ranks, thin),
-            jnp.where(is_query | is_value, nothing, gain_terms).reshape(ranks, thin),
-            jnp.zeros((ranks, 8 * HEAD_DIM - used), jnp.float32),
-        ],
-        axis=1,
-    )
-    ffn_out = lax.psum_scatter(
-        down_part.reshape(tokens, model_width), "fsdp", scatter_dimension=0, tiled=True
-    )
-    hidden_out = (middle + ffn_out.astype(jnp.float32)).astype(jnp.bfloat16)
-    gate_rows_part = jnp.dot(gate_grad, normed_a, preferred_element_type=jnp.float32)
-    grad_a, gain_total, gate_total = scatter_plane(
-        grad_a_part.astype(jnp.bfloat16).reshape(ranks, rows, model_width),
+    back, first_plane = return_heads(grad_query, grad_kv, line_blocks, 6)
+    grad_a_part, pieces, gate_rows, attn_terms, head_terms = projection_back(
+        back,
+        projected,
+        cosine,
+        sine,
+        normed_a,
+        gathered,
+        gate_grad,
+        gated,
+        plane_mid,
+        w_qkv,
+        w_head_gate,
+        head_scale,
+    )
+    reduced = lax.psum_scatter(pieces, "sp", scatter_dimension=0, tiled=True)
+    complete = lax.all_gather(reduced, "sp", axis=0, tiled=True).astype(jnp.float32)
+    grad_w_out, grad_w_qkv = complete[: w_out.shape[0]], complete[w_out.shape[0] :]
+    grad_in, gain_sums, second_grad = scatter_gains(
+        grad_a_part,
+        attn_terms,
+        grad_ffn_gain_local,
+        head_terms,
+        hidden_in,
+        attn_scale,
+        grad_middle,
+        line_blocks,
         7,
-        gain_parts.reshape(ranks, 8, HEAD_DIM),
-        gate_rows_part.reshape(-1, HEAD_DIM),
-    )
-    own_inv = inv_rms(own_inputs)
-    grad_in = grad_middle + norm_back(grad_a, own_inputs, own_inv, attn_scale)
-
-    def over_planes(part):
-        reduced = lax.psum_scatter(
-            part.astype(jnp.bfloat16), "sp", scatter_dimension=0, tiled=True
-        )
-        return lax.all_gather(reduced, "sp", axis=0, tiled=True).astype(jnp.float32)
-
-    grad_w_out = over_planes(mat_tn(gated, plane_mid))
-    grad_w_qkv = over_planes(mat_tn(grad_proj, normed_a))
-    grad_w_head_gate = gate_total.reshape(w_head_gate.shape)
-
-    line_b, grad_a = lax.optimization_barrier((line_b, grad_a))
-    grad_w_gate, grad_w_up, grad_w_down = feed_weights(
-        plane_b, plane_grad, line_b, other_grad, w_gate, w_up, w_down, 4
-    )
-
-    gain_total = gain_total.reshape(-1)
-    grad_attn_gain = gain_total[:wide]
-    grad_ffn_gain = gain_total[wide : 2 * wide]
-    grad_q_gain = gain_total[2 * wide : 2 * wide + thin]
-    grad_k_gain = gain_total[2 * wide + thin : used]
+    )
+    grad_w_gate, grad_w_up, grad_w_down, hidden_out, gain_total, grad_w_head_gate = feed_weights(
+        plane_b,
+        plane_grad,
+        acts,
+        line_blocks,
+        first_plane,
+        second_grad,
+        down_part,
+        middle,
+        gain_sums,
+        gate_rows,
+        w_gate,
+        w_up,
+        w_down,
+        4,
+    )
+    grad_attn_gain = gain_total[:2].reshape(-1)
+    grad_ffn_gain = gain_total[2:4].reshape(-1)
+    grad_q_gain = lax.dynamic_slice_in_dim(gain_total[4], rank * thin, thin)
+    grad_k_gain = lax.dynamic_slice_in_dim(gain_total[5], rank * thin, thin)
     return (
         hidden_out,
         grad_in,

time: 605 us -> 537 us (0.89)
  other arithmetic: 34.8 us -> 1.96 us
  matrix products: 24.7 us -> 0 us
  Pallas kernels: 487 us -> 466 us
  waiting for transfers between devices: 7.29 us -> 21.5 us
  local copies, waits for them, and re-layouts: 27.9 us -> 21.6 us
    dot_general x7 -> x0, matrix products: 24.7 us -> none  [the longest x3 14.5 us: mat_tn(): lax.dot_general(factor, others, (((0,), (0,)), ((), ())), preferred_eleme...]
    reduce_scatter x3 -> x1, waiting for transfers between devices: 0.04 us -> 21.4 us  [local_planes(): reduced = lax.psum_scatter(pieces, 'sp', scatter_dimension=0, tiled=True)]
    pallas_call x1, Pallas kernels: 76.5 us -> 55.5 us  [return_heads(): pl.pallas_call(functools.partial(unheads_kernel, planes), out_shape=(jax....]
    convert_element_type x8 -> x1, other arithmetic: 15.4 us -> 1.28 us  [local_planes(): own_gains = jnp.concatenate([attn_gain.reshape(-1, HEAD_DIM), ffn_gain.re...]
    pallas_call x3, Pallas kernels: 137 us -> 148 us  [the longest x1 68.5 us: front(): pl.pallas_call(functools.partial(front_kernel, planes), out_shape=(jax.Sh...]
    unnamed x54 -> x26, local copies, waits for them, and re-layouts: 16.3 us -> 13.1 us
  transfers between devices with their start and end apart: 5 -> 2, of which waited for: 1 -> 1; matrix products, arithmetic and copies ran while one was open for 6% -> 1% of each run, Pallas kernels for 47% -> 35%
where the time goes in v3:
time: 537 us; the launch traced here: 526 us
  Pallas kernels  466 us (87%)
  local copies, waits for them, and re-layouts  21.6 us (4%)
  waiting for transfers between devices  21.5 us (4%)
  between operations  14.3 us (3%)
    pallas_call x1, Pallas kernels, feed_weights(): pl.pallas_call(functools.partial(feed_weights_kernel, planes), in_specs=[...  121 us
    pallas_call x1, Pallas kernels, middle_layer(): pl.pallas_call(functools.partial(middle_kernel, planes), out_shape=(jax.S...  111 us
    pallas_call x1, Pallas kernels, front(): pl.pallas_call(functools.partial(front_kernel, planes), out_shape=(jax.Sh...  68.5 us
    pallas_call x1, Pallas kernels, scatter_gains(): pl.pallas_call(scatter_gains_kernel, out_shape=(jax.ShapeDtypeStruct((row...  60.7 us
    pallas_call x1, Pallas kernels, return_heads(): pl.pallas_call(functools.partial(unheads_kernel, planes), out_shape=(jax....  55.5 us
    reduce_scatter x1, waiting for transfers between devices, local_planes(): reduced = lax.psum_scatter(pieces, 'sp', scatter_dimension=0, tiled=True)  21.4 us
    pallas_call x1, Pallas kernels, attend_back(): pl.pallas_call(functools.partial(attend_back_kernel, ranks, planes), grid...  18.6 us
    pallas_call x1, Pallas kernels, projection_back(): pl.pallas_call(projection_back_kernel, grid=(tokens // pair,), in_specs=[...  18.5 us
  transfers between devices with their start and end apart: 2, of which 1 were waited for; matrix products, arithmetic and copies ran while one was open for 1% of the time, Pallas kernels for 35%

profile of v3, /device:TPU:1, one launch (start us, length us, event | category | flops | bytes accessed | tf_op | source)
XLA Modules:
  0.0 525.8 jit_solution(3446060575533365967)
XLA Ops:
  7.2 0.7 pad_maximum_fusion
  8.2 1.3 maximum_convert_fusion.small_ref
  9.5 68.5 %front.1 = (bf16[2,1024,128]{2,1,0:T(8,128)(2,1)}, bf16[4,2,1024,128]{3,2,1,0:T(8,128)(2,1)}, bf16[8,128,2048]{2,1,0:T(8,128)(2,1)}, bf16[8,128,2048]{2,1,0:T(8,...) custom-call(s32[5]{0:T(128)} %lengths_ref.5, ...), custom_call_target="tpu_custom_call" | custom-call | tf_op jit(solution)/shard_map/front/pallas_call | solution.py:1972
  77.9 12.7 %attend.1 = (f32[2,1024,128]{2,1,0:T(8,128)}, f32[2,1024,1]{2,1,0:T(8,128)}, bf16[1024,256]{1,0:T(8,128)(2,1)}) custom-call(s32[5]{0:T(128)} %lengths_ref.5, bf16[2,1024,128]{2,1,0:T(8,128)(2,1)} %get-tuple-element.55.q_ref, bf16[4,2,8,128,128]{4,3,2,1,0:T(8,128)(2,1)} %bitcast.16, f32[2,1024,1]{2,1,0:T(8,128)} %get-tuple-element.57.gate_ref), custom_call_target="tpu_custom_call" | custom-call | tf_op jit(solution)/shard_map/attend/pallas_call | solution.py:1014
  90.6 111.0 %middle_layer.1 = (bf16[8,128,2048]{2,1,0:T(8,128)(2,1)}, bf16[2,3,128,2048]{3,2,1,0:T(8,128)(2,1)}, bf16[8,128,2048]{2,1,0:T(8,128)(2,1)}, f32[128,2048]{1,0:T(...) custom-call(bf16[8,128,256]{2,1,0:T(8,128)(2,1)} %bitcast.24, ...), custom_call_target="tpu_custom_call" | custom-call | tf_op jit(solution)/shard_map/middle_layer/pallas_call | solution.py:1375
  201.6 18.6 %attend_back.1 = (bf16[2,1024,128]{2,1,0:T(8,128)(2,1)}, bf16[4,2,8,128,128]{4,3,2,1,0:T(8,128)(2,1)}, bf16[2,1024,1]{2,1,0:T(8,128)(2,1)}) custom-call(s32[5]{0:T(128)} %lengths_ref.5, bf16[2,1024,128]{2,1,0:T(8,128)(2,1)} %get-tuple-element.55.q_ref, bf16[4,2,8,128,128]{4,3,2,1,0:T(8,128)(2,1)} %bitcast.17, f32[2,1024,1]{2,1,0:T(8,128)} %get-tuple-element.57.gate_ref, ...), custom_call_target="tpu_custom_call" | custom-call | tf_op jit(solution)/shard_map/attend_back/pallas_call | solution.py:1103
  220.2 55.5 %return_heads.1 = (bf16[4,1024,128]{2,1,0:T(8,128)(2,1)}, bf16[2,8,128,2048]{3,2,1,0:T(8,128)(2,1)}) custom-call(bf16[2,1024,128]{2,1,0:T(8,128)(2,1)} %get-tuple-element.67.dq_ref, bf16[4,2,1024,128]{3,2,1,0:T(8,128)(2,1)} %bitcast.25, bf16[2,3,128,2048]{3,2,1,0:T(8,128)(2,1)} %get-tuple-element.63.blocks_ref.blocks_hbm), custom_call_target="tpu_custom_call" | custom-call | tf_op jit(solution)/shard_map/return_heads/pallas_call | solution.py:904
  275.8 18.5 %projection_back.1 = (bf16[8,128,2048]{2,1,0:T(8,128)(2,1)}, bf16[768,2048]{1,0:T(8,128)(2,1)}, f32[2,2048]{1,0:T(2,128)}, f32[1,2048]{1,0:T(1,128)}, f32[1,128]{1,0:T(1,128)}) custom-call(bf16[4,1024,128]{2,1,0:T(8,128)(2,1)} %get-tuple-element.70.back_ref, f32[1024,512]{1,0:T(8,128)} %get-tuple-element.71.raw_ref, f32[1024,128]{1,0:T(8,128)} %get-tuple-element.72.cos_ref, ...), custom_call_target="tpu_custom_call" | custom-call | tf_op jit(solution)/shard_map/projection_back/pallas_call | solution.py:628
  294.3 60.7 %scatter_gains.1 = (f32[128,2048]{1,0:T(8,128)}, f32[8,128]{1,0:T(8,128)}, bf16[8,128,2048]{2,1,0:T(8,128)(2,1)}) custom-call(bf16[8,128,2048]{2,1,0:T(8,128)(2,1)} %get-tuple-element.79.p_ref, f32[1,2048]{1,0:T(1,128)} %get-tuple-element.80.attn_ref, f32[1,2048]{1,0:T(1,128)} %get-tuple-element.81.ffn_ref, f32[1,128]{1,0:T(1,128)} %get-tuple-element.82.head_ref, ...), custom_call_target="tpu_custom_call" | custom-call | tf_op jit(solution)/shard_map/scatter_gains/pallas_call | solution.py:547
  355.1 21.4 %reduce-scatter.2.cloned.1.call-done = bf16[192,2048]{1,0:T(8,128)(2,1)} async-done(((bf16[768,2048]{1,0:T(8,128)(2,1)}), bf16[192,2048]{1,0:T(8,128)(2,1)}) %reduce-scatter.2.cloned.1.call-update) | async-done | bytes 786448 | tf_op jit(solution)/shard_map/reduce_scatter | solution.py:2094
  376.5 120.9 %feed_weights.1 = (f32[768,2048]{1,0:T(8,128)}, f32[768,2048]{1,0:T(8,128)}, f32[768,2048]{1,0:T(8,128)}, bf16[128,2048]{1,0:T(8,128)(2,1)}, f32[8,128]{1,0:T(8,...) custom-call(bf16[8,128,2048]{2,1,0:T(8,128)(2,1)} %get-tuple-element.61.xp_hbm, ...), custom_call_target="tpu_custom_call" | custom-call | flops 77309411328 | bytes 61865984 | tf_op jit(solution)/shard_map/feed_weights/pallas_call | solution.py:1646
  497.4 0.8 fusion
  498.2 0.6 dynamic-slice_bitcast_fusion
  498.8 1.3 slice_bitcast_fusion
  500.1 2.9 slice.25
  503.1 2.7 slice.24
  505.7 0.8 copy.32
  506.5 1.0 copy.33
  507.5 0.6 copy.34
  508.1 3.2 copy.35
  511.3 3.2 copy.36
  514.5 0.9 slice-done
  515.4 0.7 slice-done.1
  516.1 2.7 copy.37
  (29 shorter events, 0.4 us)
Async XLA Ops:
  7.2 369.3 %reduce-scatter.2.cloned.1.call-start = ((), (), s32[]{:S(2)}) async-start(), calls=%async_computation.1 | async-start | bytes 3932160 | tf_op jit(solution)/shard_map/reduce_scatter | solution.py:2094
  294.3 205.8 %all-gather.2.cloned.1.call-start = ((), (), s32[]{:S(2)}) async-start(), calls=%async_computation.2 | async-start | bytes 3932160 | tf_op jit(solution)/shard_map/all_gather | solution.py:2095
  500.1 2.9 copy-start
  500.1 8.0 %slice-start.4 = ((s8[6291456]{0:T(1024)(128)(4,1)}), s8[4194304]{0:T(1024)(128)(4,1)S(1)}, s32[]{:S(2)}) async-start(s8[6291456]{0:T(1024)(128)(4,1)} %bitcast.22), calls=%async_computation.7 | async-start | bytes 8388608
  503.0 2.7 copy-start.2
  503.0 3.5 copy-start.1
  503.0 4.5 copy-start.3
  503.0 5.1 slice-start.5
  505.7 5.6 %slice-start.2 = ((s8[6291456]{0:T(1024)(128)(4,1)}), s8[4194304]{0:T(1024)(128)(4,1)S(1)}, s32[]{:S(2)}) async-start(s8[6291456]{0:T(1024)(128)(4,1)} %bitcast.20), calls=%async_computation.5 | async-start | bytes 8388608
  508.1 3.2 slice-start.3
  508.1 7.3 %slice-start = ((s8[6291456]{0:T(1024)(128)(4,1)}), s8[4194304]{0:T(1024)(128)(4,1)S(1)}, s32[]{:S(2)}) async-start(s8[6291456]{0:T(1024)(128)(4,1)} %bitcast.18), calls=%async_computation.3 | async-start | bytes 8388608
  511.3 4.8 slice-start.1
Sparse Core Ops, SparseCore 0:
  294.4 82.0 reduce-scatter.1
  378.1 63.6 all-gather.1

commit v4 on v3

--- a/solution.py
+++ b/solution.py
@@ -427,14 +427,11 @@
 
 
 def scatter_gains_kernel(
-    p_ref, attn_ref, ffn_ref, head_ref, x_ref, scale_ref, dmid_ref, blocks_ref, o_ref, so_ref, next_ref, parts, small_buf, grad, small_send, small_recv, ag_send, ag_recv, own_sem, *rest
+    p_ref, attn_ref, ffn_ref, head_ref, x_ref, scale_ref, dmid_ref, o_ref, so_ref, parts, small_buf, grad, small_send, small_recv, *rest
 ):
     rank, plane = lax.axis_index("fsdp"), lax.axis_index("sp")
     ranks = p_ref.shape[0]
     greet([(rank ^ k, plane) for k in range(1, 8)])
-    block = blocks_ref.at[1, 1]
-    own = pltpu.make_async_copy(block, next_ref.at[rank], own_sem)
-    own.start()
     for i in range(4):
         scatter_near(p_ref, i, rest[0], rest[3], rest[4]).start()
     for r in range(ranks):
@@ -460,20 +457,14 @@
         copy.start()
         small.append(copy)
     scatter_begin(p_ref, grad, *rest, started=True)
-    gather_start(next_ref, ag_send, ag_recv, own=block)
     total = parts[rank]
     for k in range(1, 8):
         small[k - 1].wait()
         total = total + small_buf[k - 1]
     so_ref[...] = total
-    gather_pass(next_ref, ag_send, ag_recv, NEIGHBOURS_FIRST)
     scatter_end(p_ref, grad, *rest)
-    gather_pass(next_ref, ag_send, ag_recv, DIAGONAL)
     inputs = x_ref[...].astype(jnp.float32)
     o_ref[...] = dmid_ref[...] + norm_back(grad[...], inputs, inv_rms(inputs), scale_ref[...])
-    gather_wait(next_ref, ag_send, ag_recv, FROM_SIBLING)
-    gather_sent(next_ref, ag_send, ag_recv)
-    own.wait()
 
 
 SCATTER_ORDER = (6, 2, 4, 0)
@@ -539,49 +530,57 @@
     ]
 
 
-def scatter_gains(p, attn, ffn, head, x, scale, grad_middle, blocks, collective_id):
+def scatter_gains(p, attn, ffn, head, x, scale, grad_middle, collective_id):
     ranks, rows, width = p.shape
     vmem = pl.BlockSpec(memory_space=pltpu.VMEM)
-    hbm = pl.BlockSpec(memory_space=pl.ANY)
     small = (8, HEAD_DIM)
     return pl.pallas_call(
         scatter_gains_kernel,
         out_shape=(
             jax.ShapeDtypeStruct((rows, width), jnp.float32),
             jax.ShapeDtypeStruct(small, jnp.float32),
-            jax.ShapeDtypeStruct(p.shape, blocks.dtype),
         ),
-        in_specs=[vmem] * 7 + [hbm],
-        out_specs=(vmem, vmem, hbm),
+        in_specs=[vmem] * 7,
+        out_specs=(vmem, vmem),
         scratch_shapes=[
             pltpu.VMEM((ranks,) + small, jnp.float32),
             pltpu.VMEM((7,) + small, jnp.float32),
             pltpu.VMEM((rows, width), jnp.float32),
             pltpu.SemaphoreType.DMA((7,)),
             pltpu.SemaphoreType.DMA((7,)),
-            pltpu.SemaphoreType.DMA((GATHER_COPIES,)),
-            pltpu.SemaphoreType.DMA((GATHER_COPIES,)),
-            pltpu.SemaphoreType.DMA,
         ]
         + scatter_scratch(rows, width, p.dtype),
         compiler_params=pltpu.CompilerParams(
             collective_id=collective_id, has_side_effects=True, vmem_limit_bytes=VMEM_LIMIT
         ),
         name="scatter_gains",
-    )(p, attn, ffn, head, x, scale, grad_middle, blocks)
+    )(p, attn, ffn, head, x, scale, grad_middle)
 
 
 def projection_back_kernel(
-    back_ref, raw_ref, cos_ref, sin_ref, xa_ref, x_ref, dgate_ref, gated_ref, pm_ref, w_ref, wg_ref, head_ref, dxa_ref, pieces_ref, gate_ref, attn_ref, terms_ref, sums
+    back_ref, raw_ref, cos_ref, sin_ref, xa_ref, x_ref, dgate_ref, w_ref, wg_ref, head_ref, blocks_ref, dxa_ref, qkv_ref, gate_ref, attn_ref, terms_ref, next_ref, sums, ag_send, ag_recv, own_sem
 ):
-    rank = lax.axis_index("fsdp")
+    rank, plane = lax.axis_index("fsdp"), lax.axis_index("sp")
+    block = blocks_ref.at[1, 1]
+    gather = (next_ref, ag_send, ag_recv)
+    own = pltpu.make_async_copy(block, next_ref.at[rank], own_sem)
     group, rows, width = back_ref.shape
-    out_rows = gated_ref.shape[1]
 
     @pl.when(pl.program_id(0) == 0)
     def _():
+        greet([(rank ^ k, plane) for k in (1, 2, 4)])
+        own.start()
+        gather_start(*gather, own=block)
         for ref in (sums, gate_ref, attn_ref, terms_ref):
             ref[...] = jnp.zeros_like(ref)
+
+    @pl.when(pl.program_id(0) == 2)
+    def _():
+        gather_pass(*gather, NEIGHBOURS_FIRST[:2])
+
+    @pl.when(pl.program_id(0) == 3)
+    def _():
+        gather_pass(*gather, NEIGHBOURS_FIRST[2:])
 
     cosine, sine = cos_ref[...], sin_ref[...]
     columns = []
@@ -605,26 +604,29 @@
     inputs = x_ref[...].reshape(rows, -1).astype(jnp.float32)
     attn_ref[...] += jnp.sum(grad_a * inputs * inv_rms(inputs), axis=0, keepdims=True)
     dxa_ref[...] = grad_a.astype(jnp.bfloat16).reshape(dxa_ref.shape)
-    sums[:out_rows] += mat_tn(gated_ref[...], pm_ref[...].reshape(rows, -1))
-    sums[out_rows:] += mat_tn(grad_proj, normed)
+    sums[...] += mat_tn(grad_proj, normed)
 
     @pl.when(pl.program_id(0) == pl.num_programs(0) - 1)
     def _():
-        pieces_ref[...] = sums[...].astype(jnp.bfloat16)
-
-
-def projection_back(back, raw, cosine, sine, normed, inputs, gate_grad, gated, plane_mid, w_qkv, w_head_gate, head_scale):
+        qkv_ref[...] = sums[...].astype(jnp.bfloat16)
+        gather_pass(*gather, DIAGONAL)
+        gather_wait(*gather, FROM_SIBLING)
+        gather_sent(*gather)
+        own.wait()
+
+
+def projection_back(back, raw, cosine, sine, normed, inputs, gate_grad, w_qkv, w_head_gate, head_scale, line_blocks, collective_id):
     ranks, rows, model_width = normed.shape
     group, tokens, width = back.shape
     pair = 2 * rows
     blocks = pl.BlockSpec((2, rows, model_width), lambda i: (i, 0, 0))
     thin = pl.BlockSpec((pair, width), lambda i: (i, 0))
-    heads, out_rows = gate_grad.shape[0], gated.shape[1]
+    hbm = pl.BlockSpec(memory_space=pl.ANY)
+    heads = gate_grad.shape[0]
 
     def still(shape):
         return pl.BlockSpec(shape, lambda i: (0, 0))
 
-    total = (out_rows + w_qkv.shape[0], model_width)
     return pl.pallas_call(
         projection_back_kernel,
         grid=(tokens // pair,),
@@ -636,30 +638,38 @@
             blocks,
             blocks,
             pl.BlockSpec((heads, pair, 1), lambda i: (0, i, 0)),
-            pl.BlockSpec((pair, out_rows), lambda i: (i, 0)),
+            still(w_qkv.shape),
+            still(w_head_gate.shape),
+            still(head_scale.shape),
+            hbm,
+        ],
+        out_specs=(
             blocks,
             still(w_qkv.shape),
             still(w_head_gate.shape),
-            still(head_scale.shape),
-        ],
-        out_specs=(
-            blocks,
-            still(total),
-            still(w_head_gate.shape),
             still((1, model_width)),
             still((1, width)),
+            hbm,
         ),
         out_shape=(
             jax.ShapeDtypeStruct(normed.shape, jnp.bfloat16),
-            jax.ShapeDtypeStruct(total, jnp.bfloat16),
+            jax.ShapeDtypeStruct(w_qkv.shape, jnp.bfloat16),
             jax.ShapeDtypeStruct(w_head_gate.shape, jnp.float32),
             jax.ShapeDtypeStruct((1, model_width), jnp.float32),
             jax.ShapeDtypeStruct((1, width), jnp.float32),
+            jax.ShapeDtypeStruct(normed.shape, line_blocks.dtype),
         ),
-        scratch_shapes=[pltpu.VMEM(total, jnp.float32)],
-        compiler_params=pltpu.CompilerParams(vmem_limit_bytes=VMEM_LIMIT),
+        scratch_shapes=[
+            pltpu.VMEM(w_qkv.shape, jnp.float32),
+            pltpu.SemaphoreType.DMA((GATHER_COPIES,)),
+            pltpu.SemaphoreType.DMA((GATHER_COPIES,)),
+            pltpu.SemaphoreType.DMA,
+        ],
+        compiler_params=pltpu.CompilerParams(
+            collective_id=collective_id, has_side_effects=True, vmem_limit_bytes=VMEM_LIMIT
+        ),
         name="projection_back",
-    )(back, raw, cosine, sine, normed, inputs, gate_grad, gated, plane_mid, w_qkv, w_head_gate, head_scale)
+    )(back, raw, cosine, sine, normed, inputs, gate_grad, w_qkv, w_head_gate, head_scale, line_blocks)
 
 
 GATHER_COPIES = 13
@@ -792,6 +802,9 @@
     def target(j, side):
         return planes - 1 - j if side == 0 else j
 
+    for which in range(2):
+        gather_start(*gathers[which], own=blocks_ref.at[which, 0])
+
     for j in range(planes - 1):
         for which in range(2):
             for side in range(2):
@@ -813,12 +826,11 @@
                 def _():
                     step_copy(j, which, side).start()
 
-        if j == 0:
-            gather_start(*gathers[0], own=blocks_ref.at[0, 0])
-            gather_start(*gathers[1], own=blocks_ref.at[1, 0])
+        if j == 1:
+            gather_pass(*gathers[0], NEIGHBOURS_FIRST)
         if j == 2:
-            gather_pass(*gathers[0], NEIGHBOURS_FIRST)
             gather_pass(*gathers[1], NEIGHBOURS_FIRST)
+            gather_pass(*gathers[0], DIAGONAL)
 
     for which in range(2):
         total = dkv_ref[plane, which].astype(jnp.float32)
@@ -845,8 +857,7 @@
             def _():
                 kv_local(m, which).start()
 
-    for gather in gathers:
-        gather_pass(*gather, DIAGONAL)
+    gather_pass(*gathers[1], DIAGONAL)
     for gather in gathers:
         gather_wait(*gather, FROM_SIBLING)
         gather_sent(*gather)
@@ -1430,6 +1441,7 @@
     mid_ref,
     small_ref,
     rows_ref,
+    qkv_hbm,
     wg_ref,
     wu_ref,
     wd_ref,
@@ -1439,6 +1451,7 @@
     h_ref,
     so_ref,
     go_ref,
+    sum_hbm,
     more_hbm,
     xbuf,
     dbuf,
@@ -1446,6 +1459,8 @@
     parts,
     small_buf,
     rows_buf,
+    quarter,
+    quarters,
     x_sem,
     d_sem,
     act_sem,
@@ -1455,6 +1470,11 @@
     ag_recv,
     line_send,
     line_recv,
+    part_send,
+    part_recv,
+    sum_send,
+    sum_recv,
+    quarter_sem,
     near_buf,
     out_buf,
     far_buf,
@@ -1524,8 +1544,39 @@
         for k in range(planes - 1)
     ]
 
+    quarter_rows = quarter.shape[0]
+
+    def rows_of(index):
+        return pl.ds(pl.multiple_of(index * quarter_rows, quarter_rows), quarter_rows)
+
+    own_quarter = pltpu.make_async_copy(qkv_hbm.at[rows_of(plane)], quarter, quarter_sem.at[0])
+    own_sum = pltpu.make_async_copy(quarter, sum_hbm.at[rows_of(plane)], quarter_sem.at[1])
+    partials = [
+        peer_copy(
+            qkv_hbm.at[rows_of(others[k])],
+            quarters.at[k],
+            part_send.at[k],
+            part_recv.at[k],
+            rank,
+            others[k],
+        )
+        for k in range(planes - 1)
+    ]
+    sums = [
+        peer_copy(
+            quarter,
+            sum_hbm.at[rows_of(plane)],
+            sum_send.at[k],
+            sum_recv.at[k],
+            rank,
+            others[k],
+        )
+        for k in range(planes - 1)
+    ]
+
     load(0, True)
-    for copy in own_blocks + small + own_parts:
+    own_quarter.start()
+    for copy in own_blocks + small + own_parts + partials:
         copy.start()
     begin(0)
     for i in range(4):
@@ -1563,6 +1614,15 @@
             own_blocks[0].wait()
             load(step, True)
             gather_pass(*gathers[1], DIAGONAL)
+            own_quarter.wait()
+            total = quarter[...].astype(jnp.float32)
+            for k in range(planes - 1):
+                partials[k].wait()
+                total = total + quarters[k].astype(jnp.float32)
+            quarter[...] = total.astype(quarter.dtype)
+            own_sum.start()
+            for copy in sums:
+                copy.start()
 
         @pl.when(step == 5)
         def _():
@@ -1621,8 +1681,9 @@
         scatter_far(i, out_buf, far_buf, send_sem, recv_sem).wait()
         output = output + far_buf[i].astype(jnp.float32)
     h_ref[...] = output.astype(h_ref.dtype)
-    for copy in small:
+    for copy in small + sums:
         copy.wait()
+    own_sum.wait()
     total, gate_rows = small_ref[...], rows_ref[...]
     for k in range(planes - 1):
         total = total + small_buf[k]
@@ -1635,7 +1696,7 @@
         gather_sent(*gather)
 
 
-def feed_weights(plane_x, plane_grad, acts, blocks, first, second, down, middle, small, gate_rows, w_gate, w_up, w_down, collective_id):
+def feed_weights(plane_x, plane_grad, acts, blocks, first, second, down, middle, small, gate_rows, qkv_part, w_gate, w_up, w_down, collective_id):
     ranks, rows, width = plane_x.shape
     planes = lax.axis_size("sp")
     hidden = w_gate.shape[0]
@@ -1645,13 +1706,14 @@
     half, full = plane_x.dtype, jnp.float32
     return pl.pallas_call(
         functools.partial(feed_weights_kernel, planes),
-        in_specs=[hbm] * 7 + [vmem] * 6,
-        out_specs=(vmem,) * 6 + (hbm,),
+        in_specs=[hbm] * 7 + [vmem] * 3 + [hbm] + [vmem] * 3,
+        out_specs=(vmem,) * 6 + (hbm, hbm),
         out_shape=[jax.ShapeDtypeStruct(w_gate.shape, full)] * 3
         + [
             jax.ShapeDtypeStruct((rows, width), half),
             jax.ShapeDtypeStruct(small.shape, full),
             jax.ShapeDtypeStruct(gate_rows.shape, full),
+            jax.ShapeDtypeStruct(qkv_part.shape, half),
             jax.ShapeDtypeStruct((3, ranks, rows, width), half),
         ],
         scratch_shapes=[
@@ -1661,6 +1723,8 @@
             pltpu.VMEM((4, rows, width), half),
             pltpu.VMEM((planes - 1,) + small.shape, full),
             pltpu.VMEM((planes - 1,) + gate_rows.shape, full),
+            pltpu.VMEM((qkv_part.shape[0] // planes, width), half),
+            pltpu.VMEM((planes - 1, qkv_part.shape[0] // planes, width), half),
             pltpu.SemaphoreType.DMA((2,)),
             pltpu.SemaphoreType.DMA((2,)),
             pltpu.SemaphoreType.DMA,
@@ -1670,6 +1734,10 @@
             pltpu.SemaphoreType.DMA((3, GATHER_COPIES)),
             pltpu.SemaphoreType.DMA((2, planes - 1)),
             pltpu.SemaphoreType.DMA((2, planes - 1)),
+        ]
+        + [pltpu.SemaphoreType.DMA((planes - 1,))] * 4
+        + [
+            pltpu.SemaphoreType.DMA((2,)),
         ]
         + scatter_scratch(rows, width, half),
         cost_estimate=pl.CostEstimate(
@@ -1681,7 +1749,7 @@
             collective_id=collective_id, has_side_effects=True, vmem_limit_bytes=VMEM_LIMIT
         ),
         name="feed_weights",
-    )(plane_x, plane_grad, acts, blocks, first, second, down, middle, small, gate_rows, w_gate, w_up, w_down)[:6]
+    )(plane_x, plane_grad, acts, blocks, first, second, down, middle, small, gate_rows, qkv_part, w_gate, w_up, w_down)[:7]
 
 
 def front_kernel(
@@ -2073,11 +2141,13 @@
         2,
     )
     grad_gated = grad_gated.reshape(tokens, -1)
+    out_part = mat_tn(gated, plane_mid.reshape(tokens, model_width)).astype(jnp.bfloat16)
+    reduced = lax.psum_scatter(out_part, "sp", scatter_dimension=0, tiled=True)
     grad_query, grad_kv, gate_grad = attend_back(
         lengths, query, kv, gate_logit, attended, total, grad_gated, rows
     )
     back, first_plane = return_heads(grad_query, grad_kv, line_blocks, 6)
-    grad_a_part, pieces, gate_rows, attn_terms, head_terms = projection_back(
+    grad_a_part, qkv_part, gate_rows, attn_terms, head_terms, second_grad = projection_back(
         back,
         projected,
         cosine,
@@ -2085,16 +2155,15 @@
         normed_a,
         gathered,
         gate_grad,
-        gated,
-        plane_mid,
         w_qkv,
         w_head_gate,
         head_scale,
-    )
-    reduced = lax.psum_scatter(pieces, "sp", scatter_dimension=0, tiled=True)
-    complete = lax.all_gather(reduced, "sp", axis=0, tiled=True).astype(jnp.float32)
-    grad_w_out, grad_w_qkv = complete[: w_out.shape[0]], complete[w_out.shape[0] :]
-    grad_in, gain_sums, second_grad = scatter_gains(
+        line_blocks,
+        8,
+    )
+    reduced, grad_a_part = lax.optimization_barrier((reduced, grad_a_part))
+    out_sum = lax.all_gather(reduced, "sp", axis=0, tiled=True)
+    grad_in, gain_sums = scatter_gains(
         grad_a_part,
         attn_terms,
         grad_ffn_gain_local,
@@ -2102,10 +2171,11 @@
         hidden_in,
         attn_scale,
         grad_middle,
-        line_blocks,
         7,
     )
-    grad_w_gate, grad_w_up, grad_w_down, hidden_out, gain_total, grad_w_head_gate = feed_weights(
+    out_sum, gain_sums = lax.optimization_barrier((out_sum, gain_sums))
+    grad_w_out = out_sum.astype(jnp.float32)
+    grad_w_gate, grad_w_up, grad_w_down, hidden_out, gain_total, grad_w_head_gate, qkv_total = feed_weights(
         plane_b,
         plane_grad,
         acts,
@@ -2116,11 +2186,13 @@
         middle,
         gain_sums,
         gate_rows,
+        qkv_part,
         w_gate,
         w_up,
         w_down,
         4,
     )
+    grad_w_qkv = qkv_total.astype(jnp.float32)
     grad_attn_gain = gain_total[:2].reshape(-1)
     grad_ffn_gain = gain_total[2:4].reshape(-1)
     grad_q_gain = lax.dynamic_slice_in_dim(gain_total[4], rank * thin, thin)

time: 537 us -> 507 us (0.944)
  waiting for transfers between devices: 21.5 us -> 0.08 us
  Pallas kernels: 466 us -> 458 us
  local copies, waits for them, and re-layouts: 21.6 us -> 16.1 us
    pallas_call x1, Pallas kernels: 60.7 us -> 32.8 us  [scatter_gains(): pl.pallas_call(scatter_gains_kernel, out_shape=(jax.ShapeDtypeStruct((row...]
    reduce_scatter x1, waiting for transfers between devices: 21.4 us -> 0.02 us  [local_planes(): reduced = lax.psum_scatter(out_part, 'sp', scatter_dimension=0, tiled=True)]
    pallas_call x1, Pallas kernels: 18.5 us -> 36 us  [projection_back(): pl.pallas_call(projection_back_kernel, grid=(tokens // pair,), in_specs=[...]
    slice x2 -> x0, local copies, waits for them, and re-layouts: 5.6 us -> none  [the longest x1 2.94 us: local_planes(): complete[:w_out.shape[0]]]
    unnamed x26 -> x30, local copies, waits for them, and re-layouts: 13.1 us -> 13.1 us
  transfers between devices with their start and end apart: 2 -> 2, of which waited for: 1 -> 0; matrix products, arithmetic and copies ran while one was open for 1% -> 0% of each run, Pallas kernels for 35% -> 29%
where the time goes in v4:
time: 507 us; the launch traced here: 499 us
  Pallas kernels  458 us (90%)
  local copies, waits for them, and re-layouts  16.1 us (3%)
  between operations  14.4 us (3%)
  other arithmetic  6.19 us (1%)
    pallas_call x1, Pallas kernels, feed_weights(): pl.pallas_call(functools.partial(feed_weights_kernel, planes), in_specs=[...  119 us
    pallas_call x1, Pallas kernels, middle_layer(): pl.pallas_call(functools.partial(middle_kernel, planes), out_shape=(jax.S...  111 us
    pallas_call x1, Pallas kernels, front(): pl.pallas_call(functools.partial(front_kernel, planes), out_shape=(jax.Sh...  68.4 us
    pallas_call x1, Pallas kernels, return_heads(): pl.pallas_call(functools.partial(unheads_kernel, planes), out_shape=(jax....  55.4 us
    pallas_call x1, Pallas kernels, projection_back(): pl.pallas_call(projection_back_kernel, grid=(tokens // pair,), in_specs=[...  36 us
    pallas_call x1, Pallas kernels, scatter_gains(): pl.pallas_call(scatter_gains_kernel, out_shape=(jax.ShapeDtypeStruct((row...  32.8 us
    pallas_call x1, Pallas kernels, attend_back(): pl.pallas_call(functools.partial(attend_back_kernel, ranks, planes), grid...  21.9 us
    pallas_call x1, Pallas kernels, attend(): pl.pallas_call(functools.partial(attend_kernel, ranks, planes), grid_spec...  14.2 us
  transfers between devices with their start and end apart: 2, of which 0 were waited for; matrix products, arithmetic and copies ran while one was open for 0% of the time, Pallas kernels for 29%

profile of v4, /device:TPU:1, one launch (start us, length us, event | category | flops | bytes accessed | tf_op | source)
XLA Modules:
  0.0 499.3 jit_solution(14145869936654130702)
XLA Ops:
  7.2 0.7 pad_maximum_fusion
  8.2 1.3 maximum_convert_fusion.small_ref
  9.5 68.4 %front.1 = (bf16[2,1024,128]{2,1,0:T(8,128)(2,1)}, bf16[4,2,1024,128]{3,2,1,0:T(8,128)(2,1)}, bf16[8,128,2048]{2,1,0:T(8,128)(2,1)}, bf16[8,128,2048]{2,1,0:T(8,...) custom-call(s32[5]{0:T(128)} %lengths_ref.5, ...), custom_call_target="tpu_custom_call" | custom-call | tf_op jit(solution)/shard_map/front/pallas_call | solution.py:2040
  77.8 14.2 %attend.1 = (f32[2,1024,128]{2,1,0:T(8,128)}, f32[2,1024,1]{2,1,0:T(8,128)}, bf16[1024,256]{1,0:T(8,128)(2,1)}) custom-call(s32[5]{0:T(128)} %lengths_ref.5, bf16[2,1024,128]{2,1,0:T(8,128)(2,1)} %get-tuple-element.60.q_ref, bf16[4,2,8,128,128]{4,3,2,1,0:T(8,128)(2,1)} %bitcast.19, f32[2,1024,1]{2,1,0:T(8,128)} %get-tuple-element.62.gate_ref), custom_call_target="tpu_custom_call" | custom-call | tf_op jit(solution)/shard_map/attend/pallas_call | solution.py:1025
  92.0 110.9 %middle_layer.1 = (bf16[8,128,2048]{2,1,0:T(8,128)(2,1)}, bf16[2,3,128,2048]{3,2,1,0:T(8,128)(2,1)}, bf16[8,128,2048]{2,1,0:T(8,128)(2,1)}, f32[128,2048]{1,0:T(...) custom-call(bf16[8,128,256]{2,1,0:T(8,128)(2,1)} %bitcast.29, ...), custom_call_target="tpu_custom_call" | custom-call | tf_op jit(solution)/shard_map/middle_layer/pallas_call | solution.py:1386
  202.9 4.4 convolution_convert_fusion
  207.4 21.9 %attend_back.1 = (bf16[2,1024,128]{2,1,0:T(8,128)(2,1)}, bf16[4,2,8,128,128]{4,3,2,1,0:T(8,128)(2,1)}, bf16[2,1024,1]{2,1,0:T(8,128)(2,1)}) custom-call(s32[5]{0:T(128)} %lengths_ref.5, bf16[2,1024,128]{2,1,0:T(8,128)(2,1)} %get-tuple-element.60.q_ref, bf16[4,2,8,128,128]{4,3,2,1,0:T(8,128)(2,1)} %bitcast.20, f32[2,1024,1]{2,1,0:T(8,128)} %get-tuple-element.62.gate_ref, ...), custom_call_target="tpu_custom_call" | custom-call | tf_op jit(solution)/shard_map/attend_back/pallas_call | solution.py:1114
  229.3 55.4 %return_heads.1 = (bf16[4,1024,128]{2,1,0:T(8,128)(2,1)}, bf16[2,8,128,2048]{3,2,1,0:T(8,128)(2,1)}) custom-call(bf16[2,1024,128]{2,1,0:T(8,128)(2,1)} %get-tuple-element.72.dq_ref, bf16[4,2,1024,128]{3,2,1,0:T(8,128)(2,1)} %bitcast.27, bf16[2,3,128,2048]{3,2,1,0:T(8,128)(2,1)} %get-tuple-element.68.blocks_ref.blocks_hbm), custom_call_target="tpu_custom_call" | custom-call | tf_op jit(solution)/shard_map/return_heads/pallas_call | solution.py:915
  284.8 36.0 %projection_back.1 = (bf16[8,128,2048]{2,1,0:T(8,128)(2,1)}, bf16[512,2048]{1,0:T(8,128)(2,1)}, f32[2,2048]{1,0:T(2,128)}, f32[1,2048]{1,0:T(1,128)}, f32[1,128]{1,0:T(1,128)}, /*index=5*/bf16[8,128,2048]{2,1,0:T(8,128)(2,1)}) custom-call(bf16[4,1024,128]{2,1,0:T(8,128)(2,1)} %get-tuple-element.75.back_ref, f32[1024,512]{1,0:T(8,128)} %get-tuple-element.76.raw_ref, ...), custom_call_target="tpu_custom_call" | custom-call | tf_op jit(solution)/shard_map/projection_back/pallas_call | solution.py:630
  320.8 32.8 %scatter_gains.1 = (f32[128,2048]{1,0:T(8,128)}, f32[8,128]{1,0:T(8,128)}) custom-call(bf16[8,128,2048]{2,1,0:T(8,128)(2,1)} %get-tuple-element.89.p_ref, f32[1,2048]{1,0:T(1,128)} %get-tuple-element.90.attn_ref, f32[1,2048]{1,0:T(1,128)} %get-tuple-element.91.ffn_ref, f32[1,128]{1,0:T(1,128)} %get-tuple-element.92.head_ref, bf16[128,2048]{1,0:T(8,128)(2,1)} %x_ref.5, ...), custom_call_target="tpu_custom_call" | custom-call | tf_op jit(solution)/shard_map/scatter_gains/pallas_call | solution.py:537
  353.7 118.5 %feed_weights.1 = (f32[768,2048]{1,0:T(8,128)}, f32[768,2048]{1,0:T(8,128)}, f32[768,2048]{1,0:T(8,128)}, bf16[128,2048]{1,0:T(8,128)(2,1)}, f32[8,128]{1,0:T(8,...) custom-call(bf16[8,128,2048]{2,1,0:T(8,128)(2,1)} %get-tuple-element.66.xp_hbm, ...), custom_call_target="tpu_custom_call" | custom-call | flops 77309411328 | bytes 61865984 | tf_op jit(solution)/shard_map/feed_weights/pallas_call | solution.py:1707
  472.2 0.8 fusion
  473.0 1.3 slice_bitcast_fusion
  474.4 1.6 convert_element_type.15
  475.9 2.7 convert_element_type.14
  478.6 0.6 dynamic-slice_bitcast_fusion
  479.2 0.8 copy.32
  480.0 1.0 copy.33
  481.0 0.6 copy.34
  481.6 3.2 copy.35
  484.8 3.2 copy.36
  488.0 0.8 slice-done
  488.8 0.7 slice-done.1
  489.6 2.7 copy.37
  (34 shorter events, 0.5 us)
Async XLA Ops:
  7.2 313.6 %reduce-scatter.2.cloned.1.call-start = ((), (), s32[]{:S(2)}) async-start(), calls=%async_computation.1 | async-start | bytes 1310720 | tf_op jit(solution)/shard_map/reduce_scatter | solution.py:2145
  92.0 110.9 %copy-start.3 = (bf16[1024,256]{1,0:T(8,128)(2,1)S(1)}, bf16[1024,256]{1,0:T(8,128)(2,1)}, u32[]{:S(2)}) copy-start(bf16[1024,256]{1,0:T(8,128)(2,1)} %get-tuple-element.63) | copy-start | bytes 1572868
  207.3 146.3 %all-gather.2.cloned.1.call-start = ((), (), s32[]{:S(2)}) async-start(), calls=%async_computation.2 | async-start | bytes 1310720 | tf_op jit(solution)/shard_map/all_gather | solution.py:2165
  353.7 120.7 %copy-start.1 = (bf16[256,2048]{1,0:T(8,128)(2,1)S(1)}, bf16[256,2048]{1,0:T(8,128)(2,1)}, u32[]{:S(2)}) copy-start(bf16[256,2048]{1,0:T(8,128)(2,1)} %all-gather.2.cloned.1.call-done) | copy-start | bytes 3145732
  472.2 3.7 copy-start
  474.4 4.8 copy-start.4
  474.4 7.2 %slice-start.4 = ((s8[6291456]{0:T(1024)(128)(4,1)}), s8[4194304]{0:T(1024)(128)(4,1)S(1)}, s32[]{:S(2)}) async-start(s8[6291456]{0:T(1024)(128)(4,1)} %bitcast.25), calls=%async_computation.7 | async-start | bytes 8388608
  475.9 4.1 copy-start.2
  475.9 5.0 %copy-start.5 = (f32[2,2048]{1,0:T(2,128)S(1)}, f32[2,2048]{1,0:T(2,128)}, u32[]{:S(2)}) copy-start(f32[2,2048]{1,0:T(2,128)} %get-tuple-element.130) | copy-start | bytes 49156
  475.9 5.6 %slice-start.5 = ((s8[6291456]{0:T(1024)(128)(4,1)}), s8[2097152]{0:T(1024)(128)(4,1)S(1)}, s32[]{:S(2)}) async-start(s8[6291456]{0:T(1024)(128)(4,1)} %bitcast.25), calls=%async_computation.8 | async-start | bytes 4194304
  479.2 5.6 %slice-start.2 = ((s8[6291456]{0:T(1024)(128)(4,1)}), s8[4194304]{0:T(1024)(128)(4,1)S(1)}, s32[]{:S(2)}) async-start(s8[6291456]{0:T(1024)(128)(4,1)} %bitcast.23), calls=%async_computation.5 | async-start | bytes 8388608
  481.6 3.2 slice-start.3
  481.6 7.2 %slice-start = ((s8[6291456]{0:T(1024)(128)(4,1)}), s8[4194304]{0:T(1024)(128)(4,1)S(1)}, s32[]{:S(2)}) async-start(s8[6291456]{0:T(1024)(128)(4,1)} %bitcast.21), calls=%async_computation.3 | async-start | bytes 8388608
  484.8 4.8 slice-start.1
Sparse Core Ops, SparseCore 0:
  207.5 25.5 reduce-scatter.1
  321.0 24.9 all-gather.1

commit v5 on v4

--- a/solution.py
+++ b/solution.py
@@ -427,13 +427,13 @@
 
 
 def scatter_gains_kernel(
-    p_ref, attn_ref, ffn_ref, head_ref, x_ref, scale_ref, dmid_ref, o_ref, so_ref, parts, small_buf, grad, small_send, small_recv, *rest
+    p_ref, attn_ref, ffn_ref, head_ref, x_ref, scale_ref, dmid_ref, o_ref, so_ref, parts, small_buf, grad, small_send, small_recv, near_buf, out_buf, far_buf, sib_send, sib_recv, send_sem, recv_sem
 ):
     rank, plane = lax.axis_index("fsdp"), lax.axis_index("sp")
     ranks = p_ref.shape[0]
     greet([(rank ^ k, plane) for k in range(1, 8)])
     for i in range(4):
-        scatter_near(p_ref, i, rest[0], rest[3], rest[4]).start()
+        scatter_near(p_ref, i, near_buf, sib_send, sib_recv).start()
     for r in range(ranks):
         for i in range(2):
             columns = slice((2 * r + i) * HEAD_DIM, (2 * r + i + 1) * HEAD_DIM)
@@ -456,15 +456,27 @@
         )
         copy.start()
         small.append(copy)
-    scatter_begin(p_ref, grad, *rest, started=True)
+    sems = (send_sem, recv_sem)
+
+    def block_of(i):
+        scatter_near(p_ref, i, near_buf, sib_send, sib_recv).wait_recv()
+        return p_ref[rank ^ SCATTER_ORDER[i]].astype(jnp.float32) + near_buf[i].astype(jnp.float32)
+
+    def own_block():
+        grad[...] = block_of(3)
+
+    relay_blocks(out_buf, far_buf, sems, block_of, own_block)
     total = parts[rank]
     for k in range(1, 8):
         small[k - 1].wait()
         total = total + small_buf[k - 1]
     so_ref[...] = total
-    scatter_end(p_ref, grad, *rest)
+    grad[...] = relay_sum(out_buf, far_buf, sems, grad[...])
     inputs = x_ref[...].astype(jnp.float32)
     o_ref[...] = dmid_ref[...] + norm_back(grad[...], inputs, inv_rms(inputs), scale_ref[...])
+    for i in range(4):
+        scatter_near(p_ref, i, near_buf, sib_send, sib_recv).wait_send()
+    relay_sent(out_buf, far_buf, sems)
 
 
 SCATTER_ORDER = (6, 2, 4, 0)
@@ -494,28 +506,52 @@
     )
 
 
-def scatter_begin(p_ref, o_ref, near_buf, out_buf, far_buf, sib_send, sib_recv, send_sem, recv_sem, started=False):
-    rank = lax.axis_index("fsdp")
-    for i in range(0 if started else 4):
-        scatter_near(p_ref, i, near_buf, sib_send, sib_recv).start()
-    for i, k in enumerate(SCATTER_ORDER):
-        scatter_near(p_ref, i, near_buf, sib_send, sib_recv).wait_recv()
-        joined = p_ref[rank ^ k].astype(jnp.float32) + near_buf[i].astype(jnp.float32)
-        if k:
-            out_buf[i] = joined.astype(out_buf.dtype)
-            scatter_far(i, out_buf, far_buf, send_sem, recv_sem).start()
-        else:
-            o_ref[...] = joined
-
-
-def scatter_end(p_ref, o_ref, near_buf, out_buf, far_buf, sib_send, sib_recv, send_sem, recv_sem):
-    for i in (1, 2, 0):
-        scatter_far(i, out_buf, far_buf, send_sem, recv_sem).wait_recv()
-        o_ref[...] += far_buf[i].astype(jnp.float32)
-    for i in range(4):
-        scatter_near(p_ref, i, near_buf, sib_send, sib_recv).wait_send()
-    for i in range(3):
-        scatter_far(i, out_buf, far_buf, send_sem, recv_sem).wait_send()
+def relay_copy(i, out_buf, far_buf, send_sem, recv_sem):
+    rank, plane = lax.axis_index("fsdp"), lax.axis_index("sp")
+    half = out_buf.shape[1] // 2
+    top, low = pl.ds(0, half), pl.ds(half, half)
+    slot, part, to = (
+        (0, top, 2),
+        (0, low, 4),
+        (1, top, 2),
+        (2, low, 4),
+        (1, low, 2),
+        (2, top, 4),
+    )[i]
+    return peer_copy(
+        out_buf.at[slot, part],
+        far_buf.at[slot, part],
+        send_sem.at[i],
+        recv_sem.at[i],
+        rank ^ to,
+        plane,
+    )
+
+
+def relay_blocks(out_buf, far_buf, sems, block_of, own_block):
+    half = out_buf.shape[1] // 2
+    copies = [relay_copy(i, out_buf, far_buf, *sems) for i in range(6)]
+    for slot, ready in ((0, (0, 1)), (1, (2,)), (2, (3,))):
+        out_buf[slot] = block_of(slot).astype(out_buf.dtype)
+        for i in ready:
+            copies[i].start()
+    own_block()
+    for arrived, slot, onward, rows in ((0, 2, 5, slice(0, half)), (1, 1, 4, slice(half, 2 * half))):
+        copies[arrived].wait_recv()
+        joined = out_buf[slot, rows].astype(jnp.float32) + far_buf[0, rows].astype(jnp.float32)
+        out_buf[slot, rows] = joined.astype(out_buf.dtype)
+        copies[onward].start()
+
+
+def relay_sum(out_buf, far_buf, sems, total):
+    for i in (2, 3, 5, 4):
+        relay_copy(i, out_buf, far_buf, *sems).wait_recv()
+    return total + far_buf[1].astype(jnp.float32) + far_buf[2].astype(jnp.float32)
+
+
+def relay_sent(out_buf, far_buf, sems):
+    for i in range(6):
+        relay_copy(i, out_buf, far_buf, *sems).wait_send()
 
 
 def scatter_scratch(rows, width, dtype):
@@ -549,7 +585,8 @@
             pltpu.SemaphoreType.DMA((7,)),
             pltpu.SemaphoreType.DMA((7,)),
         ]
-        + scatter_scratch(rows, width, p.dtype),
+        + scatter_scratch(rows, width, p.dtype)[:-2]
+        + [pltpu.SemaphoreType.DMA((6,)), pltpu.SemaphoreType.DMA((6,))],
         compiler_params=pltpu.CompilerParams(
             collective_id=collective_id, has_side_effects=True, vmem_limit_bytes=VMEM_LIMIT
         ),
@@ -561,7 +598,7 @@
     back_ref, raw_ref, cos_ref, sin_ref, xa_ref, x_ref, dgate_ref, w_ref, wg_ref, head_ref, blocks_ref, dxa_ref, qkv_ref, gate_ref, attn_ref, terms_ref, next_ref, sums, ag_send, ag_recv, own_sem
 ):
     rank, plane = lax.axis_index("fsdp"), lax.axis_index("sp")
-    block = blocks_ref.at[1, 1]
+    block = blocks_ref.at[0, 0]
     gather = (next_ref, ag_send, ag_recv)
     own = pltpu.make_async_copy(block, next_ref.at[rank], own_sem)
     group, rows, width = back_ref.shape
@@ -753,16 +790,15 @@
     return (plane + j <= planes - 1) & (plane > 0)
 
 
-def unheads_kernel(planes, dq_ref, dkv_ref, blocks_ref, n_ref, next_ref, ag_send, ag_recv, own_sem2, line_out, line_in, done, own_sem, q_send, q_recv, kv_send, kv_recv, line_send, line_recv):
+def unheads_kernel(planes, dq_ref, dkv_ref, gated_ref, pm_hbm, blocks_ref, n_ref, wout_ref, next_ref, pm, pm_sem, ag_send, ag_recv, own_sem2, line_out, line_in, done, own_sem, q_send, q_recv, kv_send, kv_recv, line_send, line_recv):
     rank, plane = lax.axis_index("fsdp"), lax.axis_index("sp")
     greet_line(8, planes)
-    gathers = [(next_ref.at[which], ag_send.at[which], ag_recv.at[which]) for which in range(2)]
-    own_blocks = [
-        pltpu.make_async_copy(blocks_ref.at[which, 0], next_ref.at[which, rank], own_sem2.at[which])
-        for which in range(2)
-    ]
-    for copy in own_blocks:
-        copy.start()
+    block = blocks_ref.at[1, 0]
+    gather = (next_ref, ag_send, ag_recv)
+    own_block = pltpu.make_async_copy(block, next_ref.at[rank], own_sem2)
+    own_block.start()
+    mid_load = pltpu.make_async_copy(pm_hbm, pm, pm_sem)
+    mid_load.start()
 
     def q_copy(m, to):
         return peer_copy(dq_ref, n_ref.at[pl.ds(2 * m, 2)], q_send, q_recv.at[m], to, plane)
@@ -802,8 +838,7 @@
     def target(j, side):
         return planes - 1 - j if side == 0 else j
 
-    for which in range(2):
-        gather_start(*gathers[which], own=blocks_ref.at[which, 0])
+    gather_start(*gather, own=block)
 
     for j in range(planes - 1):
         for which in range(2):
@@ -826,11 +861,15 @@
                 def _():
                     step_copy(j, which, side).start()
 
+        if j == 0:
+            mid_load.wait()
+            wout_ref[...] = mat_tn(gated_ref[...], pm[...].reshape(-1, pm.shape[-1])).astype(
+                wout_ref.dtype
+            )
         if j == 1:
-            gather_pass(*gathers[0], NEIGHBOURS_FIRST)
+            gather_pass(*gather, NEIGHBOURS_FIRST)
         if j == 2:
-            gather_pass(*gathers[1], NEIGHBOURS_FIRST)
-            gather_pass(*gathers[0], DIAGONAL)
+            gather_pass(*gather, DIAGONAL)
 
     for which in range(2):
         total = dkv_ref[plane, which].astype(jnp.float32)
@@ -857,12 +896,9 @@
             def _():
                 kv_local(m, which).start()
 
-    gather_pass(*gathers[1], DIAGONAL)
-    for gather in gathers:
-        gather_wait(*gather, FROM_SIBLING)
-        gather_sent(*gather)
-    for copy in own_blocks:
-        copy.wait()
+    gather_wait(*gather, FROM_SIBLING)
+    gather_sent(*gather)
+    own_block.wait()
 
     @pl.when(rank < 4)
     def _():
@@ -906,7 +942,7 @@
                     step_copy(j, which, side).wait_send()
 
 
-def return_heads(grad_query, grad_kv, line_blocks, collective_id):
+def return_heads(grad_query, grad_kv, gated, plane_mid, line_blocks, collective_id):
     _, tokens, width = grad_query.shape
     planes = lax.axis_size("sp")
     ranks = lax.axis_size("fsdp")
@@ -916,14 +952,17 @@
         functools.partial(unheads_kernel, planes),
         out_shape=(
             jax.ShapeDtypeStruct((4, tokens, width), grad_query.dtype),
-            jax.ShapeDtypeStruct((2, ranks) + line_blocks.shape[2:], line_blocks.dtype),
+            jax.ShapeDtypeStruct((gated.shape[1], plane_mid.shape[-1]), gated.dtype),
+            jax.ShapeDtypeStruct((ranks,) + line_blocks.shape[2:], line_blocks.dtype),
         ),
-        in_specs=[vmem, vmem, hbm],
-        out_specs=(vmem, hbm),
+        in_specs=[vmem, vmem, vmem, hbm, hbm],
+        out_specs=(vmem, vmem, hbm),
         scratch_shapes=[
-            pltpu.SemaphoreType.DMA((2, GATHER_COPIES)),
-            pltpu.SemaphoreType.DMA((2, GATHER_COPIES)),
-            pltpu.SemaphoreType.DMA((2,)),
+            pltpu.VMEM(plane_mid.shape, plane_mid.dtype),
+            pltpu.SemaphoreType.DMA,
+            pltpu.SemaphoreType.DMA((GATHER_COPIES,)),
+            pltpu.SemaphoreType.DMA((GATHER_COPIES,)),
+            pltpu.SemaphoreType.DMA,
             pltpu.VMEM((2, planes - 1, 2, tokens, width), grad_query.dtype),
             pltpu.VMEM((2, planes - 1, 2, tokens, width), grad_query.dtype),
             pltpu.VMEM((2, tokens, width), grad_query.dtype),
@@ -939,7 +978,7 @@
             collective_id=collective_id, has_side_effects=True, vmem_limit_bytes=VMEM_LIMIT
         ),
         name="return_heads",
-    )(grad_query, grad_kv, line_blocks)
+    )(grad_query, grad_kv, gated, plane_mid, line_blocks)
 
 
 def stack_heads(ref):
@@ -1442,9 +1481,9 @@
     small_ref,
     rows_ref,
     qkv_hbm,
-    wg_ref,
-    wu_ref,
-    wd_ref,
+    wg_hbm,
+    wu_hbm,
+    wd_hbm,
     og_ref,
     ou_ref,
     od_ref,
@@ -1453,6 +1492,10 @@
     go_ref,
     sum_hbm,
     more_hbm,
+    wg_ref,
+    wu_ref,
+    wd_ref,
+    w_sem,
     xbuf,
     dbuf,
     act,
@@ -1490,8 +1533,8 @@
     others = [lax.rem(plane + k, planes) for k in range(1, planes)]
     greet([(rank ^ k, plane) for k in (1, 2, 4, 6)] + [(rank, other) for other in others])
 
-    picks = ((0, 1), (1, 2), (0, 2))
-    gathers = [(more_hbm.at[g], ag_send.at[g], ag_recv.at[g]) for g in range(3)]
+    picks = ((0, 1), (1, 1), (1, 2), (0, 2))
+    gathers = [(more_hbm.at[g], ag_send.at[g], ag_recv.at[g]) for g in range(4)]
     own_blocks = [
         pltpu.make_async_copy(blocks_hbm.at[pick], more_hbm.at[g, rank], own_sem.at[g])
         for g, pick in enumerate(picks)
@@ -1505,10 +1548,10 @@
         block = pl.ds(part * lax.rem(step, 2), part)
         group = step // 2
         sources = (
-            (first_hbm.at[0, block], first_hbm.at[1, block]),
             (xp_hbm.at[block], dp_hbm.at[block]),
-            (more_hbm.at[0, block], second_hbm.at[block]),
-            (more_hbm.at[2, block], more_hbm.at[1, block]),
+            (first_hbm.at[block], second_hbm.at[block]),
+            (more_hbm.at[0, block], more_hbm.at[1, block]),
+            (more_hbm.at[3, block], more_hbm.at[2, block]),
         )
         for index, (x_from, d_from) in enumerate(sources):
             @pl.when(group == index)
@@ -1575,6 +1618,15 @@
     ]
 
     load(0, True)
+    kept(0).start()
+    weights = [
+        pltpu.make_async_copy(source, target, w_sem.at[index])
+        for index, (source, target) in enumerate(
+            ((wg_hbm, wg_ref), (wu_hbm, wu_ref), (wd_hbm, wd_ref))
+        )
+    ]
+    for copy in weights:
+        copy.start()
     own_quarter.start()
     for copy in own_blocks + small + own_parts + partials:
         copy.start()
@@ -1586,19 +1638,20 @@
     def _(step):
         @pl.when(step == 1)
         def _():
-            gather_pass(*gathers[0], NEIGHBOURS_FIRST)
+            kept(1).start()
             begin(1)
 
         @pl.when(step == 2)
         def _():
-            kept(0).start()
+            for copy in weights:
+                copy.wait()
+            gather_pass(*gathers[0], NEIGHBOURS_FIRST)
+
+        @pl.when(step == 3)
+        def _():
             gather_pass(*gathers[0], DIAGONAL)
             gather_pass(*gathers[1], NEIGHBOURS_FIRST)
             begin(2)
-
-        @pl.when(step == 3)
-        def _():
-            kept(1).start()
             for i, k in enumerate(SCATTER_ORDER):
                 own_parts[i].wait()
                 scatter_near(down_hbm, i, *scatter).wait_recv()
@@ -1610,10 +1663,12 @@
 
         @pl.when(step == 4)
         def _():
-            gather_wait(*gathers[0], FROM_SIBLING)
-            own_blocks[0].wait()
+            gather_pass(*gathers[1], DIAGONAL)
+            begin(3)
+            for g in (0, 1):
+                gather_wait(*gathers[g], FROM_SIBLING)
+                own_blocks[g].wait()
             load(step, True)
-            gather_pass(*gathers[1], DIAGONAL)
             own_quarter.wait()
             total = quarter[...].astype(jnp.float32)
             for k in range(planes - 1):
@@ -1627,13 +1682,15 @@
         @pl.when(step == 5)
         def _():
             gather_pass(*gathers[2], NEIGHBOURS_FIRST)
+            gather_pass(*gathers[3], NEIGHBOURS_FIRST)
+
+        @pl.when(step == 6)
+        def _():
+            for g in (2, 3):
+                gather_pass(*gathers[g], DIAGONAL)
             for i in range(3):
                 scatter_far(i, out_buf, far_buf, send_sem, recv_sem).start()
-
-        @pl.when(step == 6)
-        def _():
-            gather_pass(*gathers[2], DIAGONAL)
-            for g in (1, 2):
+            for g in (2, 3):
                 gather_wait(*gathers[g], FROM_SIBLING)
                 own_blocks[g].wait()
             load(step, True)
@@ -1648,7 +1705,7 @@
         normed = xbuf[slot].reshape(chunk, width)
         grad = dbuf[slot].reshape(chunk, width)
 
-        own = step // 2 == 1
+        own = step < 2
 
         @pl.when(own)
         def _():
@@ -1706,7 +1763,7 @@
     half, full = plane_x.dtype, jnp.float32
     return pl.pallas_call(
         functools.partial(feed_weights_kernel, planes),
-        in_specs=[hbm] * 7 + [vmem] * 3 + [hbm] + [vmem] * 3,
+        in_specs=[hbm] * 7 + [vmem] * 3 + [hbm] * 4,
         out_specs=(vmem,) * 6 + (hbm, hbm),
         out_shape=[jax.ShapeDtypeStruct(w_gate.shape, full)] * 3
         + [
@@ -1714,9 +1771,11 @@
             jax.ShapeDtypeStruct(small.shape, full),
             jax.ShapeDtypeStruct(gate_rows.shape, full),
             jax.ShapeDtypeStruct(qkv_part.shape, half),
-            jax.ShapeDtypeStruct((3, ranks, rows, width), half),
+            jax.ShapeDtypeStruct((4, ranks, rows, width), half),
         ],
-        scratch_shapes=[
+        scratch_shapes=[pltpu.VMEM(w_gate.shape, half)] * 3
+        + [
+            pltpu.SemaphoreType.DMA((3,)),
             pltpu.VMEM((2, ranks // 2, rows, width), half),
             pltpu.VMEM((2, ranks // 2, rows, width), half),
             pltpu.VMEM((3, ranks // 2 * rows, hidden), half),
@@ -1729,9 +1788,9 @@
             pltpu.SemaphoreType.DMA((2,)),
             pltpu.SemaphoreType.DMA,
             pltpu.SemaphoreType.DMA((4,)),
-            pltpu.SemaphoreType.DMA((3,)),
-            pltpu.SemaphoreType.DMA((3, GATHER_COPIES)),
-            pltpu.SemaphoreType.DMA((3, GATHER_COPIES)),
+            pltpu.SemaphoreType.DMA((4,)),
+            pltpu.SemaphoreType.DMA((4, GATHER_COPIES)),
+            pltpu.SemaphoreType.DMA((4, GATHER_COPIES)),
             pltpu.SemaphoreType.DMA((2, planes - 1)),
             pltpu.SemaphoreType.DMA((2, planes - 1)),
         ]
@@ -2141,13 +2200,14 @@
         2,
     )
     grad_gated = grad_gated.reshape(tokens, -1)
-    out_part = mat_tn(gated, plane_mid.reshape(tokens, model_width)).astype(jnp.bfloat16)
-    reduced = lax.psum_scatter(out_part, "sp", scatter_dimension=0, tiled=True)
     grad_query, grad_kv, gate_grad = attend_back(
         lengths, query, kv, gate_logit, attended, total, grad_gated, rows
     )
-    back, first_plane = return_heads(grad_query, grad_kv, line_blocks, 6)
-    grad_a_part, qkv_part, gate_rows, attn_terms, head_terms, second_grad = projection_back(
+    back, out_part, first_grad = return_heads(
+        grad_query, grad_kv, gated, plane_mid, line_blocks, 6
+    )
+    reduced = lax.psum_scatter(out_part, "sp", scatter_dimension=0, tiled=True)
+    grad_a_part, qkv_part, gate_rows, attn_terms, head_terms, first_b = projection_back(
         back,
         projected,
         cosine,
@@ -2180,8 +2240,8 @@
         plane_grad,
         acts,
         line_blocks,
-        first_plane,
-        second_grad,
+        first_b,
+        first_grad,
         down_part,
         middle,
         gain_sums,

time: 507 us -> 488 us (0.963)
  Pallas kernels: 458 us -> 436 us
  waiting for transfers between devices: 0.08 us -> 5.28 us
    pallas_call x1, Pallas kernels: 55.4 us -> 45.2 us  [return_heads(): pl.pallas_call(functools.partial(unheads_kernel, planes), out_shape=(jax....]
    pallas_call x1, Pallas kernels: 119 us -> 111 us  [feed_weights(): pl.pallas_call(functools.partial(feed_weights_kernel, planes), in_specs=[...]
    pallas_call x1, Pallas kernels: 32.8 us -> 27.7 us  [scatter_gains(): pl.pallas_call(scatter_gains_kernel, out_shape=(jax.ShapeDtypeStruct((row...]
    unnamed x30 -> x24, local copies, waits for them, and re-layouts: 13.1 us -> 13.1 us
  transfers between devices with their start and end apart: 2 -> 2, of which waited for: 0 -> 2; matrix products, arithmetic and copies ran while one was open for 0% -> 0% of each run, Pallas kernels for 29% -> 13%
where the time goes in v5:
time: 488 us; the launch traced here: 479 us
  Pallas kernels  436 us (89%)
  local copies, waits for them, and re-layouts  16 us (3%)
  between operations  14.3 us (3%)
  other arithmetic  7.77 us (2%)
  waiting for transfers between devices  5.28 us (1%)
    pallas_call x1, Pallas kernels, middle_layer(): pl.pallas_call(functools.partial(middle_kernel, planes), out_shape=(jax.S...  112 us
    pallas_call x1, Pallas kernels, feed_weights(): pl.pallas_call(functools.partial(feed_weights_kernel, planes), in_specs=[...  111 us
    pallas_call x1, Pallas kernels, front(): pl.pallas_call(functools.partial(front_kernel, planes), out_shape=(jax.Sh...  68.5 us
    pallas_call x1, Pallas kernels, return_heads(): pl.pallas_call(functools.partial(unheads_kernel, planes), out_shape=(jax....  45.2 us
    pallas_call x1, Pallas kernels, projection_back(): pl.pallas_call(projection_back_kernel, grid=(tokens // pair,), in_specs=[...  35.6 us
    pallas_call x1, Pallas kernels, scatter_gains(): pl.pallas_call(scatter_gains_kernel, out_shape=(jax.ShapeDtypeStruct((row...  27.7 us
    pallas_call x1, Pallas kernels, attend_back(): pl.pallas_call(functools.partial(attend_back_kernel, ranks, planes), grid...  21.9 us
    pallas_call x1, Pallas kernels, attend(): pl.pallas_call(functools.partial(attend_kernel, ranks, planes), grid_spec...  14.2 us
  transfers between devices with their start and end apart: 2, of which 2 were waited for; matrix products, arithmetic and copies ran while one was open for 0% of the time, Pallas kernels for 13%

profile of v5, /device:TPU:1, one launch (start us, length us, event | category | flops | bytes accessed | tf_op | source)
XLA Modules:
  0.0 479.2 jit_solution(18247754020770897006)
XLA Ops:
  7.2 0.7 pad_maximum_fusion
  8.2 1.3 maximum_convert_fusion.small_ref
  9.5 68.5 %front.1 = (bf16[2,1024,128]{2,1,0:T(8,128)(2,1)}, bf16[4,2,1024,128]{3,2,1,0:T(8,128)(2,1)}, bf16[8,128,2048]{2,1,0:T(8,128)(2,1)}, bf16[8,128,2048]{2,1,0:T(8,...) custom-call(s32[5]{0:T(128)} %lengths_ref.5, ...), custom_call_target="tpu_custom_call" | custom-call | tf_op jit(solution)/shard_map/front/pallas_call | solution.py:2099
  77.9 14.2 %attend.1 = (f32[2,1024,128]{2,1,0:T(8,128)}, f32[2,1024,1]{2,1,0:T(8,128)}, bf16[1024,256]{1,0:T(8,128)(2,1)}) custom-call(s32[5]{0:T(128)} %lengths_ref.5, bf16[2,1024,128]{2,1,0:T(8,128)(2,1)} %get-tuple-element.61.q_ref, bf16[4,2,8,128,128]{4,3,2,1,0:T(8,128)(2,1)} %bitcast.16, f32[2,1024,1]{2,1,0:T(8,128)} %get-tuple-element.63.gate_ref), custom_call_target="tpu_custom_call" | custom-call | tf_op jit(solution)/shard_map/attend/pallas_call | solution.py:1064
  92.1 111.8 %middle_layer.1 = (bf16[8,128,2048]{2,1,0:T(8,128)(2,1)}, bf16[2,3,128,2048]{3,2,1,0:T(8,128)(2,1)}, bf16[8,128,2048]{2,1,0:T(8,128)(2,1)}, f32[128,2048]{1,0:T(...) custom-call(bf16[8,128,256]{2,1,0:T(8,128)(2,1)} %bitcast.23, ...), custom_call_target="tpu_custom_call" | custom-call | tf_op jit(solution)/shard_map/middle_layer/pallas_call | solution.py:1425
  204.0 21.9 %attend_back.1 = (bf16[2,1024,128]{2,1,0:T(8,128)(2,1)}, bf16[4,2,8,128,128]{4,3,2,1,0:T(8,128)(2,1)}, bf16[2,1024,1]{2,1,0:T(8,128)(2,1)}) custom-call(s32[5]{0:T(128)} %lengths_ref.5, bf16[2,1024,128]{2,1,0:T(8,128)(2,1)} %get-tuple-element.61.q_ref, bf16[4,2,8,128,128]{4,3,2,1,0:T(8,128)(2,1)} %bitcast.17, f32[2,1024,1]{2,1,0:T(8,128)} %get-tuple-element.63.gate_ref, ...), custom_call_target="tpu_custom_call" | custom-call | tf_op jit(solution)/shard_map/attend_back/pallas_call | solution.py:1153
  225.9 45.2 %return_heads.1 = (bf16[4,1024,128]{2,1,0:T(8,128)(2,1)}, bf16[256,2048]{1,0:T(8,128)(2,1)}, bf16[8,128,2048]{2,1,0:T(8,128)(2,1)}) custom-call(bf16[2,1024,128]{2,1,0:T(8,128)(2,1)} %get-tuple-element.73.dq_ref, bf16[4,2,1024,128]{3,2,1,0:T(8,128)(2,1)} %bitcast.22, bf16[1024,256]{1,0:T(8,128)(2,1)} %get-tuple-element.64.gated_ref, ...), custom_call_target="tpu_custom_call" | custom-call | tf_op jit(solution)/shard_map/return_heads/pallas_call | solution.py:951
  271.2 35.6 %projection_back.1 = (bf16[8,128,2048]{2,1,0:T(8,128)(2,1)}, bf16[512,2048]{1,0:T(8,128)(2,1)}, f32[2,2048]{1,0:T(2,128)}, f32[1,2048]{1,0:T(1,128)}, f32[1,128]{1,0:T(1,128)}, /*index=5*/bf16[8,128,2048]{2,1,0:T(8,128)(2,1)}) custom-call(bf16[4,1024,128]{2,1,0:T(8,128)(2,1)} %get-tuple-element.76.back_ref, f32[1024,512]{1,0:T(8,128)} %get-tuple-element.77.raw_ref, ...), custom_call_target="tpu_custom_call" | custom-call | tf_op jit(solution)/shard_map/projection_back/pallas_call | solution.py:667
  306.8 4.6 reduce-scatter.2.cloned.1.call-done
  311.5 27.7 %scatter_gains.1 = (f32[128,2048]{1,0:T(8,128)}, f32[8,128]{1,0:T(8,128)}) custom-call(bf16[8,128,2048]{2,1,0:T(8,128)(2,1)} %get-tuple-element.91.p_ref, f32[1,2048]{1,0:T(1,128)} %get-tuple-element.92.attn_ref, f32[1,2048]{1,0:T(1,128)} %get-tuple-element.93.ffn_ref, f32[1,128]{1,0:T(1,128)} %get-tuple-element.94.head_ref, bf16[128,2048]{1,0:T(8,128)(2,1)} %x_ref.5, ...), custom_call_target="tpu_custom_call" | custom-call | tf_op jit(solution)/shard_map/scatter_gains/pallas_call | solution.py:573
  339.2 0.6 all-gather.2.cloned.1.call-done
  339.8 110.8 %feed_weights.1 = (f32[768,2048]{1,0:T(8,128)}, f32[768,2048]{1,0:T(8,128)}, f32[768,2048]{1,0:T(8,128)}, bf16[128,2048]{1,0:T(8,128)(2,1)}, f32[8,128]{1,0:T(8,...) custom-call(bf16[8,128,2048]{2,1,0:T(8,128)(2,1)} %get-tuple-element.67.xp_hbm, ...), custom_call_target="tpu_custom_call" | custom-call | flops 77309411328 | bytes 61865984 | tf_op jit(solution)/shard_map/feed_weights/pallas_call | solution.py:1764
  450.6 0.8 fusion
  451.4 1.3 slice_bitcast_fusion
  452.8 4.2 convert_element_type.10
  457.0 1.6 convert_element_type.11
  459.2 0.8 copy.32
  460.0 1.0 copy.33
  460.9 0.6 copy.34
  461.5 3.2 copy.35
  464.8 3.2 copy.36
  468.0 0.7 slice-done
  468.7 0.8 slice-done.1
  469.5 2.7 copy.37
  (26 shorter events, 1.1 us)
Async XLA Ops:
  7.2 304.3 %reduce-scatter.2.cloned.1.call-start = ((), (), s32[]{:S(2)}) async-start(), calls=%async_computation.1 | async-start | bytes 1310720 | tf_op jit(solution)/shard_map/reduce_scatter | solution.py:2209
  271.2 68.6 %all-gather.2.cloned.1.call-start = ((), (), s32[]{:S(2)}) async-start(), calls=%async_computation.2 | async-start | bytes 1310720 | tf_op jit(solution)/shard_map/all_gather | solution.py:2225
  450.6 6.4 %copy-start.1 = (bf16[256,2048]{1,0:T(8,128)(2,1)S(1)}, bf16[256,2048]{1,0:T(8,128)(2,1)}, u32[]{:S(2)}) copy-start(bf16[256,2048]{1,0:T(8,128)(2,1)} %all-gather.2.cloned.1.call-done) | copy-start | bytes 3145732
  452.8 6.4 %copy-start.3 = (bf16[128,2048]{1,0:T(8,128)(2,1)S(1)}, bf16[128,2048]{1,0:T(8,128)(2,1)}, u32[]{:S(2)}) copy-start(bf16[128,2048]{1,0:T(8,128)(2,1)} %get-tuple-element.128) | copy-start | bytes 1572868
  452.8 7.2 %copy-start.2 = (f32[128,2048]{1,0:T(8,128)S(1)}, f32[128,2048]{1,0:T(8,128)}, u32[]{:S(2)}) copy-start(f32[128,2048]{1,0:T(8,128)} %get-tuple-element.129) | copy-start | bytes 3145732
  457.0 3.9 copy-start.4
  457.0 4.5 copy-start
  459.2 5.6 %slice-start.2 = ((s8[6291456]{0:T(1024)(128)(4,1)}), s8[4194304]{0:T(1024)(128)(4,1)S(1)}, s32[]{:S(2)}) async-start(s8[6291456]{0:T(1024)(128)(4,1)} %bitcast.20), calls=%async_computation.5 | async-start | bytes 8388608
  461.5 3.3 slice-start.3
  461.5 7.2 %slice-start = ((s8[6291456]{0:T(1024)(128)(4,1)}), s8[4194304]{0:T(1024)(128)(4,1)S(1)}, s32[]{:S(2)}) async-start(s8[6291456]{0:T(1024)(128)(4,1)} %bitcast.18), calls=%async_computation.3 | async-start | bytes 8388608
  464.8 4.7 slice-start.1
Sparse Core Ops, SparseCore 0:
  271.3 40.1 reduce-scatter.1
  313.1 26.6 all-gather.1

commit v6 on v5

--- a/solution.py
+++ b/solution.py
@@ -1187,7 +1187,7 @@
     wg_hbm,
     wu_hbm,
     wd_hbm,
-    xg,
+    xg_hbm,
     line_hbm,
     down_hbm,
     mid_ref,
@@ -1195,7 +1195,10 @@
     gain_ref,
     pm_ref,
     dgated_ref,
+    act_hbm,
+    xg,
     act_ref,
+    flush_sem,
     wg,
     wu,
     wd,
@@ -1317,6 +1320,12 @@
             down_buf.at[slot], down_hbm.at[pl.ds(2 * p, 2)], down_sem.at[slot]
         )
 
+    def act_copy(p):
+        where = pl.ds(pl.multiple_of(2 * rows * p, 2 * rows), 2 * rows)
+        return pltpu.make_async_copy(
+            act_ref.at[:, where], act_hbm.at[:, where], flush_sem.at[p]
+        )
+
     def feed(k):
         p = (rank ^ k) // 2
         slot = (0, 2, 4, 6).index(k) % 2
@@ -1343,6 +1352,7 @@
         hidden = (swish * up_pre).astype(jnp.bfloat16)
         for kept, value in enumerate((grad_gate, grad_up, hidden)):
             act_ref[kept, pl.ds(pl.multiple_of(2 * rows * p, 2 * rows), 2 * rows)] = value
+        act_copy(p).start()
         down = jnp.dot(hidden, wd[...], preferred_element_type=jnp.float32)
         if k in (4, 6):
             down_copy(p, slot).wait()
@@ -1366,6 +1376,8 @@
     feed(4)
     gather_wait(xg, *sems, (11, 12))
     feed(6)
+    xg_copy = pltpu.make_async_copy(xg, xg_hbm, flush_sem.at[ranks // 2])
+    xg_copy.start()
 
     grad = keep[...]
     for i, k in enumerate((2, 4, 6)):
@@ -1401,6 +1413,9 @@
     gated_grad(6)
 
     gather_sent(xg, *sems)
+    xg_copy.wait()
+    for p in range(ranks // 2):
+        act_copy(p).wait()
     gather_sent(pm_ref, *sems2)
     for copy in dy_line + xb_line:
         copy.wait()
@@ -1436,8 +1451,11 @@
             jax.ShapeDtypeStruct((3, ranks * rows, hidden), half),
         ),
         in_specs=[vmem, vmem, vmem, vmem, hbm, hbm, hbm, hbm],
-        out_specs=(vmem, hbm, hbm, vmem, vmem, vmem, vmem, vmem, vmem),
+        out_specs=(hbm, hbm, hbm, vmem, vmem, vmem, vmem, vmem, hbm),
         scratch_shapes=[
+            pltpu.VMEM((ranks, rows, width), half),
+            pltpu.VMEM((3, ranks * rows, hidden), half),
+            pltpu.SemaphoreType.DMA((ranks // 2 + 1,)),
             pltpu.VMEM((hidden, width), half),
             pltpu.VMEM((hidden, width), half),
             pltpu.VMEM((hidden, width), half),
@@ -1484,9 +1502,9 @@
     wg_hbm,
     wu_hbm,
     wd_hbm,
-    og_ref,
-    ou_ref,
-    od_ref,
+    og_hbm,
+    ou_hbm,
+    od_hbm,
     h_ref,
     so_ref,
     go_ref,
@@ -1496,6 +1514,10 @@
     wu_ref,
     wd_ref,
     w_sem,
+    og_ref,
+    ou_ref,
+    od_ref,
+    o_sem,
     xbuf,
     dbuf,
     act,
@@ -1617,6 +1639,7 @@
         for k in range(planes - 1)
     ]
 
+    totals = ((og_ref, og_hbm), (ou_ref, ou_hbm), (od_ref, od_hbm))
     load(0, True)
     kept(0).start()
     weights = [
@@ -1729,9 +1752,13 @@
             for ref in (og_ref, ou_ref, od_ref):
                 ref[...] = jnp.zeros_like(ref)
 
-        og_ref[...] += mat_tn(act[0], normed)
-        ou_ref[...] += mat_tn(act[1], normed)
-        od_ref[...] += mat_tn(act[2], grad)
+        for index, other in ((0, normed), (1, normed), (2, grad)):
+            source, target = totals[index]
+            source[...] += mat_tn(act[index], other)
+
+            @pl.when(step == 2 * planes - 1)
+            def _():
+                pltpu.make_async_copy(source, target, o_sem.at[index]).start()
 
     output = mid_ref[...] + parts[3].astype(jnp.float32)
     for i in range(3):
@@ -1751,6 +1778,8 @@
         scatter_near(down_hbm, i, *scatter).wait_send()
     for gather in gathers:
         gather_sent(*gather)
+    for index, (source, target) in enumerate(totals):
+        pltpu.make_async_copy(source, target, o_sem.at[index]).wait()
 
 
 def feed_weights(plane_x, plane_grad, acts, blocks, first, second, down, middle, small, gate_rows, qkv_part, w_gate, w_up, w_down, collective_id):
@@ -1764,7 +1793,7 @@
     return pl.pallas_call(
         functools.partial(feed_weights_kernel, planes),
         in_specs=[hbm] * 7 + [vmem] * 3 + [hbm] * 4,
-        out_specs=(vmem,) * 6 + (hbm, hbm),
+        out_specs=(hbm,) * 3 + (vmem,) * 3 + (hbm, hbm),
         out_shape=[jax.ShapeDtypeStruct(w_gate.shape, full)] * 3
         + [
             jax.ShapeDtypeStruct((rows, width), half),
@@ -1774,6 +1803,10 @@
             jax.ShapeDtypeStruct((4, ranks, rows, width), half),
         ],
         scratch_shapes=[pltpu.VMEM(w_gate.shape, half)] * 3
+        + [
+            pltpu.SemaphoreType.DMA((3,)),
+        ]
+        + [pltpu.VMEM(w_gate.shape, full)] * 3
         + [
             pltpu.SemaphoreType.DMA((3,)),
             pltpu.VMEM((2, ranks // 2, rows, width), half),
@@ -1822,15 +1855,19 @@
     q_ref,
     kv_ref,
     dy_ref,
-    xg,
-    xa_ref,
-    raw_ref,
+    xg_hbm,
+    xa_hbm,
+    raw_hbm,
     gate_ref,
     attn_ref,
     ffn_ref,
     head_ref,
     cos_ref,
     sin_ref,
+    xg,
+    xa_ref,
+    raw_ref,
+    flush_sem,
     nat,
     gains,
     small_send,
@@ -1926,6 +1963,16 @@
             nat.at[m, token_rows(p)], kv_ref.at[plane, which, token_rows(p)], local_sem.at[p]
         )
 
+    def flush(p):
+        pair = pl.ds(2 * p, 2)
+        return [
+            pltpu.make_async_copy(xg.at[pair], xg_hbm.at[pair], flush_sem.at[0, p]),
+            pltpu.make_async_copy(xa_ref.at[pair], xa_hbm.at[pair], flush_sem.at[1, p]),
+            pltpu.make_async_copy(
+                raw_ref.at[token_rows(p)], raw_hbm.at[token_rows(p)], flush_sem.at[2, p]
+            ),
+        ]
+
     def process(k):
         p = chip ^ (k // 2)
         inputs = xg[pl.ds(2 * p, 2)].reshape(pair_rows, width).astype(jnp.float32)
@@ -1933,6 +1980,8 @@
         xa_ref[pl.ds(2 * p, 2)] = normed.reshape(2, rows, width)
         projected = mat_nt(normed, w_ref[...])
         raw_ref[token_rows(p)] = projected
+        for copy in flush(p):
+            copy.start()
         logits = mat_nt(normed, wg_ref[...])
         for head in range(gate_ref.shape[0]):
             gate_ref[head, token_rows(p)] = logits[:, head : head + 1]
@@ -2057,6 +2106,9 @@
         def _():
             q_copy(0, p, 0).wait_recv()
 
+    for p in range(ranks // 2):
+        for copy in flush(p):
+            copy.wait()
     for copy in small:
         copy.wait_send()
     gather_sent(xg, *sems)
@@ -2113,8 +2165,12 @@
             jax.ShapeDtypeStruct((tokens, HEAD_DIM), full),
         ),
         in_specs=[pl.BlockSpec(memory_space=pltpu.SMEM), vmem, vmem, vmem, vmem, hbm],
-        out_specs=(hbm, hbm, hbm) + (vmem,) * 9,
+        out_specs=(hbm,) * 6 + (vmem,) * 6,
         scratch_shapes=[
+            pltpu.VMEM((ranks, rows, width), half),
+            pltpu.VMEM((ranks, rows, width), half),
+            pltpu.VMEM((tokens, w_qkv.shape[0]), full),
+            pltpu.SemaphoreType.DMA((3, pairs)),
             pltpu.VMEM((4, tokens, HEAD_DIM), half),
             pltpu.VMEM((ranks,) + small.shape, small.dtype),
             pltpu.SemaphoreType.DMA((ranks - 1,)),

time: 488 us -> 474 us (0.971)
  Pallas kernels: 436 us -> 422 us
  transfers between devices with their start and end apart: 2 -> 2, of which waited for: 2 -> 2; matrix products, arithmetic and copies ran while one was open for 0% -> 0% of each run, Pallas kernels for 13% -> 14%
where the time goes in v6:
time: 474 us; the launch traced here: 466 us
  Pallas kernels  422 us (89%)
  local copies, waits for them, and re-layouts  16 us (3%)
  between operations  14.3 us (3%)
  other arithmetic  7.77 us (2%)
  waiting for transfers between devices  5.17 us (1%)
    pallas_call x1, Pallas kernels, middle_layer(): pl.pallas_call(functools.partial(middle_kernel, planes), out_shape=(jax.S...  109 us
    pallas_call x1, Pallas kernels, feed_weights(): pl.pallas_call(functools.partial(feed_weights_kernel, planes), in_specs=[...  108 us
    pallas_call x1, Pallas kernels, front(): pl.pallas_call(functools.partial(front_kernel, planes), out_shape=(jax.Sh...  65.2 us
    pallas_call x1, Pallas kernels, return_heads(): pl.pallas_call(functools.partial(unheads_kernel, planes), out_shape=(jax....  45.5 us
    pallas_call x1, Pallas kernels, projection_back(): pl.pallas_call(projection_back_kernel, grid=(tokens // pair,), in_specs=[...  35.4 us
    pallas_call x1, Pallas kernels, scatter_gains(): pl.pallas_call(scatter_gains_kernel, out_shape=(jax.ShapeDtypeStruct((row...  27.7 us
    pallas_call x1, Pallas kernels, attend_back(): pl.pallas_call(functools.partial(attend_back_kernel, ranks, planes), grid...  19.3 us
    unnamed x24, local copies, waits for them, and re-layouts  13.1 us
  transfers between devices with their start and end apart: 2, of which 2 were waited for; matrix products, arithmetic and copies ran while one was open for 0% of the time, Pallas kernels for 14%

profile of v6, /device:TPU:1, one launch (start us, length us, event | category | flops | bytes accessed | tf_op | source)
XLA Modules:
  0.0 465.7 jit_solution(13894404338937136087)
XLA Ops:
  7.2 0.7 pad_maximum_fusion
  8.2 1.3 maximum_convert_fusion.small_ref
  9.5 65.2 %front.1 = (bf16[2,1024,128]{2,1,0:T(8,128)(2,1)}, bf16[4,2,1024,128]{3,2,1,0:T(8,128)(2,1)}, bf16[8,128,2048]{2,1,0:T(8,128)(2,1)}, bf16[8,128,2048]{2,1,0:T(8,...) custom-call(s32[5]{0:T(128)} %lengths_ref.5, ...), custom_call_target="tpu_custom_call" | custom-call | tf_op jit(solution)/shard_map/front/pallas_call | solution.py:2151
  74.7 12.8 %attend.1 = (f32[2,1024,128]{2,1,0:T(8,128)}, f32[2,1024,1]{2,1,0:T(8,128)}, bf16[1024,256]{1,0:T(8,128)(2,1)}) custom-call(s32[5]{0:T(128)} %lengths_ref.5, bf16[2,1024,128]{2,1,0:T(8,128)(2,1)} %get-tuple-element.61.q_ref, bf16[4,2,8,128,128]{4,3,2,1,0:T(8,128)(2,1)} %bitcast.16, f32[2,1024,1]{2,1,0:T(8,128)} %get-tuple-element.63.gate_ref), custom_call_target="tpu_custom_call" | custom-call | tf_op jit(solution)/shard_map/attend/pallas_call | solution.py:1064
  87.5 108.9 %middle_layer.1 = (bf16[8,128,2048]{2,1,0:T(8,128)(2,1)}, bf16[2,3,128,2048]{3,2,1,0:T(8,128)(2,1)}, bf16[8,128,2048]{2,1,0:T(8,128)(2,1)}, f32[128,2048]{1,0:T(...) custom-call(bf16[8,128,256]{2,1,0:T(8,128)(2,1)} %bitcast.23, ...), custom_call_target="tpu_custom_call" | custom-call | tf_op jit(solution)/shard_map/middle_layer/pallas_call | solution.py:1440
  196.4 19.3 %attend_back.1 = (bf16[2,1024,128]{2,1,0:T(8,128)(2,1)}, bf16[4,2,8,128,128]{4,3,2,1,0:T(8,128)(2,1)}, bf16[2,1024,1]{2,1,0:T(8,128)(2,1)}) custom-call(s32[5]{0:T(128)} %lengths_ref.5, bf16[2,1024,128]{2,1,0:T(8,128)(2,1)} %get-tuple-element.61.q_ref, bf16[4,2,8,128,128]{4,3,2,1,0:T(8,128)(2,1)} %bitcast.17, f32[2,1024,1]{2,1,0:T(8,128)} %get-tuple-element.63.gate_ref, ...), custom_call_target="tpu_custom_call" | custom-call | tf_op jit(solution)/shard_map/attend_back/pallas_call | solution.py:1153
  215.7 45.5 %return_heads.1 = (bf16[4,1024,128]{2,1,0:T(8,128)(2,1)}, bf16[256,2048]{1,0:T(8,128)(2,1)}, bf16[8,128,2048]{2,1,0:T(8,128)(2,1)}) custom-call(bf16[2,1024,128]{2,1,0:T(8,128)(2,1)} %get-tuple-element.73.dq_ref, bf16[4,2,1024,128]{3,2,1,0:T(8,128)(2,1)} %bitcast.22, bf16[1024,256]{1,0:T(8,128)(2,1)} %get-tuple-element.64.gated_ref, ...), custom_call_target="tpu_custom_call" | custom-call | tf_op jit(solution)/shard_map/return_heads/pallas_call | solution.py:951
  261.2 35.4 %projection_back.1 = (bf16[8,128,2048]{2,1,0:T(8,128)(2,1)}, bf16[512,2048]{1,0:T(8,128)(2,1)}, f32[2,2048]{1,0:T(2,128)}, f32[1,2048]{1,0:T(1,128)}, f32[1,128]{1,0:T(1,128)}, /*index=5*/bf16[8,128,2048]{2,1,0:T(8,128)(2,1)}) custom-call(bf16[4,1024,128]{2,1,0:T(8,128)(2,1)} %get-tuple-element.76.back_ref, f32[1024,512]{1,0:T(8,128)} %get-tuple-element.77.raw_ref, ...), custom_call_target="tpu_custom_call" | custom-call | tf_op jit(solution)/shard_map/projection_back/pallas_call | solution.py:667
  296.7 4.6 reduce-scatter.2.cloned.1.call-done
  301.2 27.7 %scatter_gains.1 = (f32[128,2048]{1,0:T(8,128)}, f32[8,128]{1,0:T(8,128)}) custom-call(bf16[8,128,2048]{2,1,0:T(8,128)(2,1)} %get-tuple-element.91.p_ref, f32[1,2048]{1,0:T(1,128)} %get-tuple-element.92.attn_ref, f32[1,2048]{1,0:T(1,128)} %get-tuple-element.93.ffn_ref, f32[1,128]{1,0:T(1,128)} %get-tuple-element.94.head_ref, bf16[128,2048]{1,0:T(8,128)(2,1)} %x_ref.5, ...), custom_call_target="tpu_custom_call" | custom-call | tf_op jit(solution)/shard_map/scatter_gains/pallas_call | solution.py:573
  329.5 107.6 %feed_weights.1 = (f32[768,2048]{1,0:T(8,128)}, f32[768,2048]{1,0:T(8,128)}, f32[768,2048]{1,0:T(8,128)}, bf16[128,2048]{1,0:T(8,128)(2,1)}, f32[8,128]{1,0:T(8,...) custom-call(bf16[8,128,2048]{2,1,0:T(8,128)(2,1)} %get-tuple-element.67.xp_hbm, ...), custom_call_target="tpu_custom_call" | custom-call | flops 77309411328 | bytes 61865984 | tf_op jit(solution)/shard_map/feed_weights/pallas_call | solution.py:1793
  437.1 0.8 fusion
  437.9 1.3 slice_bitcast_fusion
  439.2 4.2 convert_element_type.10
  443.5 1.6 convert_element_type.11
  445.0 0.6 dynamic-slice_bitcast_fusion
  445.6 0.8 copy.32
  446.4 1.0 copy.33
  447.4 0.6 copy.34
  448.0 3.2 copy.35
  451.3 3.2 copy.36
  454.5 0.7 slice-done
  455.2 0.8 slice-done.1
  456.0 2.7 copy.37
  (26 shorter events, 1.1 us)
Async XLA Ops:
  7.2 294.0 %reduce-scatter.2.cloned.1.call-start = ((), (), s32[]{:S(2)}) async-start(), calls=%async_computation.1 | async-start | bytes 1310720 | tf_op jit(solution)/shard_map/reduce_scatter | solution.py:2265
  261.2 68.3 %all-gather.2.cloned.1.call-start = ((), (), s32[]{:S(2)}) async-start(), calls=%async_computation.2 | async-start | bytes 1310720 | tf_op jit(solution)/shard_map/all_gather | solution.py:2281
  437.1 6.4 %copy-start.1 = (bf16[256,2048]{1,0:T(8,128)(2,1)S(1)}, bf16[256,2048]{1,0:T(8,128)(2,1)}, u32[]{:S(2)}) copy-start(bf16[256,2048]{1,0:T(8,128)(2,1)} %all-gather.2.cloned.1.call-done) | copy-start | bytes 3145732
  439.2 6.4 %copy-start.3 = (bf16[128,2048]{1,0:T(8,128)(2,1)S(1)}, bf16[128,2048]{1,0:T(8,128)(2,1)}, u32[]{:S(2)}) copy-start(bf16[128,2048]{1,0:T(8,128)(2,1)} %get-tuple-element.128) | copy-start | bytes 1572868
  439.2 7.2 %copy-start.2 = (f32[128,2048]{1,0:T(8,128)S(1)}, f32[128,2048]{1,0:T(8,128)}, u32[]{:S(2)}) copy-start(f32[128,2048]{1,0:T(8,128)} %get-tuple-element.129) | copy-start | bytes 3145732
  443.5 3.9 copy-start.4
  443.5 4.5 copy-start
  445.6 5.6 %slice-start.2 = ((s8[6291456]{0:T(1024)(128)(4,1)}), s8[4194304]{0:T(1024)(128)(4,1)S(1)}, s32[]{:S(2)}) async-start(s8[6291456]{0:T(1024)(128)(4,1)} %bitcast.20), calls=%async_computation.5 | async-start | bytes 8388608
  448.0 3.3 slice-start.3
  448.0 7.2 %slice-start = ((s8[6291456]{0:T(1024)(128)(4,1)}), s8[4194304]{0:T(1024)(128)(4,1)S(1)}, s32[]{:S(2)}) async-start(s8[6291456]{0:T(1024)(128)(4,1)} %bitcast.18), calls=%async_computation.3 | async-start | bytes 8388608
  451.3 4.7 %slice-start.1 = ((s8[6291456]{0:T(1024)(128)(4,1)}), s8[2097152]{0:T(1024)(128)(4,1)S(1)}, s32[]{:S(2)}) async-start(s8[6291456]{0:T(1024)(128)(4,1)} %bitcast.18), calls=%async_computation.4 | async-start | bytes 4194304
Sparse Core Ops, SparseCore 0:
  261.3 39.8 reduce-scatter.1
  302.9 26.6 all-gather.1

commit v7 on v6

--- a/solution.py
+++ b/solution.py
@@ -989,11 +989,20 @@
     block = pl.program_id(0)
     span = planes * rows
     first = block * span + lax.axis_index("sp") * rows
-    start, end = jnp.int32(0), jnp.int32(0)
+    start, last_start, end = jnp.int32(0), jnp.int32(0), jnp.int32(0)
     for item in range(lengths_ref.shape[0]):
         end = end + lengths_ref[item]
         start = jnp.where(first >= end, end, start)
-    return start // span, block, first
+        last_start = jnp.where(first + rows - 1 >= end, end, last_start)
+    low = start // span
+    inner = jnp.clip((last_start + span - 1) // span, low, block)
+    return low, inner, block, first
+
+
+def sweep(low, inner, high, step, running):
+    running = lax.fori_loop(low, inner, functools.partial(step, True), running)
+    running = lax.fori_loop(inner, high, functools.partial(step, False), running)
+    return step(True, high, running)
 
 
 def row_starts(lengths_ref, tokens):
@@ -1004,11 +1013,13 @@
     return start
 
 
-def chunk_weights(query, key, scale, tokens, starts, first_key):
-    scores = mat_nt(query, key) * scale
+def chunk_weights(masked, query, key, scale, tokens, starts, first_key):
+    scores = mat_nt(query, key) * (scale * math.log2(math.e))
+    if not masked:
+        return jnp.exp2(scores)
     columns = first_key + lax.broadcasted_iota(jnp.int32, scores.shape, 1)
     allowed = (columns <= tokens) & (columns >= starts)
-    return jnp.where(allowed, jnp.exp(scores), 0.0)
+    return jnp.where(allowed, jnp.exp2(scores), 0.0)
 
 
 def query_tokens(first, rows, group):
@@ -1019,26 +1030,27 @@
 def attend_kernel(ranks, planes, lengths_ref, q_ref, kv_ref, gate_ref, att_ref, total_ref, gated_ref):
     group, rows, width = q_ref.shape
     scale = HEAD_DIM ** (-0.5)
-    low, high, first = block_bounds(lengths_ref, ranks, planes, rows)
+    low, inner, high, first = block_bounds(lengths_ref, ranks, planes, rows)
     tokens = query_tokens(first, rows, group)
     starts = row_starts(lengths_ref, tokens)
     query = stack_heads(q_ref)
     span = planes * rows
 
-    def step(chunk, running):
+    def step(masked, chunk, running):
         total, unnorm = running
         key = kv_ref[:, 0, chunk].reshape(span, width)
         value = kv_ref[:, 1, chunk].reshape(span, width)
-        weights = chunk_weights(query, key, scale, tokens, starts, chunk * span)
+        weights = chunk_weights(masked, query, key, scale, tokens, starts, chunk * span)
         total = total + jnp.sum(weights, axis=1, keepdims=True)
         unnorm = unnorm + jnp.dot(
             weights.astype(jnp.bfloat16), value, preferred_element_type=jnp.float32
         )
         return total, unnorm
 
-    total, unnorm = lax.fori_loop(
+    total, unnorm = sweep(
         low,
-        high + 1,
+        inner,
+        high,
         step,
         (
             jnp.zeros((group * rows, 1), jnp.float32),
@@ -1092,7 +1104,7 @@
 ):
     group, rows, width = q_ref.shape
     scale = HEAD_DIM ** (-0.5)
-    low, high, first = block_bounds(lengths_ref, ranks, planes, rows)
+    low, inner, high, first = block_bounds(lengths_ref, ranks, planes, rows)
     tokens = query_tokens(first, rows, group)
     starts = row_starts(lengths_ref, tokens)
     query = stack_heads(q_ref)
@@ -1117,10 +1129,10 @@
     scaled = (dattended / total).astype(jnp.bfloat16)
     delta = jnp.sum(dattended * attended, axis=1, keepdims=True) / total
 
-    def step(chunk, dquery):
+    def step(masked, chunk, dquery):
         key = kv_ref[:, 0, chunk].reshape(span, width)
         value = kv_ref[:, 1, chunk].reshape(span, width)
-        weights = chunk_weights(query, key, scale, tokens, starts, chunk * span)
+        weights = chunk_weights(masked, query, key, scale, tokens, starts, chunk * span)
         dprob = mat_nt(scaled, value)
         dscore = (weights * (dprob - delta)).astype(jnp.bfloat16)
         dquery = dquery + jnp.dot(dscore, key, preferred_element_type=jnp.float32)
@@ -1130,8 +1142,8 @@
         sums[:, 1, chunk] += dvalue.reshape(planes, rows, width)
         return dquery
 
-    dquery = lax.fori_loop(
-        low, high + 1, step, jnp.zeros((group * rows, width), jnp.float32)
+    dquery = sweep(
+        low, inner, high, step, jnp.zeros((group * rows, width), jnp.float32)
     )
     dq_ref[...] = (dquery * scale).astype(jnp.bfloat16).reshape(group, rows, width)
 

time: 474 us -> 473 us (level)
  no operation moved by 1% of the time
where the time goes in v7:
time: 473 us; the launch traced here: 468 us
  Pallas kernels  424 us (90%)
  local copies, waits for them, and re-layouts  16 us (3%)
  between operations  14.3 us (3%)
  other arithmetic  7.77 us (2%)
  waiting for transfers between devices  5.47 us (1%)
    pallas_call x1, Pallas kernels, middle_layer(): pl.pallas_call(functools.partial(middle_kernel, planes), out_shape=(jax.S...  108 us
    pallas_call x1, Pallas kernels, feed_weights(): pl.pallas_call(functools.partial(feed_weights_kernel, planes), in_specs=[...  108 us
    pallas_call x1, Pallas kernels, front(): pl.pallas_call(functools.partial(front_kernel, planes), out_shape=(jax.Sh...  65.2 us
    pallas_call x1, Pallas kernels, return_heads(): pl.pallas_call(functools.partial(unheads_kernel, planes), out_shape=(jax....  44.8 us
    pallas_call x1, Pallas kernels, projection_back(): pl.pallas_call(projection_back_kernel, grid=(tokens // pair,), in_specs=[...  36.3 us
    pallas_call x1, Pallas kernels, scatter_gains(): pl.pallas_call(scatter_gains_kernel, out_shape=(jax.ShapeDtypeStruct((row...  27.7 us
    pallas_call x1, Pallas kernels, attend_back(): pl.pallas_call(functools.partial(attend_back_kernel, ranks, planes), grid...  21.3 us
    unnamed x24, local copies, waits for them, and re-layouts  13.1 us
  transfers between devices with their start and end apart: 2, of which 2 were waited for; matrix products, arithmetic and copies ran while one was open for 0% of the time, Pallas kernels for 14%

profile of v7, /device:TPU:1, one launch (start us, length us, event | category | flops | bytes accessed | tf_op | source)
XLA Modules:
  0.0 467.6 jit_solution(17308019217261052139)
XLA Ops:
  7.2 0.7 pad_maximum_fusion
  8.2 1.3 maximum_convert_fusion.small_ref
  9.5 65.2 %front.1 = (bf16[2,1024,128]{2,1,0:T(8,128)(2,1)}, bf16[4,2,1024,128]{3,2,1,0:T(8,128)(2,1)}, bf16[8,128,2048]{2,1,0:T(8,128)(2,1)}, bf16[8,128,2048]{2,1,0:T(8,...) custom-call(s32[5]{0:T(128)} %lengths_ref.5, ...), custom_call_target="tpu_custom_call" | custom-call | tf_op jit(solution)/shard_map/front/pallas_call | solution.py:2163
  74.7 13.0 %attend.1 = (f32[2,1024,128]{2,1,0:T(8,128)}, f32[2,1024,1]{2,1,0:T(8,128)}, bf16[1024,256]{1,0:T(8,128)(2,1)}) custom-call(s32[5]{0:T(128)} %lengths_ref.5, bf16[2,1024,128]{2,1,0:T(8,128)(2,1)} %get-tuple-element.61.q_ref, bf16[4,2,8,128,128]{4,3,2,1,0:T(8,128)(2,1)} %bitcast.16, f32[2,1024,1]{2,1,0:T(8,128)} %get-tuple-element.63.gate_ref), custom_call_target="tpu_custom_call" | custom-call | tf_op jit(solution)/shard_map/attend/pallas_call | solution.py:1076
  87.7 108.1 %middle_layer.1 = (bf16[8,128,2048]{2,1,0:T(8,128)(2,1)}, bf16[2,3,128,2048]{3,2,1,0:T(8,128)(2,1)}, bf16[8,128,2048]{2,1,0:T(8,128)(2,1)}, f32[128,2048]{1,0:T(...) custom-call(bf16[8,128,256]{2,1,0:T(8,128)(2,1)} %bitcast.23, ...), custom_call_target="tpu_custom_call" | custom-call | tf_op jit(solution)/shard_map/middle_layer/pallas_call | solution.py:1452
  195.8 21.3 %attend_back.1 = (bf16[2,1024,128]{2,1,0:T(8,128)(2,1)}, bf16[4,2,8,128,128]{4,3,2,1,0:T(8,128)(2,1)}, bf16[2,1024,1]{2,1,0:T(8,128)(2,1)}) custom-call(s32[5]{0:T(128)} %lengths_ref.5, bf16[2,1024,128]{2,1,0:T(8,128)(2,1)} %get-tuple-element.61.q_ref, bf16[4,2,8,128,128]{4,3,2,1,0:T(8,128)(2,1)} %bitcast.17, f32[2,1024,1]{2,1,0:T(8,128)} %get-tuple-element.63.gate_ref, ...), custom_call_target="tpu_custom_call" | custom-call | tf_op jit(solution)/shard_map/attend_back/pallas_call | solution.py:1165
  217.1 44.8 %return_heads.1 = (bf16[4,1024,128]{2,1,0:T(8,128)(2,1)}, bf16[256,2048]{1,0:T(8,128)(2,1)}, bf16[8,128,2048]{2,1,0:T(8,128)(2,1)}) custom-call(bf16[2,1024,128]{2,1,0:T(8,128)(2,1)} %get-tuple-element.73.dq_ref, bf16[4,2,1024,128]{3,2,1,0:T(8,128)(2,1)} %bitcast.22, bf16[1024,256]{1,0:T(8,128)(2,1)} %get-tuple-element.64.gated_ref, ...), custom_call_target="tpu_custom_call" | custom-call | tf_op jit(solution)/shard_map/return_heads/pallas_call | solution.py:951
  261.9 36.3 %projection_back.1 = (bf16[8,128,2048]{2,1,0:T(8,128)(2,1)}, bf16[512,2048]{1,0:T(8,128)(2,1)}, f32[2,2048]{1,0:T(2,128)}, f32[1,2048]{1,0:T(1,128)}, f32[1,128]{1,0:T(1,128)}, /*index=5*/bf16[8,128,2048]{2,1,0:T(8,128)(2,1)}) custom-call(bf16[4,1024,128]{2,1,0:T(8,128)(2,1)} %get-tuple-element.76.back_ref, f32[1024,512]{1,0:T(8,128)} %get-tuple-element.77.raw_ref, ...), custom_call_target="tpu_custom_call" | custom-call | tf_op jit(solution)/shard_map/projection_back/pallas_call | solution.py:667
  298.3 4.9 %reduce-scatter.2.cloned.1.call-done = bf16[64,2048]{1,0:T(8,128)(2,1)} async-done(((bf16[256,2048]{1,0:T(8,128)(2,1)}), bf16[64,2048]{1,0:T(8,128)(2,1)}) %reduce-scatter.2.cloned.1.call-update) | async-done | bytes 262160 | tf_op jit(solution)/shard_map/reduce_scatter | solution.py:2277
  303.2 27.7 %scatter_gains.1 = (f32[128,2048]{1,0:T(8,128)}, f32[8,128]{1,0:T(8,128)}) custom-call(bf16[8,128,2048]{2,1,0:T(8,128)(2,1)} %get-tuple-element.91.p_ref, f32[1,2048]{1,0:T(1,128)} %get-tuple-element.92.attn_ref, f32[1,2048]{1,0:T(1,128)} %get-tuple-element.93.ffn_ref, f32[1,128]{1,0:T(1,128)} %get-tuple-element.94.head_ref, bf16[128,2048]{1,0:T(8,128)(2,1)} %x_ref.5, ...), custom_call_target="tpu_custom_call" | custom-call | tf_op jit(solution)/shard_map/scatter_gains/pallas_call | solution.py:573
  331.4 107.6 %feed_weights.1 = (f32[768,2048]{1,0:T(8,128)}, f32[768,2048]{1,0:T(8,128)}, f32[768,2048]{1,0:T(8,128)}, bf16[128,2048]{1,0:T(8,128)(2,1)}, f32[8,128]{1,0:T(8,...) custom-call(bf16[8,128,2048]{2,1,0:T(8,128)(2,1)} %get-tuple-element.67.xp_hbm, ...), custom_call_target="tpu_custom_call" | custom-call | flops 77309411328 | bytes 61865984 | tf_op jit(solution)/shard_map/feed_weights/pallas_call | solution.py:1805
  439.0 0.8 fusion
  439.8 1.3 slice_bitcast_fusion
  441.1 4.2 convert_element_type.10
  445.4 1.6 convert_element_type.11
  446.9 0.6 dynamic-slice_bitcast_fusion
  447.5 0.8 copy.32
  448.3 1.0 copy.33
  449.3 0.6 copy.34
  449.9 3.2 copy.35
  453.2 3.2 copy.36
  456.4 0.7 slice-done
  457.0 0.8 slice-done.1
  457.9 2.7 copy.37
  (26 shorter events, 1.1 us)
Async XLA Ops:
  7.2 296.0 %reduce-scatter.2.cloned.1.call-start = ((), (), s32[]{:S(2)}) async-start(), calls=%async_computation.1 | async-start | bytes 1310720 | tf_op jit(solution)/shard_map/reduce_scatter | solution.py:2277
  261.9 69.5 %all-gather.2.cloned.1.call-start = ((), (), s32[]{:S(2)}) async-start(), calls=%async_computation.2 | async-start | bytes 1310720 | tf_op jit(solution)/shard_map/all_gather | solution.py:2293
  439.0 6.4 %copy-start.1 = (bf16[256,2048]{1,0:T(8,128)(2,1)S(1)}, bf16[256,2048]{1,0:T(8,128)(2,1)}, u32[]{:S(2)}) copy-start(bf16[256,2048]{1,0:T(8,128)(2,1)} %all-gather.2.cloned.1.call-done) | copy-start | bytes 3145732
  441.1 6.4 %copy-start.3 = (bf16[128,2048]{1,0:T(8,128)(2,1)S(1)}, bf16[128,2048]{1,0:T(8,128)(2,1)}, u32[]{:S(2)}) copy-start(bf16[128,2048]{1,0:T(8,128)(2,1)} %get-tuple-element.128) | copy-start | bytes 1572868
  441.1 7.2 %copy-start.2 = (f32[128,2048]{1,0:T(8,128)S(1)}, f32[128,2048]{1,0:T(8,128)}, u32[]{:S(2)}) copy-start(f32[128,2048]{1,0:T(8,128)} %get-tuple-element.129) | copy-start | bytes 3145732
  445.4 3.9 copy-start.4
  445.4 4.5 copy-start
  447.5 5.6 %slice-start.2 = ((s8[6291456]{0:T(1024)(128)(4,1)}), s8[4194304]{0:T(1024)(128)(4,1)S(1)}, s32[]{:S(2)}) async-start(s8[6291456]{0:T(1024)(128)(4,1)} %bitcast.20), calls=%async_computation.5 | async-start | bytes 8388608
  449.9 3.3 slice-start.3
  449.9 7.2 %slice-start = ((s8[6291456]{0:T(1024)(128)(4,1)}), s8[4194304]{0:T(1024)(128)(4,1)S(1)}, s32[]{:S(2)}) async-start(s8[6291456]{0:T(1024)(128)(4,1)} %bitcast.18), calls=%async_computation.3 | async-start | bytes 8388608
  453.2 4.7 slice-start.1
Sparse Core Ops, SparseCore 0:
  262.0 41.0 reduce-scatter.1
  304.8 26.5 all-gather.1
